TPU v7x, 32 devices: a whole 2x2x4 slice. The times are simulated.
32 devices in a mesh: rep: 8 (over y, x, core), shard: 4 (over z).
Axes of the slice: x: 2, y: 2, z: 4, core: 2. Of those that a mesh axis runs over, the one named last changes fastest.
Arguments:
- tokens: bfloat16 [16384, 768], P(('rep', 'shard')), may hold values from -6 to 6
- ln1_scale: bfloat16 [768], P('shard'), may hold values from 0.5 to 1.5
- ln1_shift: bfloat16 [768], P('shard'), may hold values from -1.75 to 1.75
- w_query: bfloat16 [768, 768], P('shard'), may hold values from -0.21875 to 0.21875
- b_query: bfloat16 [768], P('shard'), may hold values from -1.75 to 1.75
- w_key: bfloat16 [768, 768], P('shard'), may hold values from -0.21875 to 0.21875
- b_key: bfloat16 [768], P('shard'), may hold values from -1.75 to 1.75
- w_value: bfloat16 [768, 768], P('shard'), may hold values from -0.21875 to 0.21875
- b_value: bfloat16 [768], P('shard'), may hold values from -1.75 to 1.75
- shift_taps: bfloat16 [768, 64], P('shard'), may hold values from -0.75 to 0.75
- ssm_coef: bfloat16 [768, 64], P('shard'), may hold values from -0.125 to 0.125
- ssm_rate: bfloat16 [768, 64], P('shard'), may hold values from 0.0009994507 to 0.099609375
- ssm_skip: bfloat16 [768], P('shard'), may hold values from 0.25 to 1.75
- w_out: bfloat16 [768, 768], P('shard'), may hold values from -0.21875 to 0.21875
- b_out: bfloat16 [768], P('shard'), may hold values from -1.75 to 1.75
- ln2_scale: bfloat16 [768], P('shard'), may hold values from 0.5 to 1.5
- ln2_shift: bfloat16 [768], P('shard'), may hold values from -1.75 to 1.75
- w_up: bfloat16 [768, 3072], P('shard'), may hold values from -0.21875 to 0.21875
- b_up: bfloat16 [3072], P('shard'), may hold values from -1.75 to 1.75
- w_down: bfloat16 [3072, 768], P('shard'), may hold values from -0.109375 to 0.109375
- b_down: bfloat16 [768], P('shard'), may hold values from -1.75 to 1.75
- cotangent: bfloat16 [16384, 768], P(('rep', 'shard')), may hold values from -6 to 6
- piece_slot: int32 [1024], replicated, may hold values from 0 to 1023, as said below
- lengths: int32 [32, 4], P(('rep', 'shard')), may hold values from 64 to 320, as said below
Outputs:
- block_output: bfloat16 [16384, 768], P(('rep', 'shard'))
- grad_tokens: bfloat16 [16384, 768], P(('rep', 'shard'))
- grad_ln1_scale: float32 [768], P('shard')
- grad_ln1_shift: float32 [768], P('shard')
- grad_w_query: float32 [768, 768], P('shard')
- grad_b_query: float32 [768], P('shard')
- grad_w_key: float32 [768, 768], P('shard')
- grad_b_key: float32 [768], P('shard')
- grad_w_value: float32 [768, 768], P('shard')
- grad_b_value: float32 [768], P('shard')
- grad_shift_taps: float32 [768, 64], P('shard')
- grad_ssm_coef: float32 [768, 64], P('shard')
- grad_ssm_rate: float32 [768, 64], P('shard')
- grad_ssm_skip: float32 [768], P('shard')
- grad_w_out: float32 [768, 768], P('shard')
- grad_b_out: float32 [768], P('shard')
- grad_ln2_scale: float32 [768], P('shard')
- grad_ln2_shift: float32 [768], P('shard')
- grad_w_up: float32 [768, 3072], P('shard')
- grad_b_up: float32 [3072], P('shard')
- grad_w_down: float32 [3072, 768], P('shard')
- grad_b_down: float32 [768], P('shard')
Inputs may be any that keep to these rules, and one draw needn't show every extreme that they name: piece_slot is a permutation of the slots; the 32 pieces of each device in the given order go one to each buffer (piece_slot // 32 takes every value once in each aligned block of 32 entries). `lengths`: each row holds one sequence of 320 tokens and three of 64 tokens, in some order (multiples of 64 that sum to 512).
All inputs are finite; a program needn't handle non-finite values.
Results may differ from a plain program's by a relative error of at most 0.02.
Values may be sent and summed in bfloat16 or wider, within the bound.
A program may use at most 256 MiB of HBM per device.

v0:
```python
import jax
import jax.numpy as jnp
from jax import lax
from jax.sharding import PartitionSpec as P

PRECISE = lax.Precision.HIGHEST
EPSILON = 1e-05


def to_float(array):
    return array.astype(jnp.float32)


def to_half(array):
    return array.astype(jnp.bfloat16)


def product(factor_one, factor_two):
    return jnp.dot(factor_one, factor_two, preferred_element_type=jnp.float32)


def product_left(factor_one, factor_two):
    return lax.dot_general(
        factor_one, factor_two, (((0,), (0,)), ((), ())), preferred_element_type=jnp.float32
    )


def product_right(factor_one, factor_two):
    return lax.dot_general(
        factor_one, factor_two, (((1,), (1,)), ((), ())), preferred_element_type=jnp.float32
    )


def layer_norm(values_in, scale_in, shift_in):
    average = jnp.mean(values_in, axis=-1, keepdims=True)
    centred = values_in - average
    spread = jnp.mean(centred * centred, axis=-1, keepdims=True)
    return centred * lax.rsqrt(spread + EPSILON) * scale_in + shift_in


def smooth_gate(values_in):
    return jax.nn.gelu(values_in, approximate=True)


def toeplitz_tables(tap_count):
    lag_index = lax.broadcasted_iota(jnp.int32, (tap_count, tap_count, tap_count), 0)
    row_index = lax.broadcasted_iota(jnp.int32, (tap_count, tap_count, tap_count), 1)
    col_index = lax.broadcasted_iota(jnp.int32, (tap_count, tap_count, tap_count), 2)
    lower_band = jnp.where(row_index - col_index == lag_index, 1.0, 0.0).astype(jnp.float32)
    upper_band = jnp.where(row_index - col_index + tap_count == lag_index, 1.0, 0.0).astype(
        jnp.float32
    )
    return (lower_band, upper_band)


def mixing(key_blocks, value_blocks, shift_taps, ssm_coef, ssm_rate, ssm_skip, carried):
    tap_count = shift_taps.shape[1]
    lower_band, upper_band = toeplitz_tables(tap_count)
    keys_low = to_half(key_blocks)
    near_taps = to_half(jnp.einsum("cj,jab->cab", shift_taps, lower_band))
    far_taps = to_half(jnp.einsum("cj,jab->cab", shift_taps, upper_band))
    before = jnp.concatenate([jnp.zeros_like(keys_low[:1]), keys_low[:-1]], axis=0)
    shifted = jnp.einsum("cab,ibc->iac", near_taps, keys_low, preferred_element_type=jnp.float32)
    shifted = shifted + carried[:, None, None] * jnp.einsum(
        "cab,ibc->iac", far_taps, before, preferred_element_type=jnp.float32
    )
    inputs = shifted * value_blocks
    inputs_low = to_half(inputs)
    lag_steps = jnp.arange(tap_count).astype(jnp.float32)
    decay_table = jnp.exp(-ssm_rate[:, :, None] * lag_steps[None, None, :])
    kernel = jnp.einsum("cn,cnm->cm", ssm_coef, decay_table, precision=PRECISE)
    inner_band = to_half(jnp.einsum("cm,mab->cab", kernel, lower_band, precision=PRECISE))
    within = jnp.einsum("cab,ibc->iac", inner_band, inputs_low, preferred_element_type=jnp.float32)
    tail_decay = to_half(jnp.flip(decay_table, axis=2))
    local_state = jnp.einsum(
        "cnb,ibc->icn", tail_decay, inputs_low, preferred_element_type=jnp.float32
    )
    block_decay = jnp.exp(-ssm_rate * tap_count)

    def advance(carried_state, step_input):
        fresh_state, keep_flag = step_input
        next_state = keep_flag * block_decay * carried_state + fresh_state
        return (next_state, carried_state)

    _, previous = lax.scan(advance, jnp.zeros_like(local_state[0]), (local_state, carried))
    previous_low = to_half(previous)
    lead_decay = to_half(ssm_coef[:, :, None] * decay_table * jnp.exp(-ssm_rate)[:, :, None])
    across = carried[:, None, None] * jnp.einsum(
        "cna,icn->iac", lead_decay, previous_low, preferred_element_type=jnp.float32
    )
    return within + across + ssm_skip * inputs


def carry_flags(length_list, block_count, tap_count):
    block_sizes = length_list // tap_count
    start_blocks = jnp.cumsum(block_sizes) - block_sizes
    block_ids = jnp.arange(block_count)
    opening = jnp.any(block_ids[:, None] == start_blocks[None, :], axis=1)
    return jnp.where(opening, 0.0, 1.0).astype(jnp.float32)


def forward_pass(balanced, weights, carried):
    (
        ln1_scale,
        ln1_shift,
        w_query,
        b_query,
        w_key,
        b_key,
        w_value,
        b_value,
        shift_taps,
        ssm_coef,
        ssm_rate,
        ssm_skip,
        w_out,
        b_out,
        ln2_scale,
        ln2_shift,
        w_up,
        b_up,
        w_down,
        b_down,
    ) = weights
    tap_count = shift_taps.shape[1]
    model_dim = balanced.shape[1]
    block_count = balanced.shape[0] // tap_count
    normed, first_back = jax.vjp(layer_norm, balanced, to_float(ln1_scale), to_float(ln1_shift))
    normed_low = normed.astype(jnp.bfloat16)
    queries = product(normed_low, w_query) + to_float(b_query)
    key_proj = product(normed_low, w_key) + to_float(b_key)
    value_proj = product(normed_low, w_value) + to_float(b_value)
    mixed_out, mix_back = jax.vjp(
        mixing,
        key_proj.reshape(block_count, tap_count, model_dim),
        value_proj.reshape(block_count, tap_count, model_dim),
        to_float(shift_taps),
        to_float(ssm_coef),
        to_float(ssm_rate),
        to_float(ssm_skip),
        carried,
    )
    mixed_flat = mixed_out.reshape(balanced.shape)
    gated_low = (queries * mixed_flat).astype(jnp.bfloat16)
    middle = balanced + (product(gated_low, w_out) + to_float(b_out))
    normed_two, second_back = jax.vjp(layer_norm, middle, to_float(ln2_scale), to_float(ln2_shift))
    second_low = normed_two.astype(jnp.bfloat16)
    hidden = product(second_low, w_up) + to_float(b_up)
    active, gelu_back = jax.vjp(smooth_gate, hidden)
    active_low = active.astype(jnp.bfloat16)
    result = middle + (product(active_low, w_down) + to_float(b_down))
    kept_state = (
        first_back,
        normed_low,
        queries,
        mix_back,
        mixed_flat,
        gated_low,
        second_back,
        second_low,
        gelu_back,
        active_low,
    )
    return (result, kept_state)


def backward_pass(weights, kept_state, grad_out):
    (
        ln1_scale,
        ln1_shift,
        w_query,
        b_query,
        w_key,
        b_key,
        w_value,
        b_value,
        shift_taps,
        ssm_coef,
        ssm_rate,
        ssm_skip,
        w_out,
        b_out,
        ln2_scale,
        ln2_shift,
        w_up,
        b_up,
        w_down,
        b_down,
    ) = weights
    (
        first_back,
        normed_low,
        queries,
        mix_back,
        mixed_flat,
        gated_low,
        second_back,
        second_low,
        gelu_back,
        active_low,
    ) = kept_state
    tap_count = shift_taps.shape[1]
    model_dim = grad_out.shape[1]
    block_count = grad_out.shape[0] // tap_count
    grad_low = grad_out.astype(jnp.bfloat16)
    grad_w_down = product_left(active_low, grad_low)
    grad_b_down = jnp.sum(grad_low, axis=0, dtype=jnp.float32)
    grad_hidden = gelu_back(product_right(grad_low, w_down))[0].astype(jnp.bfloat16)
    grad_w_up = product_left(second_low, grad_hidden)
    grad_b_up = jnp.sum(grad_hidden, axis=0, dtype=jnp.float32)
    grad_middle, grad_ln2_scale, grad_ln2_shift = second_back(product_right(grad_hidden, w_up))
    grad_middle = grad_middle + grad_out
    grad_branch = grad_middle.astype(jnp.bfloat16)
    grad_w_out = product_left(gated_low, grad_branch)
    grad_b_out = jnp.sum(grad_branch, axis=0, dtype=jnp.float32)
    grad_gated = product_right(grad_branch, w_out)
    grad_query = (grad_gated * mixed_flat).astype(jnp.bfloat16)
    grad_mixed = (grad_gated * queries).reshape(block_count, tap_count, model_dim)
    (
        grad_keys,
        grad_values,
        grad_shift_taps,
        grad_ssm_coef,
        grad_ssm_rate,
        grad_ssm_skip,
        grad_carry,
    ) = mix_back(grad_mixed)
    grad_key = grad_keys.reshape(grad_out.shape).astype(jnp.bfloat16)
    grad_value = grad_values.reshape(grad_out.shape).astype(jnp.bfloat16)
    grad_w_query = product_left(normed_low, grad_query)
    grad_w_key = product_left(normed_low, grad_key)
    grad_w_value = product_left(normed_low, grad_value)
    grad_b_query = jnp.sum(grad_query, axis=0, dtype=jnp.float32)
    grad_b_key = jnp.sum(grad_key, axis=0, dtype=jnp.float32)
    grad_b_value = jnp.sum(grad_value, axis=0, dtype=jnp.float32)
    grad_normed = (
        product_right(grad_query, w_query)
        + product_right(grad_key, w_key)
        + product_right(grad_value, w_value)
    )
    grad_input, grad_ln1_scale, grad_ln1_shift = first_back(grad_normed)
    grad_input = grad_input + grad_middle
    grad_terms = (
        grad_ln1_scale,
        grad_ln1_shift,
        grad_w_query,
        grad_b_query,
        grad_w_key,
        grad_b_key,
        grad_w_value,
        grad_b_value,
        grad_shift_taps,
        grad_ssm_coef,
        grad_ssm_rate,
        grad_ssm_skip,
        grad_w_out,
        grad_b_out,
        grad_ln2_scale,
        grad_ln2_shift,
        grad_w_up,
        grad_b_up,
        grad_w_down,
        grad_b_down,
    )
    return (grad_input, grad_terms)


def local(
    tokens,
    ln1_scale,
    ln1_shift,
    w_query,
    b_query,
    w_key,
    b_key,
    w_value,
    b_value,
    shift_taps,
    ssm_coef,
    ssm_rate,
    ssm_skip,
    w_out,
    b_out,
    ln2_scale,
    ln2_shift,
    w_up,
    b_up,
    w_down,
    b_down,
    cotangent,
    piece_slot,
    lengths,
):
    rep_count = lax.axis_size("rep")
    shard_count = lax.axis_size("shard")
    slot_count = rep_count * shard_count
    my_index = lax.axis_index("rep") * shard_count + lax.axis_index("shard")
    model_dim = tokens.shape[1]
    piece_rows = tokens.shape[0] // slot_count
    tap_count = shift_taps.shape[1]
    block_count = tokens.shape[0] // tap_count
    slot_table = piece_slot.reshape(slot_count, slot_count)
    target = slot_table // slot_count
    landing = slot_table % slot_count
    own_target = lax.dynamic_index_in_dim(target, my_index, 0, keepdims=False)
    sending = jnp.argsort(own_target)
    arrival = jnp.sum(jnp.where(target == my_index, landing, 0), axis=1)
    unpacking = jnp.argsort(arrival)
    token_pieces = tokens.reshape(slot_count, piece_rows, model_dim)[sending]
    cot_pieces = cotangent.reshape(slot_count, piece_rows, model_dim)[sending]
    arrived = (
        lax.all_to_all(token_pieces, ("rep", "shard"), split_axis=0, concat_axis=0, tiled=True),
        lax.all_to_all(cot_pieces, ("rep", "shard"), split_axis=0, concat_axis=0, tiled=True),
    )
    balanced = to_float(arrived[0][unpacking].reshape(-1, model_dim))
    grad_out = to_float(arrived[1][unpacking].reshape(-1, model_dim))
    carried = carry_flags(lengths[0], block_count, tap_count)
    weights = (
        lax.all_gather(ln1_scale, "shard", axis=0, tiled=True),
        lax.all_gather(ln1_shift, "shard", axis=0, tiled=True),
        lax.all_gather(w_query, "shard", axis=0, tiled=True),
        lax.all_gather(b_query, "shard", axis=0, tiled=True),
        lax.all_gather(w_key, "shard", axis=0, tiled=True),
        lax.all_gather(b_key, "shard", axis=0, tiled=True),
        lax.all_gather(w_value, "shard", axis=0, tiled=True),
        lax.all_gather(b_value, "shard", axis=0, tiled=True),
        lax.all_gather(shift_taps, "shard", axis=0, tiled=True),
        lax.all_gather(ssm_coef, "shard", axis=0, tiled=True),
        lax.all_gather(ssm_rate, "shard", axis=0, tiled=True),
        lax.all_gather(ssm_skip, "shard", axis=0, tiled=True),
        lax.all_gather(w_out, "shard", axis=0, tiled=True),
        lax.all_gather(b_out, "shard", axis=0, tiled=True),
        lax.all_gather(ln2_scale, "shard", axis=0, tiled=True),
        lax.all_gather(ln2_shift, "shard", axis=0, tiled=True),
        lax.all_gather(w_up, "shard", axis=0, tiled=True),
        lax.all_gather(b_up, "shard", axis=0, tiled=True),
        lax.all_gather(w_down, "shard", axis=0, tiled=True),
        lax.all_gather(b_down, "shard", axis=0, tiled=True),
    )
    result, unused_state = forward_pass(balanced, weights, carried)
    out_low = result.astype(jnp.bfloat16)
    weights_two = (
        lax.all_gather(ln1_scale, "shard", axis=0, tiled=True),
        lax.all_gather(ln1_shift, "shard", axis=0, tiled=True),
        lax.all_gather(w_query, "shard", axis=0, tiled=True),
        lax.all_gather(b_query, "shard", axis=0, tiled=True),
        lax.all_gather(w_key, "shard", axis=0, tiled=True),
        lax.all_gather(b_key, "shard", axis=0, tiled=True),
        lax.all_gather(w_value, "shard", axis=0, tiled=True),
        lax.all_gather(b_value, "shard", axis=0, tiled=True),
        lax.all_gather(shift_taps, "shard", axis=0, tiled=True),
        lax.all_gather(ssm_coef, "shard", axis=0, tiled=True),
        lax.all_gather(ssm_rate, "shard", axis=0, tiled=True),
        lax.all_gather(ssm_skip, "shard", axis=0, tiled=True),
        lax.all_gather(w_out, "shard", axis=0, tiled=True),
        lax.all_gather(b_out, "shard", axis=0, tiled=True),
        lax.all_gather(ln2_scale, "shard", axis=0, tiled=True),
        lax.all_gather(ln2_shift, "shard", axis=0, tiled=True),
        lax.all_gather(w_up, "shard", axis=0, tiled=True),
        lax.all_gather(b_up, "shard", axis=0, tiled=True),
        lax.all_gather(w_down, "shard", axis=0, tiled=True),
        lax.all_gather(b_down, "shard", axis=0, tiled=True),
    )
    result_two, kept_state = forward_pass(balanced, weights_two, carried)
    grad_input, grad_terms = backward_pass(weights_two, kept_state, grad_out)
    out_pieces = out_low.reshape(slot_count, piece_rows, model_dim)[arrival]
    grad_pieces = grad_input.astype(jnp.bfloat16).reshape(slot_count, piece_rows, model_dim)[
        arrival
    ]
    returned = (
        lax.all_to_all(out_pieces, ("rep", "shard"), split_axis=0, concat_axis=0, tiled=True),
        lax.all_to_all(grad_pieces, ("rep", "shard"), split_axis=0, concat_axis=0, tiled=True),
    )
    block_output = returned[0][own_target].reshape(-1, model_dim)
    grad_tokens = returned[1][own_target].reshape(-1, model_dim)
    (
        g_ln1_scale,
        g_ln1_shift,
        g_w_query,
        g_b_query,
        g_w_key,
        g_b_key,
        g_w_value,
        g_b_value,
        g_shift_taps,
        g_ssm_coef,
        g_ssm_rate,
        g_ssm_skip,
        g_w_out,
        g_b_out,
        g_ln2_scale,
        g_ln2_shift,
        g_w_up,
        g_b_up,
        g_w_down,
        g_b_down,
    ) = grad_terms
    grad_parts = (
        lax.psum_scatter(
            g_ln1_scale.astype(jnp.bfloat16), "shard", scatter_dimension=0, tiled=True
        ).astype(jnp.float32),
        lax.psum_scatter(
            g_ln1_shift.astype(jnp.bfloat16), "shard", scatter_dimension=0, tiled=True
        ).astype(jnp.float32),
        lax.psum_scatter(
            g_w_query.astype(jnp.bfloat16), "shard", scatter_dimension=0, tiled=True
        ).astype(jnp.float32),
        lax.psum_scatter(
            g_b_query.astype(jnp.bfloat16), "shard", scatter_dimension=0, tiled=True
        ).astype(jnp.float32),
        lax.psum_scatter(
            g_w_key.astype(jnp.bfloat16), "shard", scatter_dimension=0, tiled=True
        ).astype(jnp.float32),
        lax.psum_scatter(
            g_b_key.astype(jnp.bfloat16), "shard", scatter_dimension=0, tiled=True
        ).astype(jnp.float32),
        lax.psum_scatter(
            g_w_value.astype(jnp.bfloat16), "shard", scatter_dimension=0, tiled=True
        ).astype(jnp.float32),
        lax.psum_scatter(
            g_b_value.astype(jnp.bfloat16), "shard", scatter_dimension=0, tiled=True
        ).astype(jnp.float32),
        lax.psum_scatter(
            g_shift_taps.astype(jnp.bfloat16), "shard", scatter_dimension=0, tiled=True
        ).astype(jnp.float32),
        lax.psum_scatter(
            g_ssm_coef.astype(jnp.bfloat16), "shard", scatter_dimension=0, tiled=True
        ).astype(jnp.float32),
        lax.psum_scatter(
            g_ssm_rate.astype(jnp.bfloat16), "shard", scatter_dimension=0, tiled=True
        ).astype(jnp.float32),
        lax.psum_scatter(
            g_ssm_skip.astype(jnp.bfloat16), "shard", scatter_dimension=0, tiled=True
        ).astype(jnp.float32),
        lax.psum_scatter(
            g_w_out.astype(jnp.bfloat16), "shard", scatter_dimension=0, tiled=True
        ).astype(jnp.float32),
        lax.psum_scatter(
            g_b_out.astype(jnp.bfloat16), "shard", scatter_dimension=0, tiled=True
        ).astype(jnp.float32),
        lax.psum_scatter(
            g_ln2_scale.astype(jnp.bfloat16), "shard", scatter_dimension=0, tiled=True
        ).astype(jnp.float32),
        lax.psum_scatter(
            g_ln2_shift.astype(jnp.bfloat16), "shard", scatter_dimension=0, tiled=True
        ).astype(jnp.float32),
        lax.psum_scatter(
            g_w_up.astype(jnp.bfloat16), "shard", scatter_dimension=0, tiled=True
        ).astype(jnp.float32),
        lax.psum_scatter(
            g_b_up.astype(jnp.bfloat16), "shard", scatter_dimension=0, tiled=True
        ).astype(jnp.float32),
        lax.psum_scatter(
            g_w_down.astype(jnp.bfloat16), "shard", scatter_dimension=0, tiled=True
        ).astype(jnp.float32),
        lax.psum_scatter(
            g_b_down.astype(jnp.bfloat16), "shard", scatter_dimension=0, tiled=True
        ).astype(jnp.float32),
    )
    grad_owned = (
        lax.psum(grad_parts[0].astype(jnp.bfloat16), "rep").astype(jnp.float32),
        lax.psum(grad_parts[1].astype(jnp.bfloat16), "rep").astype(jnp.float32),
        lax.psum(grad_parts[2].astype(jnp.bfloat16), "rep").astype(jnp.float32),
        lax.psum(grad_parts[3].astype(jnp.bfloat16), "rep").astype(jnp.float32),
        lax.psum(grad_parts[4].astype(jnp.bfloat16), "rep").astype(jnp.float32),
        lax.psum(grad_parts[5].astype(jnp.bfloat16), "rep").astype(jnp.float32),
        lax.psum(grad_parts[6].astype(jnp.bfloat16), "rep").astype(jnp.float32),
        lax.psum(grad_parts[7].astype(jnp.bfloat16), "rep").astype(jnp.float32),
        lax.psum(grad_parts[8].astype(jnp.bfloat16), "rep").astype(jnp.float32),
        lax.psum(grad_parts[9].astype(jnp.bfloat16), "rep").astype(jnp.float32),
        lax.psum(grad_parts[10].astype(jnp.bfloat16), "rep").astype(jnp.float32),
        lax.psum(grad_parts[11].astype(jnp.bfloat16), "rep").astype(jnp.float32),
        lax.psum(grad_parts[12].astype(jnp.bfloat16), "rep").astype(jnp.float32),
        lax.psum(grad_parts[13].astype(jnp.bfloat16), "rep").astype(jnp.float32),
        lax.psum(grad_parts[14].astype(jnp.bfloat16), "rep").astype(jnp.float32),
        lax.psum(grad_parts[15].astype(jnp.bfloat16), "rep").astype(jnp.float32),
        lax.psum(grad_parts[16].astype(jnp.bfloat16), "rep").astype(jnp.float32),
        lax.psum(grad_parts[17].astype(jnp.bfloat16), "rep").astype(jnp.float32),
        lax.psum(grad_parts[18].astype(jnp.bfloat16), "rep").astype(jnp.float32),
        lax.psum(grad_parts[19].astype(jnp.bfloat16), "rep").astype(jnp.float32),
    )
    return (
        block_output,
        grad_tokens,
        grad_owned[0],
        grad_owned[1],
        grad_owned[2],
        grad_owned[3],
        grad_owned[4],
        grad_owned[5],
        grad_owned[6],
        grad_owned[7],
        grad_owned[8],
        grad_owned[9],
        grad_owned[10],
        grad_owned[11],
        grad_owned[12],
        grad_owned[13],
        grad_owned[14],
        grad_owned[15],
        grad_owned[16],
        grad_owned[17],
        grad_owned[18],
        grad_owned[19],
    )


def solution(mesh):
    in_specs = (
        P(("rep", "shard"), None),
        P("shard"),
        P("shard"),
        P("shard", None),
        P("shard"),
        P("shard", None),
        P("shard"),
        P("shard", None),
        P("shard"),
        P("shard", None),
        P("shard", None),
        P("shard", None),
        P("shard"),
        P("shard", None),
        P("shard"),
        P("shard"),
        P("shard"),
        P("shard", None),
        P("shard"),
        P("shard", None),
        P("shard"),
        P(("rep", "shard"), None),
        P(),
        P(("rep", "shard"), None),
    )
    out_specs = (
        P(("rep", "shard"), None),
        P(("rep", "shard"), None),
        P("shard"),
        P("shard"),
        P("shard", None),
        P("shard"),
        P("shard", None),
        P("shard"),
        P("shard", None),
        P("shard"),
        P("shard", None),
        P("shard", None),
        P("shard", None),
        P("shard"),
        P("shard", None),
        P("shard"),
        P("shard"),
        P("shard"),
        P("shard", None),
        P("shard"),
        P("shard", None),
        P("shard"),
    )
    return jax.shard_map(local, mesh=mesh, in_specs=in_specs, out_specs=out_specs, check_vma=False)
```

profile of v0, /device:TPU:1, one launch (start us, length us, event | category | flops | bytes accessed | tf_op | source)
XLA Modules:
  0.0 1280.7 jit_solution(3487228852720723063)
XLA Ops:
  26.0 37.2 %all-gather = bf16[4,192,64]{1,2,0:T(8,128)(2,1)S(1)} all-gather(bf16[1,192,64]{1,2,0:T(8,128)(2,1)S(1)} %bitcast.290), channel_id=1, replica_groups=mesh['rep'=8,'shard'=4] {'shard'}, dimensions={0}, use_global_device_ids=true | all-gather | bytes 122880 | tf_op jit(solution)/shard_map/all_gather | solution.py:327
  68.6 11.4 all-gather.2
  80.3 12.0 all-gather.1
  111.8 12.3 fusion.178
  124.2 12.7 all-to-all-start.2
  141.3 38.6 %all-reduce.26 = (bf16[768]{0:T(1024)(128)(2,1)S(1)}, bf16[768]{0:T(1024)(128)(2,1)S(1)}, bf16[768]{0:T(1024)(128)(2,1)S(1)}, bf16[768]{0:T(1024)(128)(2,1)S(1)}...) all-reduce(bf16[768]{0:T(1024)(128)(2,1)S(1)} %dynamic-update-slice, ...), channel_id=1, replica_groups=mesh['rep'=8,'shard'=4] {'shard'}, use_global_device_ids=true, to_apply=%add.3 | all-reduce | flops 6912 | bytes 27648
  181.7 18.6 %copy.229 = bf16[768,64,64]{2,1,0:T(8,128)(2,1)} copy(bf16[768,64,64]{0,2,1:T(8,128)(2,1)} %convert_bitcast_fusion.1) | data formatting | bytes 12582912 | tf_op jit(solution)/shard_map/jvp()/convert_element_type | solution.py:15
  200.2 18.5 %copy.232 = bf16[768,64,64]{2,1,0:T(8,128)(2,1)} copy(bf16[768,64,64]{0,2,1:T(8,128)(2,1)} %convert_bitcast_fusion) | data formatting | bytes 12582912 | tf_op jit(solution)/shard_map/jvp()/convert_element_type | solution.py:15
  218.7 8.2 convert_element_type.430
  226.9 18.5 %copy.240 = bf16[768,64,64]{2,1,0:T(8,128)(2,1)} copy(bf16[768,64,64]{0,2,1:T(8,128)(2,1)} %convert_element_type.430) | data formatting | bytes 12582912 | tf_op jit(solution)/shard_map/jvp()/convert_element_type | solution.py:15
  245.4 18.5 %copy.246 = bf16[768,64,64]{2,1,0:T(8,128)(2,1)} copy(bf16[768,64,64]{0,2,1:T(8,128)(2,1)} %get-tuple-element.559) | data formatting | bytes 12582912 | tf_op jit(solution)/shard_map/jvp()/convert_element_type | solution.py:15
  263.8 15.5 %rev.9 = bf16[768,64,64]{0,2,1:T(8,128)(2,1)} reverse(bf16[768,64,64]{0,2,1:T(8,128)(2,1)} %multiply_exponential_fusion), dimensions={2} | reverse | bytes 12582912 | tf_op jit(solution)/shard_map/jvp(jit(_flip))/rev | solution.py:74
  279.3 18.5 %copy.242 = bf16[768,64,64]{2,1,0:T(8,128)(2,1)} copy(bf16[768,64,64]{0,2,1:T(8,128)(2,1)} %rev.9) | data formatting | bytes 12582912 | tf_op jit(solution)/shard_map/jvp()/convert_element_type | solution.py:15
  298.5 11.2 all-gather.3
  325.6 10.6 fusion.177
  341.6 13.3 %fusion.77 = f32[768,8,64]{2,1,0:T(8,128)} fusion(bf16[768,64,64]{2,1,0:T(8,128)(2,1)} %copy.232, bf16[7,64,768]{1,0,2:T(8,128)(2,1)} %copy.230), kind=kOutput, calls=%fused_computation.153 | convolution fusion | flops 50331648 | bytes 8552448 | tf_op jit(solution)/shard_map/jvp(cab,ibc->iac)/dot_general | solution.py:64
  364.5 11.2 fusion.179
  379.0 9.0 convolution_bitcast_fusion
  394.1 32.7 %while.48 = (s32[]{:T(128)}, f32[768,64]{1,0:T(8,128)S(1)}, f32[8,768,64]{2,1,0:T(8,128)}, f32[8,768,64]{2,1,0:T(8,128)}, f32[8]{0:T(128)S(1)}, /*index=5*/f32[7...) while((s32[]{:T(128)}, f32[768,64]{1,0:T(8,128)S(1)}, ...), condition=%wide.region_12.13_spmd.clone, body=%wide.region_11.12_spmd.clone.sunk | while | flops 294915 | bytes 1966728 | solution.py:85
  430.1 9.2 fusion.74
  442.7 20.4 %while.47 = (s32[]{:T(128)}, f32[768,64]{1,0:T(8,128)S(1)}, bf16[8,768,64]{2,1,0:T(8,128)(2,1)S(1)}, f32[8]{0:T(128)S(1)}, f32[768,64]{1,0:T(8,128)S(1)}, /*index=5*/f32[8,768,64]{2,1,0:T(8,128)}, s32[]{:T(128)}, s32[]{:T(128)}) while((s32[]{:T(128)}, f32[768,64]{1,0:T(8,128)S(1)}, bf16[8,768,64]{2,1,0:T(8,128)(2,1)S(1)}, ...), condition=%wide.region_8.9_spmd.clone, body=%wide.region_7.8_spmd.clone.sunk | while | flops 245763 | bytes 1376384 | solution.py:85
  463.1 8.9 fusion.69
  495.0 10.2 fusion.162
  517.3 13.4 %convert_bitcast_fusion.2 = f32[8,768,64]{2,0,1:T(8,128)} fusion(bf16[768,8,64]{2,1,0:T(8,128)(2,1)} %copy.254, bf16[768,64,64]{2,1,0:T(8,128)(2,1)} %copy.246), kind=kOutput, calls=%fused_computation.69 | convolution fusion | flops 50724864 | bytes 8650752 | tf_op jit(solution)/shard_map/transpose(jvp(cna,icn->iac))/dot_general | solution.py:88
  530.7 7.7 fusion.72
  540.7 9.7 fusion.181
  556.8 44.1 %while.49 = (s32[]{:T(128)}, f32[768,64]{1,0:T(8,128)S(1)}, f32[768,64]{1,0:T(8,128)S(1)}, bf16[8,768,64]{2,1,0:T(8,128)(2,1)}, f32[8]{0:T(128)S(1)}, /*index=5*...) while((s32[]{:T(128)}, f32[768,64]{1,0:T(8,128)S(1)}, ...), condition=%wide.region_18.19_spmd.clone, body=%wide.region_17.18_spmd.clone.sunk | while | flops 393220 | bytes 2162856 | solution.py:85
  601.0 9.8 fusion.42
  610.8 7.9 fusion.40
  634.2 9.9 fusion.184
  644.2 13.7 %fusion.84 = f32[768,64]{0,1:T(8,128)S(1)} fusion(bf16[768,64,64]{2,1,0:T(8,128)(2,1)} %fusion.184), kind=kOutput, calls=%fused_computation.156 | convolution fusion | flops 403439616 | bytes 6488064 | tf_op jit(solution)/shard_map/transpose(jvp(cj,jab->cab))/dot_general | solution.py:60
  664.4 10.1 fusion.99
  675.5 19.6 %copy.275 = bf16[768,64,64]{0,2,1:T(8,128)(2,1)} copy(bf16[768,64,64]{1,2,0:T(8,128)(2,1)} %fusion.72) | data formatting | bytes 12582912 | tf_op jit(solution)/shard_map/transpose(jvp(cna,icn->iac))/dot_general | solution.py:88
  695.0 20.7 %fusion.89 = f32[768,64]{0,1:T(8,128)S(1)} fusion(bf16[768,64,64]{2,1,0:T(8,128)(2,1)} %fusion.183), kind=kOutput, calls=%fused_computation.157 | convolution fusion | flops 2416705536 | bytes 6488064 | tf_op jit(solution)/shard_map/transpose(jvp(cm,mab->cab))/dot_general | solution.py:72
  715.7 15.2 %copy.284 = bf16[768,64,64]{0,2,1:T(8,128)(2,1)} copy(bf16[768,64,64]{2,1,0:T(8,128)(2,1)} %fusion.40) | data formatting | bytes 12582912 | tf_op jit(solution)/shard_map/transpose(jvp(cnb,ibc->icn))/dot_general | solution.py:75
  730.9 16.6 %rev.10 = f32[768,64,64]{0,2,1:T(8,128)} reverse(bf16[768,64,64]{0,2,1:T(8,128)(2,1)} %copy.284), dimensions={2} | reverse | bytes 18874368 | tf_op jit(solution)/shard_map/transpose(jvp(jit(_flip)))/rev | solution.py:74
  751.0 14.6 %fusion.11 = (f32[768,64]{0,1:T(8,128)}, f32[768,64]{0,1:T(8,128)}, f32[768,64]{0,1:T(8,128)S(1)}) fusion(f32[768,64]{0,1:T(8,128)S(1)} %copy-done.35, f32[64]{0:T(128)S(1)} %copy-done.97, f32[768,64]{0,1:T(8,128)S(1)} %copy-done.33, bf16[768,64,64]{0,2,1:T(8,128)(2,1)} %copy.275, f32[768,64]{0,1:T(8,128)} %copy-done.62, f32[768,64,64]{0,2,1:T(8,128)} %rev.10, ...), kind=kLoop, calls=%fused_computation.30 | loop fusion | flops 47038464 | bytes 20250880 | tf_op jit(solution)/shard_map/transpose(jvp())/reduce_sum | solution.py:87
  787.6 9.4 fusion.175
  815.3 8.6 convolution_convert_fusion.3
  835.0 14.9 %all-reduce.25 = (bf16[768]{0:T(1024)(128)(2,1)S(1)}, bf16[768]{0:T(1024)(128)(2,1)S(1)}, bf16[768]{0:T(1024)(128)(2,1)S(1)}, bf16[768]{0:T(1024)(128)(2,1)S(1)}...) all-reduce(bf16[768]{0:T(1024)(128)(2,1)S(1)} %copy-done.93, ...), channel_id=1, replica_groups=mesh['rep'=8,'shard'=4] {'shard'}, use_global_device_ids=true, to_apply=%add.11 | all-reduce | flops 11520 | bytes 46080
  849.9 11.0 add_convert_fusion.2
  863.7 11.7 all-to-all-start.1
  887.9 26.9 %reduce-scatter.20.cloned.1.call-done = bf16[192,768]{1,0:T(8,128)(2,1)} async-done(((bf16[768,768]{1,0:T(8,128)(2,1)}), bf16[192,768]{1,0:T(8,128)(2,1)}) %reduce-scatter.20.cloned.1.call-update) | async-done | bytes 294928 | tf_op jit(solution)/shard_map/reduce_scatter | solution.py:417
  914.9 30.8 %reduce-scatter.22.cloned.1.call-done = bf16[192,768]{1,0:T(8,128)(2,1)} async-done(((bf16[768,768]{1,0:T(8,128)(2,1)}), bf16[192,768]{1,0:T(8,128)(2,1)}) %reduce-scatter.22.cloned.1.call-update) | async-done | bytes 294928 | tf_op jit(solution)/shard_map/reduce_scatter | solution.py:435
  945.7 86.5 %reduce-scatter.24.cloned.1.call-done = bf16[192,3072]{1,0:T(8,128)(2,1)} async-done(((bf16[768,3072]{1,0:T(8,128)(2,1)}), bf16[192,3072]{1,0:T(8,128)(2,1)}) %reduce-scatter.24.cloned.1.call-update) | async-done | bytes 1179664 | tf_op jit(solution)/shard_map/reduce_scatter | solution.py:447
  1032.1 88.1 %reduce-scatter.26.cloned.1.call-done = bf16[768,768]{1,0:T(8,128)(2,1)} async-done(((bf16[3072,768]{1,0:T(8,128)(2,1)}), bf16[768,768]{1,0:T(8,128)(2,1)}) %reduce-scatter.26.cloned.1.call-update) | async-done | bytes 1179664 | tf_op jit(solution)/shard_map/reduce_scatter | solution.py:453
  1132.8 53.9 %all-reduce.30.cloned.1.call-done = (bf16[192]{0:T(256)(128)(2,1)}, bf16[192]{0:T(256)(128)(2,1)}, bf16[192]{0:T(256)(128)(2,1)}, bf16[192]{0:T(256)(128)(2,1)},...) async-done(((bf16[192]{0:T(256)(128)(2,1)}, ...) | async-done | bytes 79120 | tf_op jit(solution)/shard_map/psum | solution.py:461
  1208.3 56.9 %all-reduce.32.cloned.1.call-done = (bf16[192,768]{1,0:T(8,128)(2,1)}, bf16[192,768]{1,0:T(8,128)(2,1)}, bf16[192,768]{1,0:T(8,128)(2,1)}, bf16[192,768]{1,0:T(8...) async-done(((bf16[192,768]{1,0:T(8,128)(2,1)}, bf16[192,768]{1,0:T(8,128)(2,1)}, bf16[192,768]{1,0:T(8,128)(2,1)}, bf16[192,768]{1,0:T(8,128)(2,1)}, ...) | async-done | bytes 3538960 | tf_op jit(solution)/shard_map/psum | solution.py:463
  (578 shorter events, 370.8 us)
Async XLA Ops:
  7.2 311.8 %all-gather.13.cloned.1.call-start = ((), (), s32[]{:S(2)}) async-start(), calls=%async_computation.14 | async-start | bytes 1474560 | tf_op jit(solution)/shard_map/all_gather | solution.py:323
  8.0 350.2 %all-gather.15.cloned.1.call-start = ((), (), s32[]{:S(2)}) async-start(), calls=%async_computation.15 | async-start | bytes 1474560 | tf_op jit(solution)/shard_map/all_gather | solution.py:325
  8.7 471.3 %all-gather.11.cloned.1.call-start = ((), (), s32[]{:S(2)}) async-start(), calls=%async_computation.13 | async-start | bytes 1474560 | tf_op jit(solution)/shard_map/all_gather | solution.py:321
  9.4 475.3 %all-gather.17.cloned.1.call-start = ((), (), s32[]{:S(2)}) async-start(), calls=%async_computation.16 | async-start | bytes 1474560 | tf_op jit(solution)/shard_map/all_gather | solution.py:331
  10.0 477.5 %all-gather.19.cloned.1.call-start = ((), (), s32[]{:S(2)}) async-start(), calls=%async_computation.17 | async-start | bytes 5898240 | tf_op jit(solution)/shard_map/all_gather | solution.py:335
  14.5 109.7 %all-to-all-start = ((bf16[32,16,768]{2,1,0:T(8,128)(2,1)}), bf16[32,16,768]{2,1,0:T(8,128)(2,1)}, u32[]{:S(2)}, u32[]{:S(2)}) async-start(bf16[32,16,768]{2,1,0:T(8,128)(2,1)} %gather_fusion), calls=%async_computation | async-start | bytes 1572864 | tf_op jit(solution)/shard_map/all_to_all | solution.py:312
  21.7 473.3 %all-gather.21.cloned.1.call-start = ((), (), s32[]{:S(2)}) async-start(), calls=%async_computation.18 | async-start | bytes 5898240 | tf_op jit(solution)/shard_map/all_gather | solution.py:337
  22.3 84.2 %copy-start.96 = (f32[64]{0:T(128)}, f32[64]{0:T(128)S(1)}, u32[]{:S(2)}) copy-start(f32[64]{0:T(128)S(1)} %iota_convert_fusion) | copy-start | bytes 772
  63.4 16.9 %copy-start.72 = (bf16[192,64]{0,1:T(8,128)(2,1)S(1)}, bf16[192,64]{0,1:T(8,128)(2,1)}, u32[]{:S(2)}) copy-start(bf16[192,64]{0,1:T(8,128)(2,1)} %param.41) | copy-start | bytes 73732
  80.3 26.2 %copy-start.34 = (f32[768,64]{0,1:T(8,128)}, f32[768,64]{0,1:T(8,128)S(1)}, u32[]{:S(2)}) copy-start(f32[768,64]{0,1:T(8,128)S(1)} %convert.10) | copy-start | bytes 589828
  92.8 13.7 %copy-start.43 = (f32[768,64]{0,1:T(8,128)}, f32[768,64]{0,1:T(8,128)S(1)}, u32[]{:S(2)}) copy-start(f32[768,64]{0,1:T(8,128)S(1)} %copy.244) | copy-start | bytes 589828
  124.1 15.0 %copy-start.115 = (bf16[192]{0:T(256)(128)(2,1)S(1)}, bf16[192]{0:T(256)(128)(2,1)}, u32[]{:S(2)}) copy-start(bf16[192]{0:T(256)(128)(2,1)} %param.32) | copy-start | bytes 1156
  124.1 15.3 %copy-start.116 = (bf16[192]{0:T(256)(128)(2,1)S(1)}, bf16[192]{0:T(256)(128)(2,1)}, u32[]{:S(2)}) copy-start(bf16[192]{0:T(256)(128)(2,1)} %param.31) | copy-start | bytes 1156
  124.1 15.5 %copy-start.117 = (bf16[192]{0:T(256)(128)(2,1)S(1)}, bf16[192]{0:T(256)(128)(2,1)}, u32[]{:S(2)}) copy-start(bf16[192]{0:T(256)(128)(2,1)} %param.34) | copy-start | bytes 1156
  124.1 15.7 %copy-start.118 = (bf16[192]{0:T(256)(128)(2,1)S(1)}, bf16[192]{0:T(256)(128)(2,1)}, u32[]{:S(2)}) copy-start(bf16[192]{0:T(256)(128)(2,1)} %param.38) | copy-start | bytes 1156
  124.1 16.0 %copy-start.119 = (bf16[192]{0:T(256)(128)(2,1)S(1)}, bf16[192]{0:T(256)(128)(2,1)}, u32[]{:S(2)}) copy-start(bf16[192]{0:T(256)(128)(2,1)} %param.36) | copy-start | bytes 1156
  124.1 16.2 %copy-start.120 = (bf16[192]{0:T(256)(128)(2,1)S(1)}, bf16[192]{0:T(256)(128)(2,1)}, u32[]{:S(2)}) copy-start(bf16[192]{0:T(256)(128)(2,1)} %param.42) | copy-start | bytes 1156
  124.1 16.4 %copy-start.121 = (bf16[192]{0:T(256)(128)(2,1)S(1)}, bf16[192]{0:T(256)(128)(2,1)}, u32[]{:S(2)}) copy-start(bf16[192]{0:T(256)(128)(2,1)} %param.44) | copy-start | bytes 1156
  124.2 16.6 %copy-start.122 = (bf16[192]{0:T(256)(128)(2,1)S(1)}, bf16[192]{0:T(256)(128)(2,1)}, u32[]{:S(2)}) copy-start(bf16[192]{0:T(256)(128)(2,1)} %param.46) | copy-start | bytes 1156
  124.2 16.9 %copy-start.123 = (bf16[192]{0:T(256)(128)(2,1)S(1)}, bf16[192]{0:T(256)(128)(2,1)}, u32[]{:S(2)}) copy-start(bf16[192]{0:T(256)(128)(2,1)} %param.45) | copy-start | bytes 1156
  124.2 192.0 %all-to-all-start.2 = ((bf16[32,16,768]{2,1,0:T(8,128)(2,1)}), bf16[32,16,768]{2,1,0:T(8,128)(2,1)}, u32[]{:S(2)}, u32[]{:S(2)}) async-start(bf16[32,16,768]{2,1,0:T(8,128)(2,1)} %gather_fusion.4), calls=%async_computation.2 | async-start | bytes 1572864 | tf_op jit(solution)/shard_map/all_to_all | solution.py:313
  136.9 746.4 %reduce-scatter.28.cloned.1.call-start = ((), (), s32[]{:S(2)}) async-start(), calls=%async_computation.25 | async-start | bytes 245760
  137.7 160.1 %copy-start.6 = (bf16[8,768,64]{2,1,0:T(8,128)(2,1)}, bf16[8,768,64]{2,1,0:T(8,128)(2,1)S(1)}, u32[]{:S(2)}) copy-start(bf16[8,768,64]{2,1,0:T(8,128)(2,1)S(1)} %fusion.172) | copy-start | bytes 2359300
  180.5 135.3 %copy-start.68 = (f32[768]{0:T(1024)}, f32[768]{0:T(1024)S(1)}, u32[]{:S(2)}) copy-start(f32[768]{0:T(1024)S(1)} %convert_element_type.416) | copy-start | bytes 9220
  180.5 135.3 %copy-start.63 = (f32[768]{0:T(1024)}, f32[768]{0:T(1024)S(1)}, u32[]{:S(2)}) copy-start(f32[768]{0:T(1024)S(1)} %convert_element_type.415) | copy-start | bytes 9220
  297.8 13.7 %copy-start.111 = (s32[32]{0:T(128)S(1)}, s32[32]{0:T(128)}, u32[]{:S(2)}) copy-start(s32[32]{0:T(128)} %compare_select_fusion.2) | copy-start | bytes 388
  338.6 22.0 %copy-start.12 = (f32[768,8,64]{0,2,1:T(8,128)}, f32[768,8,64]{0,2,1:T(8,128)S(1)}, u32[]{:S(2)}) copy-start(f32[768,8,64]{0,2,1:T(8,128)S(1)} %copy.234) | copy-start | bytes 4718596
  364.5 14.5 %copy-start.3 = (bf16[8,64,768]{1,0,2:T(8,128)(2,1)}, bf16[8,64,768]{1,0,2:T(8,128)(2,1)S(1)}, u32[]{:S(2)}) copy-start(bf16[8,64,768]{1,0,2:T(8,128)(2,1)S(1)} %copy.239) | copy-start | bytes 2359300
  487.1 21.6 %copy-start.30 = (f32[512,768]{1,0:T(8,128)}, f32[512,768]{1,0:T(8,128)S(1)}, u32[]{:S(2)}) copy-start(f32[512,768]{1,0:T(8,128)S(1)} %get-tuple-element.571) | copy-start | bytes 4718596
  487.5 21.3 %copy-start.90 = (f32[512]{0:T(512)}, f32[512]{0:T(512)S(1)}, u32[]{:S(2)}) copy-start(f32[512]{0:T(512)S(1)} %fusion.132) | copy-start | bytes 6148
  644.2 13.8 %copy-start.19 = (bf16[7,64,768]{1,0,2:T(8,128)(2,1)S(1)}, bf16[7,64,768]{1,0,2:T(8,128)(2,1)}, u32[]{:S(2)}) copy-start(bf16[7,64,768]{1,0,2:T(8,128)(2,1)} %copy.230) | copy-start | bytes 2064388
  675.4 209.3 %reduce-scatter.30.cloned.1.call-start = ((), (), s32[]{:S(2)}) async-start(), calls=%async_computation.26 | async-start | bytes 245760
  715.7 31.8 %copy-start.62 = (f32[768,64]{0,1:T(8,128)}, f32[768,64]{0,1:T(8,128)S(1)}, u32[]{:S(2)}) copy-start(f32[768,64]{0,1:T(8,128)S(1)} %fusion.89) | copy-start | bytes 589828
  730.9 16.6 %copy-start.33 = (f32[768,64]{0,1:T(8,128)S(1)}, f32[768,64]{0,1:T(8,128)}, u32[]{:S(2)}) copy-start(f32[768,64]{0,1:T(8,128)} %copy-done.32) | copy-start | bytes 589828
  730.9 16.6 %copy-start.97 = (f32[64]{0:T(128)S(1)}, f32[64]{0:T(128)}, u32[]{:S(2)}) copy-start(f32[64]{0:T(128)} %copy-done.96) | copy-start | bytes 772
  773.2 113.0 %reduce-scatter.32.cloned.1.call-start = ((), (), s32[]{:S(2)}) async-start(), calls=%async_computation.27 | async-start | bytes 245760
  775.2 112.7 %reduce-scatter.16.cloned.1.call-start = ((), (), s32[]{:S(2)}) async-start(), calls=%async_computation.19 | async-start | bytes 1474560 | tf_op jit(solution)/shard_map/reduce_scatter | solution.py:405
  778.5 109.4 %reduce-scatter.18.cloned.1.call-start = ((), (), s32[]{:S(2)}) async-start(), calls=%async_computation.20 | async-start | bytes 1474560 | tf_op jit(solution)/shard_map/reduce_scatter | solution.py:411
  802.0 112.8 %reduce-scatter.20.cloned.1.call-start = ((), (), s32[]{:S(2)}) async-start(), calls=%async_computation.21 | async-start | bytes 1474560 | tf_op jit(solution)/shard_map/reduce_scatter | solution.py:417
  804.0 141.7 %reduce-scatter.22.cloned.1.call-start = ((), (), s32[]{:S(2)}) async-start(), calls=%async_computation.22 | async-start | bytes 1474560 | tf_op jit(solution)/shard_map/reduce_scatter | solution.py:435
  807.7 224.5 %reduce-scatter.24.cloned.1.call-start = ((), (), s32[]{:S(2)}) async-start(), calls=%async_computation.23 | async-start | bytes 5898240 | tf_op jit(solution)/shard_map/reduce_scatter | solution.py:447
  814.2 306.0 %reduce-scatter.26.cloned.1.call-start = ((), (), s32[]{:S(2)}) async-start(), calls=%async_computation.24 | async-start | bytes 5898240 | tf_op jit(solution)/shard_map/reduce_scatter | solution.py:453
  834.1 15.8 %copy-start.84 = (f32[4,1,768]{2,1,0:T(1,128)S(1)}, f32[4,1,768]{2,1,0:T(1,128)}, u32[]{:S(2)}) copy-start(f32[4,1,768]{2,1,0:T(1,128)} %convert_element_type.515) | copy-start | bytes 36868
  834.1 15.8 %copy-start.101 = (f32[768]{0:T(1024)S(1)}, f32[768]{0:T(1024)}, u32[]{:S(2)}) copy-start(f32[768]{0:T(1024)} %convert_element_type.439) | copy-start | bytes 9220
  863.7 262.9 %all-to-all-start.1 = ((bf16[32,16,768]{2,1,0:T(8,128)(2,1)}), bf16[32,16,768]{2,1,0:T(8,128)(2,1)}, u32[]{:S(2)}, u32[]{:S(2)}) async-start(bf16[32,16,768]{2,1,0:T(8,128)(2,1)} %gather_fusion.2), calls=%async_computation.1 | async-start | bytes 1572864 | tf_op jit(solution)/shard_map/all_to_all | solution.py:371
  875.4 311.3 %all-reduce.30.cloned.1.call-start = ((), (), s32[]{:S(2)}) async-start(), calls=%async_computation.28 | async-start | bytes 210944 | tf_op jit(solution)/shard_map/psum | solution.py:461
  887.8 377.4 %all-reduce.32.cloned.1.call-start = ((), (), s32[]{:S(2)}) async-start(), calls=%async_computation.29 | async-start | bytes 7077888 | tf_op jit(solution)/shard_map/psum | solution.py:463
  1126.6 80.2 %all-to-all-start.3 = ((bf16[32,16,768]{2,1,0:T(8,128)(2,1)}), bf16[32,16,768]{2,1,0:T(8,128)(2,1)S(1)}, u32[]{:S(2)}, u32[]{:S(2)}) async-start(bf16[32,16,768]{2,1,0:T(8,128)(2,1)} %gather_fusion.6), calls=%async_computation.3 | async-start | bytes 1572864 | tf_op jit(solution)/shard_map/all_to_all | solution.py:372
  (99 other events, 371.9 us)
Sparse Core Ops, SparseCore 0:
  9.6 49.8 all-gather.12
  61.1 32.8 all-gather.14
  95.5 29.5 all-gather.10
  126.5 46.7 all-gather.16
  174.8 88.7 all-gather.18
  265.0 88.0 all-gather.20
  675.5 22.5 reduce-scatter.27
  773.4 22.5 reduce-scatter.29
  798.8 17.5 reduce-scatter.31
  818.7 29.8 reduce-scatter.15
  851.5 28.1 reduce-scatter.17
  882.0 32.8 reduce-scatter.19
  917.3 28.3 reduce-scatter.21
  947.9 84.1 reduce-scatter.23
  1034.4 85.7 reduce-scatter.25
  1127.3 59.4 all-reduce.29
  1190.6 74.5 all-reduce.31
where the time goes:
time: 1290 us; the launch traced here: 1280 us
  waiting for transfers between devices  347 us (27%)
  local copies, waits for them, and re-layouts  291 us (23%)
  matrix products  291 us (23%)
  other arithmetic  169 us (13%)
  blocking collectives  125 us (10%)
  starting transfers between devices  38.6 us (3%)
  between operations  17.7 us (1%)
    convert_element_type x7, local copies, waits for them, and re-layouts, to_half(): return array.astype(jnp.bfloat16)  96.6 us
    reduce_scatter x1, waiting for transfers between devices, local(): lax.psum_scatter(g_w_down.astype(jnp.bfloat16), 'shard', scatter_dimensio...  88.1 us
    reduce_scatter x1, waiting for transfers between devices, local(): lax.psum_scatter(g_w_up.astype(jnp.bfloat16), 'shard', scatter_dimension=...  86.5 us
    psum x1, waiting for transfers between devices, local(): lax.psum(grad_parts[2].astype(jnp.bfloat16), 'rep').astype(jnp.float32)  56.9 us
    psum x1, waiting for transfers between devices, local(): lax.psum(grad_parts[0].astype(jnp.bfloat16), 'rep').astype(jnp.float32)  53.9 us
    unnamed x2, blocking collectives  53.5 us
    dot_general x4, matrix products, mixing(): jnp.einsum('cna,icn->iac', lead_decay, previous_low, preferred_element_ty...  39.3 us
    all_gather x1, blocking collectives, local(): lax.all_gather(shift_taps, 'shard', axis=0, tiled=True)  37.2 us
  transfers between devices with their start and end apart: 21, of which 6 were waited for; matrix products, arithmetic and copies ran while one was open for 43% of the time, Pallas kernels for 0%

commit v1 on v0

v1 whole, which is shorter than its diff:
```python
import jax
import jax.numpy as jnp
from jax import lax
from jax.experimental import pallas as pl
from jax.experimental.pallas import tpu as pltpu
from jax.sharding import PartitionSpec as P

EPSILON = 1e-05
GELU_A = 0.7978845608028654
GELU_B = 0.044715


def to_float(array):
    return array.astype(jnp.float32)


def to_half(array):
    return array.astype(jnp.bfloat16)


def dot_nn(one, two, out=jnp.float32):
    return jnp.dot(one, two, preferred_element_type=jnp.float32).astype(out)


def dot_tn(one, two, out=jnp.float32):
    return lax.dot_general(
        one, two, (((0,), (0,)), ((), ())), preferred_element_type=jnp.float32
    ).astype(out)


def dot_nt(one, two, out=jnp.float32):
    return lax.dot_general(
        one, two, (((1,), (1,)), ((), ())), preferred_element_type=jnp.float32
    ).astype(out)


MESH = pl.DeviceIdType.MESH


class Place:
    def __init__(self, rep_count, shard_count):
        self.rep_count, self.shard_count = rep_count, shard_count
        self.rep, self.shard = lax.axis_index("rep"), lax.axis_index("shard")

    def by_rep(self, mask):
        return (lax.bitwise_xor(self.rep, mask), self.shard)

    def by_shard(self, mask):
        return (self.rep, lax.bitwise_xor(self.shard, mask))

    def bit(self, mask):
        return lax.bitwise_and(lax.div(self.rep, mask), 1)

    def partners(self):
        found, mask = [], 1
        while mask < self.rep_count:
            found.append(self.by_rep(mask))
            mask *= 2
        return found + [self.by_shard(k) for k in range(1, self.shard_count)]

    def meet(self):
        barrier = pltpu.get_barrier_semaphore()
        partners = self.partners()
        for device in partners:
            pl.semaphore_signal(barrier, inc=1, device_id=device, device_id_type=MESH)
        pl.semaphore_wait(barrier, len(partners))


def plane_masks(rep_count, order):
    masks, mask = [], 2
    while mask < rep_count:
        masks.append(mask)
        mask *= 2
    return masks if order == 0 else masks[::-1]


def offset_of(index, masks):
    total = 0
    for i, mask in enumerate(masks):
        if (index >> i) & 1:
            total |= mask
    return total


def remote(source, target, sems, index, device):
    send, receive = sems
    return pltpu.make_async_remote_copy(
        src_ref=source,
        dst_ref=target,
        send_sem=send.at[index],
        recv_sem=receive.at[index],
        device_id=device,
        device_id_type=MESH,
    )


AHEAD = 3


def gather_body(rep_count, shard_count, units, *refs):
    tensors = 1 + max(tensor for tensor, _ in units)
    locals_, pack = refs[:tensors], refs[tensors]
    outs, pack_out = refs[tensors + 1 : 2 * tensors + 1], refs[2 * tensors + 1]
    held, send, receive, pack_send, pack_receive, done = refs[2 * tensors + 2 :]
    place = Place(rep_count, shard_count)
    place.meet()
    me, shard = place.rep, place.shard
    others = shard_count - 1
    stages = len(plane_masks(rep_count, 0)) + 1
    width = others + stages
    keep = []

    small = []
    for k in range(1, shard_count):
        copy = remote(
            pack, pack_out.at[shard], (pack_send, pack_receive), k - 1, place.by_shard(k)
        )
        copy.start()
        small.append(copy)
    own = pltpu.make_async_copy(pack, pack_out.at[shard], done.at[tensors])
    own.start()
    for tensor in range(tensors):
        pltpu.make_async_copy(
            locals_[tensor], outs[tensor].at[shard], done.at[tensor]
        ).start()

    def across(unit):
        tensor, pick = units[unit]
        copies = []
        for k in range(1, shard_count):
            copies.append(
                remote(
                    pick(locals_[tensor].at[me]),
                    held.at[unit, 0, k - 1],
                    (send, receive),
                    unit * width + k - 1,
                    place.by_shard(k),
                )
            )
        return copies

    def doubling(unit, stage):
        masks = plane_masks(rep_count, unit % 2) + [1]
        count = 1 << stage
        return remote(
            held.at[unit, pl.ds(0, count)],
            held.at[unit, pl.ds(count, count)],
            (send, receive),
            unit * width + others + stage,
            place.by_rep(masks[stage]),
        )

    def write(unit, first, count):
        tensor, pick = units[unit]
        masks = plane_masks(rep_count, unit % 2) + [1]
        for m in range(first, first + count):
            piece = lax.bitwise_xor(me, offset_of(m, masks))
            for k in range(1, shard_count):
                pltpu.make_async_copy(
                    held.at[unit, m, k - 1],
                    pick(outs[tensor].at[lax.bitwise_xor(shard, k), piece]),
                    done.at[tensor],
                ).start()

    flights = {}
    total = len(units)
    for unit in range(min(AHEAD, total)):
        flights[unit, -1] = across(unit)
        for copy in flights[unit, -1]:
            copy.start()
    for step in range(total + stages):
        for stage in range(stages, -1, -1):
            unit = step - stage
            if not 0 <= unit < total:
                continue
            if stage == 0:
                for copy in flights[unit, -1]:
                    copy.wait_recv()
                if unit + AHEAD < total:
                    flights[unit + AHEAD, -1] = across(unit + AHEAD)
                    for copy in flights[unit + AHEAD, -1]:
                        copy.start()
            else:
                flights[unit, stage - 1].wait_recv()
            if stage < stages:
                flights[unit, stage] = doubling(unit, stage)
                flights[unit, stage].start()
            if stage == 0:
                write(unit, 0, 1)
            else:
                write(unit, 1 << (stage - 1), 1 << (stage - 1))
    for copy in small:
        copy.wait()
    own.wait()
    for unit in range(total):
        for copy in flights[unit, -1]:
            copy.wait_send()
        for stage in range(stages):
            flights[unit, stage].wait_send()
    for tensor in range(tensors):
        pltpu.make_async_copy(outs[tensor], outs[tensor], done.at[tensor]).wait()


def gather_weights(squares, up, down, pack, rep_count, shard_count):
    rows, width = squares[0].shape
    piece = rows // rep_count
    parts = up.shape[1] // width
    locals_ = [w.reshape(rep_count, piece, width) for w in squares]
    locals_.append(up.reshape(rep_count, piece, up.shape[1]))
    locals_.append(down.reshape(rep_count, parts, piece, width))
    units = [(i, lambda ref: ref) for i in range(len(squares))]
    for q in range(parts):
        units.append((len(squares), lambda ref, q=q: ref.at[:, pl.ds(q * width, width)]))
    for q in range(parts):
        units.append((len(squares) + 1, lambda ref, q=q: ref.at[q]))
    anywhere = pl.BlockSpec(memory_space=pl.ANY)
    copies = len(units) * (shard_count + len(plane_masks(rep_count, 0)))
    outs = [jax.ShapeDtypeStruct((shard_count,) + w.shape, w.dtype) for w in locals_ + [pack]]
    found = pl.pallas_call(
        lambda *refs: gather_body(rep_count, shard_count, units, *refs),
        in_specs=[anywhere] * (len(locals_) + 1),
        out_specs=[anywhere] * len(outs),
        out_shape=outs,
        scratch_shapes=[
            pltpu.VMEM((len(units), rep_count, shard_count - 1, piece, width), jnp.bfloat16),
            pltpu.SemaphoreType.DMA((copies,)),
            pltpu.SemaphoreType.DMA((copies,)),
            pltpu.SemaphoreType.DMA((shard_count - 1,)),
            pltpu.SemaphoreType.DMA((shard_count - 1,)),
            pltpu.SemaphoreType.DMA((len(outs),)),
        ],
        compiler_params=pltpu.CompilerParams(
            collective_id=0, has_side_effects=True, vmem_limit_bytes=40 * 1024 * 1024
        ),
        cost_estimate=pl.CostEstimate(flops=0, bytes_accessed=200_000_000, transcendentals=0),
        name="gather_weights",
    )(*locals_, pack)
    whole = [w.reshape(shard_count * rows, width) for w in found[: len(squares)]]
    whole.append(found[-3].reshape(shard_count * rows, up.shape[1]))
    whole.append(found[-2].reshape(shard_count * down.shape[0], width))
    return whole, found[-1]


def add_into(target, other, count):
    def step(i, unused):
        target[i] = to_half(to_float(target[i]) + to_float(other[i]))
        return unused

    lax.fori_loop(0, count, step, 0)


class Reduction:
    def __init__(self, place, order, source, half, came, back, sems, base, write):
        self.place, self.source, self.half, self.came, self.back = place, source, half, came, back
        self.sems, self.base, self.write = sems, base, write
        self.masks = plane_masks(place.rep_count, order)
        self.flight = None
        self.kept = None
        self.sent = []
        self.rest = place.rep_count // 2

    def start(self):
        place = self.place
        core = place.bit(1)
        self.kept = pltpu.make_async_copy(
            self.source.at[:, :, core], self.half, self.sems[2].at[self.base]
        )
        self.kept.start()
        self.fly(self.source.at[:, :, 1 - core], self.came[0], 0, place.by_rep(1))

    def fly(self, source, target, index, device):
        copy = remote(source, target, self.sems[:2], self.base + index, device)
        copy.start()
        self.sent.append(copy)
        self.flight = copy

    def steps(self):
        place = self.place
        shards = place.shard_count
        count = len(self.masks)
        todo = []

        def after_core():
            self.kept.wait()
            self.flight.wait_recv()
            half, came = self.half, self.came[0]

            def step(i, unused):
                for j in range(self.rest):
                    half[i, j] = to_half(to_float(half[i, j]) + to_float(came[i, j]))
                return unused

            lax.fori_loop(0, shards, step, 0)
            leave(0)

        def index_of(chosen):
            free = [mask for mask in plane_masks(place.rep_count, 0) if mask not in chosen]
            spots = []
            for bits in range(1 << len(free)):
                spot = 0
                for i, mask in enumerate(free):
                    if (bits >> i) & 1:
                        spot += mask // 2
                spots.append(spot)
            return spots

        def own_spot(chosen):
            total = 0
            for mask in chosen:
                total = total + place.bit(mask) * (mask // 2)
            return total

        def leave(stage):
            mask = self.masks[stage]
            chosen = self.masks[: stage + 1]
            base = own_spot(self.masks[:stage]) + (1 - place.bit(mask)) * (mask // 2)
            self.group = []
            for n, spot in enumerate(index_of(chosen)):
                copy = remote(
                    self.half.at[:, base + spot],
                    self.came[1 + stage].at[n],
                    self.sems[:2],
                    self.base + 1 + stage * self.rest + n,
                    place.by_rep(mask),
                )
                copy.start()
                self.sent.append(copy)
                self.group.append(copy)

        def after_plane(stage):
            mask = self.masks[stage]
            chosen = self.masks[: stage + 1]
            base = own_spot(chosen)
            spots = index_of(chosen)
            for copy in self.group:
                copy.wait_recv()
            half, came = self.half, self.came[1 + stage]

            def step(i, unused):
                for n, spot in enumerate(spots):
                    at = base + spot
                    half[i, at] = to_half(to_float(half[i, at]) + to_float(came[n, i]))
                return unused

            lax.fori_loop(0, shards, step, 0)
            if stage + 1 < count:
                leave(stage + 1)
                return
            self.group = []
            for k in range(1, shards):
                copy = remote(
                    self.half.at[lax.bitwise_xor(place.shard, k), own_spot(self.masks)],
                    self.came[1 + count].at[k - 1],
                    self.sems[:2],
                    self.base + 1 + count * self.rest + k - 1,
                    place.by_shard(k),
                )
                copy.start()
                self.sent.append(copy)
                self.group.append(copy)

        def after_shard():
            total = to_float(self.half[place.shard, own_spot(self.masks)])
            for copy in self.group:
                copy.wait_recv()
            for k in range(1, shards):
                total = total + to_float(self.came[1 + count][k - 1])
            self.back[0] = to_half(total)
            double(0)
            self.write(place.rep, self.back[0])

        def double(stage):
            masks = self.masks + [1]
            size = 1 << stage
            self.fly(
                self.back.at[pl.ds(0, size)],
                self.back.at[pl.ds(size, size)],
                1 + count * self.rest + shards - 1 + stage,
                place.by_rep(masks[stage]),
            )

        def after_double(stage):
            masks = self.masks + [1]
            size = 1 << stage
            self.flight.wait_recv()
            if stage < count:
                double(stage + 1)
            for m in range(size, 2 * size):
                self.write(lax.bitwise_xor(place.rep, offset_of(m, masks)), self.back[m])

        todo.append(after_core)
        for stage in range(count):
            todo.append(lambda stage=stage: after_plane(stage))
        todo.append(after_shard)
        for stage in range(count + 1):
            todo.append(lambda stage=stage: after_double(stage))
        return todo

    def finish(self):
        for copy in self.sent:
            copy.wait_send()


def flights_of(rep_count, shard_count):
    planes = len(plane_masks(rep_count, 0))
    return 1 + planes * (rep_count // 2) + shard_count - 1 + planes + 1


REDUCE_AHEAD = 4


def reduce_body(rep_count, shard_count, units, tensors, *refs):
    planes = len(plane_masks(rep_count, 0))
    sources, outs = refs[:tensors], refs[tensors : 2 * tensors]
    rest = refs[2 * tensors :]
    per_kind = planes + 4
    kinds = [rest[i * per_kind : (i + 1) * per_kind] for i in range(2)]
    send, receive, kept = rest[2 * per_kind :]
    place = Place(rep_count, shard_count)
    place.meet()
    count = flights_of(rep_count, shard_count)
    works = []
    for index, (tensor, pick, writer, kind, slot) in enumerate(units):
        bufs = kinds[kind]
        came = [buf.at[slot] for buf in bufs[1 : 1 + planes + 2]]
        works.append(
            Reduction(
                place,
                index % 2,
                pick(sources[tensor]),
                bufs[0].at[slot],
                came,
                bufs[-1].at[slot],
                (send, receive, kept),
                index * count,
                lambda piece, value, tensor=tensor, writer=writer: writer(
                    outs[tensor], piece, to_float(value)
                ),
            )
        )
    todo = [work.steps() for work in works]
    for work in works[:REDUCE_AHEAD]:
        work.start()
    length = len(todo[0])
    for step in range(len(works) + length - 1):
        for position in range(length - 1, -1, -1):
            index = step - position
            if 0 <= index < len(works):
                todo[index][position]()
                if position == 0 and index + REDUCE_AHEAD < len(works):
                    works[index + REDUCE_AHEAD].start()
    for work in works:
        work.finish()


def reduce_grads(down, up, squares, pack, rep_count, shard_count):
    width = squares[0].shape[1]
    piece = squares[0].shape[0] // (shard_count * rep_count)
    parts = up.shape[1] // width
    lead = (shard_count, rep_count // 2, 2)
    tensors = [down.reshape(lead + (parts, piece, width)), up.reshape(lead + (piece, up.shape[1]))]
    tensors += [g.reshape(lead + (piece, width)) for g in squares]
    pack_rows, pack_width = pack.shape[1] // rep_count, pack.shape[2]
    tensors.append(pack.reshape(lead + (pack_rows, pack_width)))
    outs = [jax.ShapeDtypeStruct((rep_count, parts, piece, width), jnp.float32)]
    outs.append(jax.ShapeDtypeStruct((rep_count, piece, up.shape[1]), jnp.float32))
    outs += [jax.ShapeDtypeStruct((rep_count, piece, width), jnp.float32)] * len(squares)
    outs.append(jax.ShapeDtypeStruct((rep_count, pack_rows, pack_width), jnp.float32))

    def whole_writer(out, at, value):
        out[at] = value

    units = []
    for q in range(parts):

        def part_writer(out, at, value, q=q):
            out[at, q] = value

        units.append((0, lambda ref, q=q: ref.at[:, :, :, q], part_writer, 0, len(units)))
    for q in range(parts):

        def column_writer(out, at, value, q=q):
            out[at, :, q * width : (q + 1) * width] = value

        units.append(
            (
                1,
                lambda ref, q=q: ref.at[:, :, :, :, pl.ds(q * width, width)],
                column_writer,
                0,
                len(units),
            )
        )
    for i in range(len(squares)):
        units.append((2 + i, lambda ref: ref, whole_writer, 0, len(units)))
    plain = len(units)
    units.append((2 + len(squares), lambda ref: ref, whole_writer, 1, 0))
    half = rep_count // 2
    planes = len(plane_masks(rep_count, 0))

    def buffers(count, rows, columns):
        shapes = [(shard_count, half), (shard_count, half)]
        size = half
        for _ in range(planes):
            size //= 2
            shapes.append((size, shard_count))
        shapes += [(shard_count - 1,), (rep_count,)]
        return [pltpu.VMEM((count,) + shape + (rows, columns), jnp.bfloat16) for shape in shapes]

    flights = len(units) * flights_of(rep_count, shard_count)
    anywhere = pl.BlockSpec(memory_space=pl.ANY)
    found = pl.pallas_call(
        lambda *refs: reduce_body(rep_count, shard_count, units, len(tensors), *refs),
        in_specs=[anywhere] * len(tensors),
        out_specs=[pl.BlockSpec(memory_space=pltpu.VMEM)] * len(outs),
        out_shape=outs,
        scratch_shapes=buffers(plain, piece, width)
        + buffers(1, pack_rows, pack_width)
        + [pltpu.SemaphoreType.DMA((flights,))] * 3,
        compiler_params=pltpu.CompilerParams(
            collective_id=1, has_side_effects=True, vmem_limit_bytes=60 * 1024 * 1024
        ),
        cost_estimate=pl.CostEstimate(flops=0, bytes_accessed=200_000_000, transcendentals=0),
        name="reduce_grads",
    )(*tensors)
    rows = rep_count * piece
    return (
        found[0].reshape(rows * parts, width),
        found[1].reshape(rows, up.shape[1]),
        [g.reshape(rows, width) for g in found[2:-1]],
        found[-1].reshape(pack.shape[1], pack_width),
    )


def ssm_kernel_body(coef_ref, rate_ref, out_ref):
    states, lanes = coef_ref.shape
    taps = 64
    count = out_ref.shape[0] // taps
    lag = to_float(lax.broadcasted_iota(jnp.int32, (taps, lanes), 0))

    def step(n, totals):
        rate = rate_ref[pl.ds(n, 1), :]
        factor = coef_ref[pl.ds(n, 1), :]
        block = jnp.exp(-rate * taps)
        decay = jnp.exp(-rate * lag)
        new = []
        for q in range(count):
            new.append(totals[q] + factor * decay)
            factor = factor * block
        return tuple(new)

    zero = jnp.zeros((taps, lanes), jnp.float32)
    totals = lax.fori_loop(0, states, step, (zero,) * count)
    for q in range(count):
        out_ref[q * taps : (q + 1) * taps, :] = totals[q]


def ssm_kernel(coef, rate, length):
    states, channels = coef.shape
    return pl.pallas_call(
        ssm_kernel_body,
        grid=(channels // 128,),
        in_specs=[pl.BlockSpec((states, 128), lambda i: (0, i))] * 2,
        out_specs=pl.BlockSpec((length, 128), lambda i: (0, i)),
        out_shape=jax.ShapeDtypeStruct((length, channels), jnp.float32),
        cost_estimate=pl.CostEstimate(
            flops=2 * states * length * channels,
            bytes_accessed=4 * channels * (2 * states + length),
            transcendentals=states * 64 * channels,
        ),
        name="ssm_kernel",
    )(coef, rate)


def ssm_grad_body(coef_ref, rate_ref, grad_ref, coef_out, rate_out):
    states, lanes = coef_ref.shape
    taps = 64
    count = grad_ref.shape[0] // taps
    lag = to_float(lax.broadcasted_iota(jnp.int32, (taps, lanes), 0))

    def step(n, unused):
        rate = rate_ref[pl.ds(n, 1), :]
        block = jnp.exp(-rate * taps)
        decay = jnp.exp(-rate * lag)
        plain = jnp.zeros((taps, lanes), jnp.float32)
        ramp = jnp.zeros((taps, lanes), jnp.float32)
        for q in range(count - 1, -1, -1):
            grad = grad_ref[q * taps : (q + 1) * taps, :]
            plain = plain * block + grad
            ramp = ramp * block + grad * float(q * taps)
        ramp = ramp + plain * lag
        coef_out[pl.ds(n, 1), :] = jnp.sum(plain * decay, axis=0, keepdims=True)
        rate_out[pl.ds(n, 1), :] = -coef_ref[pl.ds(n, 1), :] * jnp.sum(
            ramp * decay, axis=0, keepdims=True
        )
        return unused

    lax.fori_loop(0, states, step, 0)


def ssm_grad(coef, rate, grad):
    states, channels = coef.shape
    length = grad.shape[0]
    return pl.pallas_call(
        ssm_grad_body,
        grid=(channels // 128,),
        in_specs=[pl.BlockSpec((states, 128), lambda i: (0, i))] * 2
        + [pl.BlockSpec((length, 128), lambda i: (0, i))],
        out_specs=[pl.BlockSpec((states, 128), lambda i: (0, i))] * 2,
        out_shape=[jax.ShapeDtypeStruct((states, channels), jnp.float32)] * 2,
        cost_estimate=pl.CostEstimate(
            flops=6 * states * length * channels,
            bytes_accessed=4 * channels * (4 * states + length),
            transcendentals=states * 64 * channels,
        ),
        name="ssm_grad",
    )(coef, rate, grad)


def wave_tables(rows, period, length):
    freq = lax.broadcasted_iota(jnp.int32, (rows, length), 0)
    time = lax.broadcasted_iota(jnp.int32, (rows, length), 1)
    phase = ((2 * freq + 1) * time) % (2 * period)
    angle = to_float(phase) * (jnp.pi / period)
    return jnp.cos(angle), -jnp.sin(angle)


class Waves:
    def __init__(self, length, short, count):
        self.length, self.short, self.count = length, short, count
        self.half = length + short * count
        top = wave_tables(length, 2 * length, length)
        low = wave_tables(short, 2 * short, short)
        self.long_rows = top
        self.short_rows = low
        parts = []
        for a, b in zip(top, low):
            rows = [jnp.pad(a, ((0, 0), (0, short * count)))]
            for i in range(count):
                rows.append(
                    jnp.pad(b, ((0, 0), (length + i * short, (count - 1 - i) * short)))
                )
            parts.append(jnp.concatenate(rows))
        full = jnp.concatenate(parts)
        self.exact = lax.optimization_barrier(full)
        self.low = lax.optimization_barrier(to_half(full))
        self.gain = jnp.concatenate(
            [
                jnp.full((length, 1), 1.0 / length, jnp.float32),
                jnp.full((short * count, 1), 1.0 / short, jnp.float32),
            ]
        )

    def forward(self, rows):
        return dot_nn(self.low, to_half(rows))

    def back(self, real, imag):
        return dot_tn(self.low, jnp.concatenate([to_half(real), to_half(imag)]))

    def filter(self, taps):
        lags, channels = taps.shape
        first = jnp.pad(taps, ((0, self.length - lags), (0, 0)))
        rows = jnp.concatenate([first] + [taps[: self.short]] * self.count)
        wave = jnp.dot(self.exact, rows, precision=lax.Precision.HIGH)
        return wave[: self.half] * self.gain, wave[self.half :] * self.gain

    def lags(self, real, imag, count):
        real, imag = real * self.gain, imag * self.gain
        channels = real.shape[1]
        length, short = self.length, self.short
        top = jnp.concatenate([real[:length], imag[:length]])
        low = jnp.concatenate(
            [
                jnp.sum(part[length:].reshape(self.count, short, channels), axis=0)
                for part in (real, imag)
            ]
        )
        half, width = self.half, min(count, length)
        table = jnp.concatenate([self.low[:length, :width], self.low[half : half + length, :width]])
        small = jnp.concatenate(
            [
                self.low[length : length + short, length : length + short],
                self.low[half + length : half + length + short, length : length + short],
            ]
        )
        total = dot_tn(table, to_half(top))
        head = total[:short] + dot_tn(small, to_half(low))
        return jnp.concatenate([head, total[short:]]) if count > short else head


def row_stats(values):
    average = jnp.mean(values, axis=-1, keepdims=True)
    centred = values - average
    spread = jnp.mean(centred * centred, axis=-1, keepdims=True)
    scale = lax.rsqrt(spread + EPSILON)
    return centred * scale, scale


def norm_back(error, hat, scale, gain):
    pulled = error * gain
    return scale * (
        pulled
        - jnp.mean(pulled, axis=-1, keepdims=True)
        - hat * jnp.mean(pulled * hat, axis=-1, keepdims=True)
    )


def column_sum(array):
    return jnp.sum(to_float(array), axis=0)


def local(
    tokens,
    ln1_scale,
    ln1_shift,
    w_query,
    b_query,
    w_key,
    b_key,
    w_value,
    b_value,
    shift_taps,
    ssm_coef,
    ssm_rate,
    ssm_skip,
    w_out,
    b_out,
    ln2_scale,
    ln2_shift,
    w_up,
    b_up,
    w_down,
    b_down,
    cotangent,
    piece_slot,
    lengths,
):
    rep_count, shard_count = lax.axis_size("rep"), lax.axis_size("shard")
    slots = rep_count * shard_count
    me = lax.axis_index("rep") * shard_count + lax.axis_index("shard")
    rows, width = tokens.shape
    piece_rows = rows // slots
    taps = shift_taps.shape[1]
    blocks = rows // taps
    owned = ssm_skip.shape[0]
    shorts = lengths.shape[1] - 1
    long_blocks = blocks - shorts
    per_block = slots // blocks

    ids = jnp.arange(slots, dtype=jnp.int32)
    table = piece_slot.reshape(slots, slots)
    target = table // slots
    arrival = jnp.sum(jnp.where(target == me, table % slots, 0), axis=1)
    own_target = jnp.sum(jnp.where(ids[:, None] == me, target, 0), axis=0)
    sizes = lengths[0] // taps
    starts = jnp.cumsum(sizes) - sizes
    first = jnp.sum(jnp.where(sizes == long_blocks, starts, 0))
    block = arrival // per_block
    moved = jnp.where(
        block < first,
        block + long_blocks,
        jnp.where(block < first + long_blocks, block - first, block),
    )
    arrival = moved * per_block + arrival % per_block
    sending = jnp.sum(jnp.where(own_target[None, :] == ids[:, None], ids[None, :], 0), axis=1)
    unpacking = jnp.sum(jnp.where(arrival[None, :] == ids[:, None], ids[None, :], 0), axis=1)

    def deal(array):
        pieces = array.reshape(slots, piece_rows, width)[sending]
        came = lax.all_to_all(pieces, ("rep", "shard"), split_axis=0, concat_axis=0, tiled=True)
        return came[unpacking].reshape(rows, width)

    def give_back(array):
        pieces = array.reshape(slots, piece_rows, width)[arrival]
        came = lax.all_to_all(pieces, ("rep", "shard"), split_axis=0, concat_axis=0, tiled=True)
        return came[own_target].reshape(rows, width)

    balanced = to_float(deal(tokens))

    pack = jnp.concatenate(
        [shift_taps.T, ssm_coef.T, ssm_rate.T]
        + [
            vector.reshape(1, owned)
            for vector in (
                ln1_scale,
                ln1_shift,
                b_query,
                b_key,
                b_value,
                ssm_skip,
                b_out,
                ln2_scale,
                ln2_shift,
                b_down,
            )
        ]
        + [b_up.reshape(-1, owned)]
    )
    (weight_q, weight_k, weight_v, weight_o, weight_up, weight_down), packs = gather_weights(
        [w_query, w_key, w_value, w_out], w_up, w_down, pack, rep_count, shard_count
    )
    tops = 3 * taps + 10
    up_bias = to_float(packs[:, tops:].reshape(1, -1))
    small = to_float(jnp.swapaxes(packs[:, :tops], 0, 1).reshape(tops, width))
    tap_rows, coef_rows, rate_rows = small[:taps], small[taps : 2 * taps], small[2 * taps : 3 * taps]
    (
        gain_one,
        bias_one,
        query_bias,
        key_bias,
        value_bias,
        skip,
        out_bias,
        gain_two,
        bias_two,
        down_bias,
    ) = [small[3 * taps + i][None] for i in range(10)]

    waves = Waves(long_blocks * taps, taps, shorts)
    half = waves.half
    kernel = ssm_kernel(coef_rows, rate_rows, long_blocks * taps)
    ker_re, ker_im = waves.filter(kernel)
    tap_re, tap_im = waves.filter(tap_rows)

    hat_one, scale_one = row_stats(balanced)
    normed = to_half(hat_one * gain_one + bias_one)
    queries = dot_nn(normed, weight_q) + query_bias
    keys = to_half(dot_nn(normed, weight_k) + key_bias)
    values = dot_nn(normed, weight_v) + value_bias
    wave_k = waves.forward(keys)
    key_re, key_im = wave_k[:half], wave_k[half:]
    shifted = waves.back(key_re * tap_re - key_im * tap_im, key_re * tap_im + key_im * tap_re)
    inputs = shifted * values
    wave_u = waves.forward(inputs)
    in_re, in_im = wave_u[:half], wave_u[half:]
    mixed = (
        waves.back(in_re * ker_re - in_im * ker_im, in_re * ker_im + in_im * ker_re)
        + skip * inputs
    )
    gated = to_half(queries * mixed)
    middle = balanced + (dot_nn(gated, weight_o) + out_bias)
    hat_two, scale_two = row_stats(middle)
    normed_two = to_half(hat_two * gain_two + bias_two)

    hidden = dot_nn(normed_two, weight_up) + up_bias
    bent = jnp.tanh(GELU_A * (hidden + GELU_B * hidden * hidden * hidden))
    active = to_half(0.5 * hidden * (1.0 + bent))
    slope = 0.5 * (1.0 + bent) + 0.5 * hidden * (1.0 - bent * bent) * GELU_A * (
        1.0 + 3.0 * GELU_B * hidden * hidden
    )
    branch = dot_nn(active, weight_down)
    result = middle + (branch + down_bias)
    block_output = give_back(to_half(result))

    grad_low = deal(cotangent)
    grad_out = to_float(grad_low)
    part_down = dot_tn(active, grad_low, jnp.bfloat16)
    g_b_down = column_sum(grad_low)
    grad_hidden = to_half(dot_nt(grad_low, weight_down) * slope)
    part_up = dot_tn(normed_two, grad_hidden, jnp.bfloat16)
    g_b_up = column_sum(grad_hidden)
    error = dot_nt(grad_hidden, weight_up)
    g_ln2_scale = jnp.sum(error * hat_two, axis=0)
    g_ln2_shift = jnp.sum(error, axis=0)
    grad_middle = grad_out + norm_back(error, hat_two, scale_two, gain_two)
    grad_branch = to_half(grad_middle)
    part_out = dot_tn(gated, grad_branch, jnp.bfloat16)
    g_b_out = column_sum(grad_branch)
    grad_gated = dot_nt(grad_branch, weight_o)
    grad_query = to_half(grad_gated * mixed)
    part_query = dot_tn(normed, grad_query, jnp.bfloat16)
    grad_mixed = grad_gated * queries
    wave_g = waves.forward(grad_mixed)
    g_re, g_im = wave_g[:half], wave_g[half:]
    grad_inputs = (
        waves.back(g_re * ker_re + g_im * ker_im, g_im * ker_re - g_re * ker_im)
        + skip * grad_mixed
    )
    g_skip = jnp.sum(grad_mixed * inputs, axis=0)
    grad_kernel = waves.lags(
        g_re * in_re + g_im * in_im, g_im * in_re - g_re * in_im, long_blocks * taps
    )
    g_coef, g_rate = ssm_grad(coef_rows, rate_rows, grad_kernel)
    grad_shifted = grad_inputs * values
    grad_value = to_half(grad_inputs * shifted)
    part_value = dot_tn(normed, grad_value, jnp.bfloat16)
    wave_s = waves.forward(grad_shifted)
    s_re, s_im = wave_s[:half], wave_s[half:]
    grad_key = to_half(waves.back(s_re * tap_re + s_im * tap_im, s_im * tap_re - s_re * tap_im))
    g_taps = waves.lags(s_re * key_re + s_im * key_im, s_im * key_re - s_re * key_im, taps)
    part_key = dot_tn(normed, grad_key, jnp.bfloat16)
    grad_normed = (
        dot_nt(grad_query, weight_q) + dot_nt(grad_key, weight_k) + dot_nt(grad_value, weight_v)
    )
    g_ln1_scale = jnp.sum(grad_normed * hat_one, axis=0)
    g_ln1_shift = jnp.sum(grad_normed, axis=0)
    grad_input = grad_middle + norm_back(grad_normed, hat_one, scale_one, gain_one)
    grad_tokens = give_back(to_half(grad_input))

    vectors = [
        g_ln1_scale,
        g_ln1_shift,
        column_sum(grad_query),
        column_sum(grad_key),
        column_sum(grad_value),
        g_skip,
        g_b_out,
        g_ln2_scale,
        g_ln2_shift,
        g_b_down,
    ]
    wide = jnp.concatenate([g_taps, g_coef, g_rate] + [v[None] for v in vectors])
    wide = jnp.swapaxes(wide.reshape(tops, shard_count, owned), 0, 1)
    wide = jnp.concatenate([wide, g_b_up.reshape(shard_count, -1, owned)], axis=1)
    wide = to_half(jnp.pad(wide, ((0, 0), (0, -wide.shape[1] % rep_count), (0, 0))))
    ups = b_up.shape[0] // owned
    grad_w_down, grad_w_up, squares, mine = reduce_grads(
        part_down,
        part_up,
        [part_out, part_query, part_value, part_key],
        wide,
        rep_count,
        shard_count,
    )
    grad_w_out, grad_w_query, grad_w_value, grad_w_key = squares
    vec = [mine[3 * taps + i] for i in range(10)]
    return (
        block_output,
        grad_tokens,
        vec[0],
        vec[1],
        grad_w_query,
        vec[2],
        grad_w_key,
        vec[3],
        grad_w_value,
        vec[4],
        mine[:taps].T,
        mine[taps : 2 * taps].T,
        mine[2 * taps : 3 * taps].T,
        vec[5],
        grad_w_out,
        vec[6],
        vec[7],
        vec[8],
        grad_w_up,
        mine[tops : tops + ups].reshape(-1),
        grad_w_down,
        vec[9],
    )


def solution(mesh):
    both = P(("rep", "shard"), None)
    row, mat = P("shard"), P("shard", None)
    in_specs = (
        (both, row, row, mat, row, mat, row, mat, row, mat, mat, mat, row)
        + (mat, row, row, row, mat, row, mat, row, both, P(), both)
    )
    out_specs = (
        (both, both, row, row, mat, row, mat, row, mat, row, mat, mat, mat, row)
        + (mat, row, row, row, mat, row, mat, row)
    )
    return jax.shard_map(local, mesh=mesh, in_specs=in_specs, out_specs=out_specs, check_vma=False)
```

time: 1290 us -> 525 us (0.41)
  waiting for transfers between devices: 347 us -> 0.01 us
  Pallas kernels: 0 us -> 281 us
  local copies, waits for them, and re-layouts: 291 us -> 81.8 us
  matrix products: 291 us -> 97.5 us
  other arithmetic: 169 us -> 29.8 us
  blocking collectives: 125 us -> 0 us
  between operations: 17.7 us -> 3.03 us
  starting transfers between devices: 38.6 us -> 24.6 us
    pallas_call x0 -> x4, Pallas kernels: none -> 281 us  [the longest x1 139 us: reduce_grads(): pl.pallas_call(lambda *refs: reduce_body(rep_count, shard_count, units, l...]
    reduce_scatter x6 -> x0, waiting for transfers between devices: 232 us -> none  [the longest x1 88.1 us: local(): lax.psum_scatter(g_w_down.astype(jnp.bfloat16), 'shard', scatter_dimensio...]
    dot_general x40 -> x31, matrix products: 279 us -> 97.5 us  [the longest x14 35.6 us: dot_tn(): lax.dot_general(one, two, (((0,), (0,)), ((), ())), preferred_element_typ...]
    psum x2 -> x0, waiting for transfers between devices: 111 us -> none  [the longest x1 56.9 us: local(): lax.psum(grad_parts[2].astype(jnp.bfloat16), 'rep').astype(jnp.float32)]
    convert_element_type x7 -> x1, local copies, waits for them, and re-layouts: 96.6 us -> 0.68 us  [to_float(): return array.astype(jnp.float32)]
    all_gather x4 -> x0, blocking collectives: 71.8 us -> none  [the longest x1 37.2 us: local(): lax.all_gather(shift_taps, 'shard', axis=0, tiled=True)]
    dot_general x10 -> x0, local copies, waits for them, and re-layouts: 57.8 us -> none  [the longest x3 26.3 us: mixing(): jnp.einsum('cna,icn->iac', lead_decay, previous_low, preferred_element_ty...]
    unnamed x2 -> x0, blocking collectives: 53.5 us -> none
  transfers between devices with their start and end apart: 21 -> 4, of which waited for: 6 -> 0; matrix products, arithmetic and copies ran while one was open for 43% -> 24% of each run, Pallas kernels for 0% -> 54%
where the time goes in v1:
time: 525 us; the launch traced here: 518 us
  Pallas kernels  281 us (54%)
  matrix products  97.5 us (19%)
  local copies, waits for them, and re-layouts  81.8 us (16%)
  other arithmetic  29.8 us (6%)
  starting transfers between devices  24.6 us (5%)
    pallas_call x1, Pallas kernels, reduce_grads(): pl.pallas_call(lambda *refs: reduce_body(rep_count, shard_count, units, l...  139 us
    pallas_call x1, Pallas kernels, gather_weights(): pl.pallas_call(lambda *refs: gather_body(rep_count, shard_count, units, *...  103 us
    unnamed x295, local copies, waits for them, and re-layouts  36.2 us
    dot_general x14, matrix products, dot_tn(): lax.dot_general(one, two, (((0,), (0,)), ((), ())), preferred_element_typ...  35.6 us
    dot_general x9, matrix products, dot_nn(): return jnp.dot(one, two, preferred_element_type=jnp.float32).astype(out)  26.6 us
    dot_general x6, matrix products, dot_nt(): lax.dot_general(one, two, (((1,), (1,)), ((), ())), preferred_element_typ...  24.9 us
    pallas_call x1, Pallas kernels, ssm_grad(): pl.pallas_call(ssm_grad_body, grid=(channels // 128,), in_specs=[pl.Block...  24.2 us
    pallas_call x1, Pallas kernels, ssm_kernel(): pl.pallas_call(ssm_kernel_body, grid=(channels // 128,), in_specs=[pl.Blo...  14.7 us
  transfers between devices with their start and end apart: 4, of which 0 were waited for; matrix products, arithmetic and copies ran while one was open for 24% of the time, Pallas kernels for 54%

profile of v1, /device:TPU:1, one launch (start us, length us, event | category | flops | bytes accessed | tf_op | source)
XLA Modules:
  0.0 517.8 jit_solution(9486474492757999052)
XLA Ops:
  5.8 1.5 gather_fusion
  7.3 7.1 %all-to-all-start = ((bf16[32,16,768]{2,1,0:T(8,128)(2,1)}), bf16[32,16,768]{2,1,0:T(8,128)(2,1)}, u32[]{:S(2)}, u32[]{:S(2)}) async-start(bf16[32,16,768]{2,1,0:T(8,128)(2,1)} %gather_fusion), calls=%async_computation | async-start | bytes 1572864 | tf_op jit(solution)/shard_map/all_to_all | solution.py:770
  15.1 2.1 sine_negate_fusion
  19.9 3.1 concatenate.88.refs_6_
  27.8 103.5 %gather_weights.1 = (bf16[4,8,24,768]{3,2,1,0:T(8,128)(2,1)S(1)}, bf16[4,8,24,768]{3,2,1,0:T(8,128)(2,1)S(1)}, bf16[4,8,24,768]{3,2,1,0:T(8,128)(2,1)S(1)}, bf16...) custom-call(bf16[8,24,768]{2,1,0:T(8,128)(2,1)S(1)} %bitcast.188, ...), custom_call_target="tpu_custom_call" | custom-call | bytes 200000000 | tf_op jit(solution)/shard_map/gather_weights/pallas_call | solution.py:219
  132.3 2.1 copy-done.11
  140.6 14.7 %ssm_kernel.1 = f32[320,768]{1,0:T(8,128)} custom-call(f32[64,768]{1,0:T(8,128)} %slice.213.coef_ref, f32[64,768]{1,0:T(8,128)} %slice.215.rate_ref), custom_call_target="tpu_custom_call" | custom-call | flops 31457280 | bytes 1376256 | tf_op jit(solution)/shard_map/ssm_kernel/pallas_call | solution.py:560
  159.3 1.5 gather_fusion.4
  163.6 6.0 %fusion.9 = f32[1024,768]{1,0:T(8,128)} fusion(f32[1024,512]{1,0:T(8,128)} %copy-done.35, f32[64,768]{1,0:T(8,128)S(1)} %slice.206), kind=kOutput, calls=%fused_computation.27 | convolution fusion | flops 2417885184 | bytes 5439488 | tf_op jit(solution)/shard_map/dot_general | solution.py:664
  169.6 4.3 fusion.19
  174.0 5.4 %all-to-all-start.2 = ((bf16[32,16,768]{2,1,0:T(8,128)(2,1)}), bf16[32,16,768]{2,1,0:T(8,128)(2,1)}, u32[]{:S(2)}, u32[]{:S(2)}) async-start(bf16[32,16,768]{2,1,0:T(8,128)(2,1)} %gather_fusion.4), calls=%async_computation.2 | async-start | bytes 1572864 | tf_op jit(solution)/shard_map/all_to_all | solution.py:770
  179.4 1.7 gather_fusion.1
  183.5 2.7 convolution_add_fusion
  186.2 4.9 fusion.66
  191.1 3.5 subtract_convert_fusion.3
  194.7 2.2 fusion.146
  197.9 1.5 copy-done.22
  202.2 1.9 multiply_convert_fusion.4
  207.5 4.9 fusion.138
  212.4 2.8 gather_fusion.5
  215.2 9.6 %fusion.148 = (bf16[3072]{0:T(1024)(128)(2,1)}, bf16[512,3072]{1,0:T(8,128)(2,1)S(1)}) fusion(f32[512,3072]{1,0:T(8,128)} %fusion.138, f32[3072]{0:T(1024)} %reshape.919, bf16[512,768]{1,0:T(8,128)(2,1)} %bitcast.200, bf16[3072,768]{1,0:T(8,128)(2,1)} %bitcast.240), kind=kOutput, calls=%fused_computation.310 | convolution fusion | flops 2448946176 | bytes 14960640 | tf_op jit(solution)/shard_map/dot_general | solution.py:32
  224.9 7.1 %multiply_reduce_fusion = (bf16[768]{0:T(1024)(128)(2,1)}, f32[512]{0:T(512)S(1)}, f32[512]{0:T(512)S(1)}, bf16[768]{0:T(1024)(128)(2,1)}, f32[512,768]{1,0:T(8,128)S(1)}) fusion(f32[512,768]{1,0:T(8,128)S(1)} %copy-done.43, f32[512]{0:T(512)S(1)} %copy-done.99, f32[512]{0:T(512)S(1)} %copy-done.84, f32[768]{0:T(1024)S(1)} %copy-done.90, ...), kind=kOutput, calls=%fused_computation.80 | convolution fusion | flops 2419455488 | bytes 11024384 | tf_op jit(solution)/shard_map/dot_general | solution.py:32
  233.4 2.3 fusion.140
  238.6 1.9 add_multiply_fusion
  240.6 3.9 fusion.139
  247.3 2.2 add_multiply_fusion.1
  257.3 8.3 %add_convert_fusion.2 = bf16[512,768]{1,0:T(8,128)(2,1)S(1)} fusion(f32[512,768]{1,0:T(8,128)S(1)} %copy-done.43, bf16[3072,768]{1,0:T(8,128)(2,1)} %bitcast.241, f32[768]{0:T(1024)S(1)} %copy-done.111, f32[512,3072]{1,0:T(8,128)} %fusion.138, f32[3072]{0:T(1024)S(1)} %copy-done.92), kind=kOutput, calls=%fused_computation.97 | convolution fusion | flops 2432827392 | bytes 13384704 | tf_op jit(solution)/shard_map/dot_general | solution.py:22
  265.6 1.6 gather_fusion.2
  267.2 5.8 %all-to-all-start.1 = ((bf16[32,16,768]{2,1,0:T(8,128)(2,1)}), bf16[32,16,768]{2,1,0:T(8,128)(2,1)S(1)}, u32[]{:S(2)}, u32[]{:S(2)}) async-start(bf16[32,16,768]{2,1,0:T(8,128)(2,1)} %gather_fusion.2), calls=%async_computation.1 | async-start | bytes 1572864 | tf_op jit(solution)/shard_map/all_to_all | solution.py:775
  273.1 2.1 fusion.150
  275.2 1.6 fusion.149
  278.5 3.0 fusion.57
  282.8 1.8 convolution_convert_fusion.4
  284.8 1.6 fusion.67
  287.4 1.5 fusion.71
  294.3 24.2 %ssm_grad.1 = (f32[64,768]{1,0:T(8,128)}, f32[64,768]{1,0:T(8,128)}) custom-call(f32[64,768]{1,0:T(8,128)} %slice.213.coef_ref, f32[64,768]{1,0:T(8,128)} %slice.215.rate_ref, f32[320,768]{1,0:T(8,128)} %pad_maximum_fusion.grad_ref), custom_call_target="tpu_custom_call" | custom-call | flops 94371840 | bytes 1769472 | tf_op jit(solution)/shard_map/ssm_grad/pallas_call | solution.py:604
  329.1 2.8 fusion.54
  332.5 2.8 gather_fusion.6
  335.5 3.3 convolution_convert_fusion.3
  338.9 1.8 convolution_convert_fusion.2
  340.7 1.8 convolution_convert_fusion.5
  342.6 4.8 convolution_convert_fusion
  347.4 6.2 %all-to-all-start.3 = ((bf16[32,16,768]{2,1,0:T(8,128)(2,1)}), bf16[32,16,768]{2,1,0:T(8,128)(2,1)S(1)}, u32[]{:S(2)}, u32[]{:S(2)}) async-start(bf16[32,16,768]{2,1,0:T(8,128)(2,1)} %gather_fusion.6), calls=%async_computation.3 | async-start | bytes 1572864 | tf_op jit(solution)/shard_map/all_to_all | solution.py:775
  356.4 8.7 %convolution_convert_fusion.1 = bf16[3072,768]{1,0:T(8,128)(2,1)} fusion(bf16[512,768]{1,0:T(8,128)(2,1)S(1)} %bitcast.201, f32[512,3072]{1,0:T(8,128)} %fusion.138, f32[3072]{0:T(1024)S(1)} %copy-done.93), kind=kOutput, calls=%fused_computation.19 | convolution fusion | flops 2434007040 | bytes 11808768 | tf_op jit(solution)/shard_map/dot_general | solution.py:26
  365.1 138.8 %reduce_grads.1 = (f32[8,4,24,768]{3,2,1,0:T(8,128)}, f32[8,24,3072]{2,1,0:T(8,128)}, f32[8,24,768]{2,1,0:T(8,128)}, f32[8,24,768]{2,1,0:T(8,128)}, f32[8,24,768...) custom-call(bf16[4,4,2,4,24,768]{5,4,3,2,1,0:T(8,128)(2,1)} %bitcast.204, ...), custom_call_target="tpu_custom_call" | custom-call | bytes 200000000 | tf_op jit(solution)/shard_map/reduce_grads/pallas_call | solution.py:512
  506.8 1.6 gather_fusion.3
  508.5 1.7 gather_fusion.7
  513.5 1.4 copy.94
  (420 shorter events, 82.8 us)
Async XLA Ops:
  0.7 5.2 copy-start
  7.3 166.7 %all-to-all-start = ((bf16[32,16,768]{2,1,0:T(8,128)(2,1)}), bf16[32,16,768]{2,1,0:T(8,128)(2,1)}, u32[]{:S(2)}, u32[]{:S(2)}) async-start(bf16[32,16,768]{2,1,0:T(8,128)(2,1)} %gather_fusion), calls=%async_computation | async-start | bytes 1572864 | tf_op jit(solution)/shard_map/all_to_all | solution.py:770
  18.1 4.9 copy-start.2
  18.1 4.9 copy-start.3
  136.6 42.8 %copy-start.107 = (s32[1024]{0:T(1024)}, s32[1024]{0:T(1024)S(1)}, u32[]{:S(2)}) copy-start(s32[1024]{0:T(1024)S(1)} %pad_clamp_fusion.2) | copy-start | bytes 12292
  136.7 46.4 %copy-start.86 = (f32[768]{0:T(1024)}, f32[768]{0:T(1024)S(1)}, u32[]{:S(2)}) copy-start(f32[768]{0:T(1024)S(1)} %add.389) | copy-start | bytes 9220
  136.8 46.3 %copy-start.75 = (f32[768]{0:T(1024)}, f32[768]{0:T(1024)S(1)}, u32[]{:S(2)}) copy-start(f32[768]{0:T(1024)S(1)} %mul.448) | copy-start | bytes 9220
  140.6 18.8 %copy-start.60 = (bf16[512,768]{1,0:T(8,128)(2,1)S(1)}, bf16[512,768]{1,0:T(8,128)(2,1)}, u32[]{:S(2)}) copy-start(bf16[512,768]{1,0:T(8,128)(2,1)} %param.45) | copy-start | bytes 2359300
  155.3 6.1 %copy-start.17 = (bf16[1024,512]{1,0:T(8,128)(2,1)S(1)}, bf16[1024,512]{1,0:T(8,128)(2,1)}, u32[]{:S(2)}) copy-start(bf16[1024,512]{1,0:T(8,128)(2,1)} %convert_element_type.222) | copy-start | bytes 3145732
  163.6 6.0 %copy-start.36 = (f32[1024,512]{1,0:T(8,128)S(1)}, f32[1024,512]{1,0:T(8,128)}, u32[]{:S(2)}) copy-start(f32[1024,512]{1,0:T(8,128)} %copy-done.35) | copy-start | bytes 6291460
  163.6 6.0 %copy-start.57 = (f32[320,768]{1,0:T(8,128)S(1)}, f32[320,768]{1,0:T(8,128)}, u32[]{:S(2)}) copy-start(f32[320,768]{1,0:T(8,128)} %ssm_kernel.1) | copy-start | bytes 2949124
  163.6 6.0 %slice-start.2 = ((f32[320,768]{1,0:T(8,128)}), f32[64,768]{1,0:T(8,128)S(1)}, s32[]{:S(2)}) async-start(f32[320,768]{1,0:T(8,128)} %ssm_kernel.1), calls=%async_computation.6 | async-start | bytes 393216 | tf_op jit(solution)/shard_map/slice | solution.py:663
  174.0 38.4 %all-to-all-start.2 = ((bf16[32,16,768]{2,1,0:T(8,128)(2,1)}), bf16[32,16,768]{2,1,0:T(8,128)(2,1)}, u32[]{:S(2)}, u32[]{:S(2)}) async-start(bf16[32,16,768]{2,1,0:T(8,128)(2,1)} %gather_fusion.4), calls=%async_computation.2 | async-start | bytes 1572864 | tf_op jit(solution)/shard_map/all_to_all | solution.py:770
  191.1 3.5 copy-start.18
  191.1 3.6 copy-start.40
  196.9 4.1 copy-start.31
  201.0 6.5 %slice-start = ((s8[4718592]{0:T(1024)(128)(4,1)}), s8[4194304]{0:T(1024)(128)(4,1)S(1)}, s32[]{:S(2)}) async-start(s8[4718592]{0:T(1024)(128)(4,1)} %bitcast.193), calls=%async_computation.4 | async-start | bytes 8388608
  202.2 5.3 %slice-start.1 = ((s8[4718592]{0:T(1024)(128)(4,1)}), s8[524288]{0:T(1024)(128)(4,1)S(1)}, s32[]{:S(2)}) async-start(s8[4718592]{0:T(1024)(128)(4,1)} %bitcast.193), calls=%async_computation.5 | async-start | bytes 1048576
  215.2 9.6 %copy-start.43 = (f32[512,768]{1,0:T(8,128)S(1)}, f32[512,768]{1,0:T(8,128)}, u32[]{:S(2)}) copy-start(f32[512,768]{1,0:T(8,128)} %copy-done.42) | copy-start | bytes 4718596
  215.2 9.7 %copy-start.84 = (f32[512]{0:T(512)S(1)}, f32[512]{0:T(512)}, u32[]{:S(2)}) copy-start(f32[512]{0:T(512)} %copy-done.83) | copy-start | bytes 6148
  215.2 9.7 %copy-start.90 = (f32[768]{0:T(1024)S(1)}, f32[768]{0:T(1024)}, u32[]{:S(2)}) copy-start(f32[768]{0:T(1024)} %mul.482) | copy-start | bytes 9220
  215.2 9.7 %copy-start.99 = (f32[512]{0:T(512)S(1)}, f32[512]{0:T(512)}, u32[]{:S(2)}) copy-start(f32[512]{0:T(512)} %copy-done.98) | copy-start | bytes 6148
  224.8 7.1 %copy-start.131 = (bf16[512,3072]{1,0:T(8,128)(2,1)}, bf16[512,3072]{1,0:T(8,128)(2,1)S(1)}, u32[]{:S(2)}) copy-start(bf16[512,3072]{1,0:T(8,128)(2,1)S(1)} %get-tuple-element.134) | copy-start | bytes 9437188
  224.9 7.1 %copy-start.38 = (bf16[32,16,768]{2,1,0:T(8,128)(2,1)S(1)}, bf16[32,16,768]{2,1,0:T(8,128)(2,1)}, u32[]{:S(2)}) copy-start(bf16[32,16,768]{2,1,0:T(8,128)(2,1)} %gather_fusion.5) | copy-start | bytes 2359300
  240.6 3.9 copy-start.41
  267.2 80.2 %all-to-all-start.1 = ((bf16[32,16,768]{2,1,0:T(8,128)(2,1)}), bf16[32,16,768]{2,1,0:T(8,128)(2,1)S(1)}, u32[]{:S(2)}, u32[]{:S(2)}) async-start(bf16[32,16,768]{2,1,0:T(8,128)(2,1)} %gather_fusion.2), calls=%async_computation.1 | async-start | bytes 1572864 | tf_op jit(solution)/shard_map/all_to_all | solution.py:775
  278.5 4.3 copy-start.59
  294.3 28.1 %copy-start.102 = (bf16[768]{0:T(1024)(128)(2,1)S(1)}, bf16[768]{0:T(1024)(128)(2,1)}, u32[]{:S(2)}) copy-start(bf16[768]{0:T(1024)(128)(2,1)} %get-tuple-element.78) | copy-start | bytes 4612
  294.3 28.1 %copy-start.116 = (bf16[768]{0:T(1024)(128)(2,1)S(1)}, bf16[768]{0:T(1024)(128)(2,1)}, u32[]{:S(2)}) copy-start(bf16[768]{0:T(1024)(128)(2,1)} %get-tuple-element.135) | copy-start | bytes 4612
  294.3 28.2 %copy-start.103 = (bf16[768]{0:T(1024)(128)(2,1)S(1)}, bf16[768]{0:T(1024)(128)(2,1)}, u32[]{:S(2)}) copy-start(bf16[768]{0:T(1024)(128)(2,1)} %get-tuple-element.76) | copy-start | bytes 4612
  294.3 28.3 %copy-start.106 = (bf16[768]{0:T(1024)(128)(2,1)S(1)}, bf16[768]{0:T(1024)(128)(2,1)}, u32[]{:S(2)}) copy-start(bf16[768]{0:T(1024)(128)(2,1)} %multiply_reduce_fusion.1) | copy-start | bytes 4612
  294.3 28.4 %copy-start.101 = (bf16[768]{0:T(1024)(128)(2,1)S(1)}, bf16[768]{0:T(1024)(128)(2,1)}, u32[]{:S(2)}) copy-start(bf16[768]{0:T(1024)(128)(2,1)} %get-tuple-element.74) | copy-start | bytes 4612
  294.3 28.5 %copy-start.115 = (bf16[768]{0:T(1024)(128)(2,1)S(1)}, bf16[768]{0:T(1024)(128)(2,1)}, u32[]{:S(2)}) copy-start(bf16[768]{0:T(1024)(128)(2,1)} %get-tuple-element.54) | copy-start | bytes 4612
  294.3 28.6 %copy-start.114 = (bf16[768]{0:T(1024)(128)(2,1)S(1)}, bf16[768]{0:T(1024)(128)(2,1)}, u32[]{:S(2)}) copy-start(bf16[768]{0:T(1024)(128)(2,1)} %get-tuple-element.60) | copy-start | bytes 4612
  318.5 10.5 %copy-start.27 = (f32[512,768]{1,0:T(8,128)S(1)}, f32[512,768]{1,0:T(8,128)}, u32[]{:S(2)}) copy-start(f32[512,768]{1,0:T(8,128)} %copy-done.26) | copy-start | bytes 4718596
  318.5 10.5 %copy-start.77 = (f32[768]{0:T(1024)S(1)}, f32[768]{0:T(1024)}, u32[]{:S(2)}) copy-start(f32[768]{0:T(1024)} %copy-done.75) | copy-start | bytes 9220
  318.5 10.5 %copy-start.95 = (f32[512]{0:T(512)S(1)}, f32[512]{0:T(512)}, u32[]{:S(2)}) copy-start(f32[512]{0:T(512)} %div.105) | copy-start | bytes 6148
  318.5 10.5 %copy-start.97 = (f32[512]{0:T(512)S(1)}, f32[512]{0:T(512)}, u32[]{:S(2)}) copy-start(f32[512]{0:T(512)} %rsqrt.22) | copy-start | bytes 6148
  318.5 10.5 %copy-start.104 = (f32[512]{0:T(512)S(1)}, f32[512]{0:T(512)}, u32[]{:S(2)}) copy-start(f32[512]{0:T(512)} %broadcast_multiply_fusion.1) | copy-start | bytes 6148
  318.5 10.5 %copy-start.105 = (f32[512]{0:T(512)S(1)}, f32[512]{0:T(512)}, u32[]{:S(2)}) copy-start(f32[512]{0:T(512)} %broadcast_multiply_fusion.2) | copy-start | bytes 6148
  331.9 3.4 copy-start.39
  335.5 3.3 copy-start.128
  335.5 3.3 copy-start.130
  338.8 3.7 copy-start.132
  347.4 6.8 %copy-start.108 = (bf16[3072]{0:T(1024)(128)(2,1)S(1)}, bf16[3072]{0:T(1024)(128)(2,1)}, u32[]{:S(2)}) copy-start(bf16[3072]{0:T(1024)(128)(2,1)} %get-tuple-element.133) | copy-start | bytes 18436
  347.4 9.0 %copy-start.93 = (f32[3072]{0:T(1024)S(1)}, f32[3072]{0:T(1024)}, u32[]{:S(2)}) copy-start(f32[3072]{0:T(1024)} %reshape.919) | copy-start | bytes 36868
  347.4 161.0 %all-to-all-start.3 = ((bf16[32,16,768]{2,1,0:T(8,128)(2,1)}), bf16[32,16,768]{2,1,0:T(8,128)(2,1)S(1)}, u32[]{:S(2)}, u32[]{:S(2)}) async-start(bf16[32,16,768]{2,1,0:T(8,128)(2,1)} %gather_fusion.6), calls=%async_computation.3 | async-start | bytes 1572864 | tf_op jit(solution)/shard_map/all_to_all | solution.py:775
  513.5 3.9 copy-start.1
  (92 other events, 171.2 us)

commit v2 on v1

--- a/solution.py
+++ b/solution.py
@@ -64,6 +64,24 @@
         for device in partners:
             pl.semaphore_signal(barrier, inc=1, device_id=device, device_id_type=MESH)
         pl.semaphore_wait(barrier, len(partners))
+
+    def meet_all(self):
+        barrier = pltpu.get_barrier_semaphore()
+        slots = self.rep_count * self.shard_count
+        me = self.rep * self.shard_count + self.shard
+
+        def greet(offset, unused):
+            device = lax.rem(me + offset, slots)
+            pl.semaphore_signal(
+                barrier,
+                inc=1,
+                device_id=(lax.div(device, self.shard_count), lax.rem(device, self.shard_count)),
+                device_id_type=MESH,
+            )
+            return unused
+
+        lax.fori_loop(1, slots, greet, 0)
+        pl.semaphore_wait(barrier, slots - 1)
 
 
 def plane_masks(rep_count, order):
@@ -94,31 +112,186 @@
     )
 
 
-AHEAD = 3
-
-
-def gather_body(rep_count, shard_count, units, *refs):
+def deal_start(pieces, order, staged, landed, sems, place):
+    slots = place.rep_count * place.shard_count
+    me = place.rep * place.shard_count + place.shard
+
+    def step(offset, unused):
+        device = lax.rem(me + offset, slots)
+        chosen = order[device]
+        for i, array in enumerate(pieces):
+            staged[offset, i] = array[chosen]
+        deal_copy(staged, landed, sems, place, offset).start()
+        return unused
+
+    lax.fori_loop(1, slots, step, 0)
+    for i, array in enumerate(pieces):
+        landed[me, i] = array[order[me]]
+
+
+def deal_copy(staged, landed, sems, place, offset):
+    slots = place.rep_count * place.shard_count
+    me = place.rep * place.shard_count + place.shard
+    device = lax.rem(me + offset, slots)
+    return remote(
+        staged.at[offset],
+        landed.at[me],
+        sems,
+        offset,
+        (lax.div(device, place.shard_count), lax.rem(device, place.shard_count)),
+    )
+
+
+def deal_end(outs, order, staged, landed, sems, place):
+    slots = place.rep_count * place.shard_count
+
+    def wait(offset, unused):
+        deal_copy(staged, landed, sems, place, offset).wait()
+        return unused
+
+    def step(spot, unused):
+        chosen = order[spot]
+        for i, out in enumerate(outs):
+            out[spot] = landed[chosen, i]
+        return unused
+
+    lax.fori_loop(1, slots, wait, 0)
+    lax.fori_loop(0, slots, step, 0)
+
+
+def split_half(array):
+    high = to_half(array)
+    return high, to_half(array - to_float(high))
+
+
+def dot_fine(one, two):
+    (one_high, one_low), (two_high, two_low) = one, two
+    total = dot_nn(one_high, two_high) + dot_nn(one_low, two_high)
+    return total + dot_nn(one_high, two_low)
+
+
+def wave_tables(rows, period, length):
+    freq = lax.broadcasted_iota(jnp.int32, (rows, length), 0)
+    time = lax.broadcasted_iota(jnp.int32, (rows, length), 1)
+    phase = lax.rem((2 * freq + 1) * time, 4 * period)
+    angle = to_float(phase) * (jnp.pi / (2 * period))
+    return jnp.cos(angle), -jnp.sin(angle)
+
+
+def tile_kernel(coef_ref, rate_ref, out_ref, lanes):
+    states, length = coef_ref.shape[0], out_ref.shape[0]
+    count = length // 8
+    row = to_float(lax.broadcasted_iota(jnp.int32, (8, 128), 0))
+
+    batch = 8
+
+    def step(block, totals):
+        first = pl.multiple_of(block * batch, batch)
+        rates = rate_ref[pl.ds(first, batch), lanes]
+        coefs = coef_ref[pl.ds(first, batch), lanes]
+        for n in range(batch):
+            rate = jnp.broadcast_to(rates[n : n + 1], (8, 128))
+            coef = jnp.broadcast_to(coefs[n : n + 1], (8, 128))
+            hop = jnp.exp(rate * -8.0)
+            far = jnp.exp(rate * -64.0)
+            terms = [coef * jnp.exp(-rate * row)]
+            terms.append(terms[0] * hop)
+            hop = hop * hop
+            terms += [terms[0] * hop, terms[1] * hop]
+            hop = hop * hop
+            terms += [terms[0] * hop, terms[1] * hop, terms[2] * hop, terms[3] * hop]
+            new = []
+            for i in range(count):
+                if i >= 8:
+                    terms[i % 8] = terms[i % 8] * far
+                new.append(totals[i] + terms[i % 8])
+            totals = new
+        return tuple(totals)
+
+    totals = lax.fori_loop(0, states // batch, step, (jnp.zeros((8, 128), jnp.float32),) * count)
+    for i in range(count):
+        out_ref[8 * i : 8 * i + 8, lanes] = totals[i]
+
+
+def tile_grads(coef_ref, rate_ref, grad_ref, coef_out, rate_out, lanes):
+    states, length = coef_ref.shape[0], grad_ref.shape[0]
+    count = length // 8
+    row = to_float(lax.broadcasted_iota(jnp.int32, (8, 128), 0))
+    batch = 8
+
+    def step(block, unused):
+        first = pl.multiple_of(block * batch, batch)
+        rates = rate_ref[pl.ds(first, batch), lanes]
+        rate = [jnp.broadcast_to(rates[i : i + 1], (8, 128)) for i in range(batch)]
+        hop = [jnp.exp(r * -8.0) for r in rate]
+        plain = [jnp.zeros((8, 128), jnp.float32) for _ in range(batch)]
+        slope = [jnp.zeros((8, 128), jnp.float32) for _ in range(batch)]
+        for j in range(count - 1, -1, -1):
+            grad = grad_ref[8 * j : 8 * j + 8, lanes]
+            for i in range(batch):
+                slope[i] = slope[i] * hop[i] + plain[i]
+                plain[i] = plain[i] * hop[i] + grad
+        ones, twos = [], []
+        for i in range(batch):
+            start = jnp.exp(-rate[i] * row)
+            ones.append(jnp.sum(start * plain[i], axis=0, keepdims=True))
+            ramp = start * (8.0 * hop[i] * slope[i] + row * plain[i])
+            twos.append(jnp.sum(ramp, axis=0, keepdims=True))
+        coef_out[pl.ds(first, batch), lanes] = jnp.concatenate(ones)
+        rate_out[pl.ds(first, batch), lanes] = -coef_ref[pl.ds(first, batch), lanes] * (
+            jnp.concatenate(twos)
+        )
+        return unused
+
+    lax.fori_loop(0, states // batch, step, 0)
+
+
+AHEAD = 6
+LAG = 2
+
+
+def gather_body(rep_count, shard_count, units, shorts, *refs):
     tensors = 1 + max(tensor for tensor, _ in units)
-    locals_, pack = refs[:tensors], refs[tensors]
-    outs, pack_out = refs[tensors + 1 : 2 * tensors + 1], refs[2 * tensors + 1]
-    held, send, receive, pack_send, pack_receive, done = refs[2 * tensors + 2 :]
+    order, unpack, tokens, cotangent = refs[:4]
+    locals_, pack, params = refs[4 : 4 + tensors], refs[4 + tensors], refs[5 + tensors : 8 + tensors]
+    rest = refs[8 + tensors :]
+    outs, pack_out = rest[:tensors], rest[tensors]
+    tokens_out, cotangent_out, kernel_wave, taps_wave, waves, coef_ref, rate_ref = rest[
+        tensors + 1 : tensors + 8
+    ]
+    (held, table, kernel, params_in, staged, landed) = rest[tensors + 8 : tensors + 14]
+    send, receive, small_send, small_receive, done, deal_send, deal_receive = rest[tensors + 14 :]
     place = Place(rep_count, shard_count)
-    place.meet()
+    place.meet_all()
     me, shard = place.rep, place.shard
     others = shard_count - 1
     stages = len(plane_masks(rep_count, 0)) + 1
     width = others + stages
-    keep = []
 
     small = []
+    owned = params[0].shape[0]
+    spot = pl.multiple_of(shard * owned, 8)
     for k in range(1, shard_count):
-        copy = remote(
-            pack, pack_out.at[shard], (pack_send, pack_receive), k - 1, place.by_shard(k)
-        )
+        for i, source in enumerate((pack,) + tuple(params)):
+            target = pack_out.at[shard] if i == 0 else params_in.at[i - 1, shard]
+            copy = remote(
+                source,
+                target,
+                (small_send, small_receive),
+                (k - 1) * 4 + i,
+                place.by_shard(k),
+            )
+            copy.start()
+            small.append(copy)
+    own = []
+    for i, source in enumerate((pack,) + tuple(params)):
+        target = pack_out.at[shard] if i == 0 else params_in.at[i - 1, shard]
+        copy = pltpu.make_async_copy(source, target, done.at[tensors + i])
         copy.start()
-        small.append(copy)
-    own = pltpu.make_async_copy(pack, pack_out.at[shard], done.at[tensors])
-    own.start()
+        own.append(copy)
+    deal_start(
+        (tokens, cotangent), order, staged, landed, (deal_send, deal_receive), place
+    )
     for tensor in range(tensors):
         pltpu.make_async_copy(
             locals_[tensor], outs[tensor].at[shard], done.at[tensor]
@@ -162,15 +335,82 @@
                     done.at[tensor],
                 ).start()
 
+    channels = kernel.shape[1]
+    length, taps = kernel.shape[0], params[0].shape[1]
+    half = length + shorts * taps
+    jobs = []
+
+    def tables():
+        for part, (long, short) in enumerate(
+            zip(wave_tables(length, length, length), wave_tables(taps, taps, taps))
+        ):
+            base = part * half
+            table[base : base + half, :] = jnp.zeros((half, half), jnp.float32)
+            table[base : base + length, 0:length] = long
+            for i in range(shorts):
+                at = length + i * taps
+                table[base + at : base + at + taps, at : at + taps] = short
+        waves[...] = to_half(table[...])
+
+    def arrive():
+        for copy in small + own:
+            copy.wait()
+
+    def arrange(tile):
+        lanes = slice(tile * 128, tile * 128 + 128)
+        rows = [
+            to_float(params_in[i].reshape(channels, taps)[lanes]) for i in range(3)
+        ]
+        both = jnp.concatenate([rows[1], rows[2]], axis=1).T
+        coef_ref[:, lanes] = both[:taps]
+        rate_ref[:, lanes] = both[taps:]
+        lags = jnp.concatenate([rows[0], rows[0]], axis=1).T
+        kernel[0:taps, lanes] = lags[:taps]
+
+    def wave_of(lags, out, fine):
+        source = kernel[0:lags, :]
+        right = split_half(source) if fine else (to_half(source), None)
+        for base in (0, half):
+            left = split_half(table[base : base + length, 0:lags])
+            if fine:
+                top = dot_fine(left, right)
+            else:
+                top = dot_nn(left[0], right[0]) + dot_nn(left[1], right[0])
+            out[base : base + length, :] = top * (1.0 / length)
+            left = split_half(table[base + length : base + length + taps, length : length + taps])
+            head = [part[:taps] if part is not None else None for part in right]
+            if fine:
+                low = dot_fine(left, head)
+            else:
+                low = dot_nn(left[0], head[0]) + dot_nn(left[1], head[0])
+            for i in range(shorts):
+                at = base + length + i * taps
+                out[at : at + taps, :] = low * (1.0 / taps)
+
+    jobs.append(tables)
+    jobs.append(arrive)
+    for tile in range(channels // 128):
+        jobs.append(lambda tile=tile: arrange(tile))
+    jobs.append(lambda: wave_of(taps, taps_wave, False))
+    for tile in range(channels // 128):
+        jobs.append(
+            lambda tile=tile: tile_kernel(
+                coef_ref, rate_ref, kernel, slice(tile * 128, tile * 128 + 128)
+            )
+        )
+    jobs.append(lambda: wave_of(length, kernel_wave, True))
+
     flights = {}
     total = len(units)
     for unit in range(min(AHEAD, total)):
         flights[unit, -1] = across(unit)
         for copy in flights[unit, -1]:
             copy.start()
-    for step in range(total + stages):
+    steps = total + stages * LAG
+    per_step = -(-len(jobs) // steps)
+    for step in range(steps):
         for stage in range(stages, -1, -1):
-            unit = step - stage
+            unit = step - stage * LAG
             if not 0 <= unit < total:
                 continue
             if stage == 0:
@@ -189,9 +429,11 @@
                 write(unit, 0, 1)
             else:
                 write(unit, 1 << (stage - 1), 1 << (stage - 1))
-    for copy in small:
-        copy.wait()
-    own.wait()
+        for job in jobs[step * per_step : (step + 1) * per_step]:
+            job()
+    deal_end(
+        (tokens_out, cotangent_out), unpack, staged, landed, (deal_send, deal_receive), place
+    )
     for unit in range(total):
         for copy in flights[unit, -1]:
             copy.wait_send()
@@ -201,7 +443,9 @@
         pltpu.make_async_copy(outs[tensor], outs[tensor], done.at[tensor]).wait()
 
 
-def gather_weights(squares, up, down, pack, rep_count, shard_count):
+def gather_all(order, unpack, tokens, cotangent, squares, up, down, pack, params, counts, shorts):
+    rep_count, shard_count = counts
+    slots = rep_count * shard_count
     rows, width = squares[0].shape
     piece = rows // rep_count
     parts = up.shape[1] // width
@@ -214,39 +458,61 @@
     for q in range(parts):
         units.append((len(squares) + 1, lambda ref, q=q: ref.at[q]))
     anywhere = pl.BlockSpec(memory_space=pl.ANY)
+    here = pl.BlockSpec(memory_space=pltpu.VMEM)
+    scalars = pl.BlockSpec(memory_space=pltpu.SMEM)
     copies = len(units) * (shard_count + len(plane_masks(rep_count, 0)))
+    smalls = (shard_count - 1) * 4
+    owned, taps = params[0].shape
+    channels = owned * shard_count
+    half = tokens.shape[0]
+    length = half - shorts * taps
+    piece_shape = (slots, half // slots, width)
     outs = [jax.ShapeDtypeStruct((shard_count,) + w.shape, w.dtype) for w in locals_ + [pack]]
+    spaces = [anywhere] * len(outs) + [here] * 7
+    outs += [jax.ShapeDtypeStruct(piece_shape, tokens.dtype)] * 2
+    outs += [jax.ShapeDtypeStruct((2 * half, channels), jnp.float32)] * 2
+    outs += [jax.ShapeDtypeStruct((2 * half, half), jnp.bfloat16)]
+    outs += [jax.ShapeDtypeStruct((taps, channels), jnp.float32)] * 2
     found = pl.pallas_call(
-        lambda *refs: gather_body(rep_count, shard_count, units, *refs),
-        in_specs=[anywhere] * (len(locals_) + 1),
-        out_specs=[anywhere] * len(outs),
+        lambda *refs: gather_body(rep_count, shard_count, units, shorts, *refs),
+        in_specs=[scalars] * 2 + [here] * 2 + [anywhere] * (len(locals_) + 4),
+        out_specs=spaces,
         out_shape=outs,
         scratch_shapes=[
             pltpu.VMEM((len(units), rep_count, shard_count - 1, piece, width), jnp.bfloat16),
+            pltpu.VMEM((2 * half, half), jnp.float32),
+            pltpu.VMEM((length, channels), jnp.float32),
+            pltpu.VMEM((3, shard_count, owned, taps), jnp.bfloat16),
+            pltpu.VMEM((slots, 2) + piece_shape[1:], jnp.bfloat16),
+            pltpu.VMEM((slots, 2) + piece_shape[1:], jnp.bfloat16),
             pltpu.SemaphoreType.DMA((copies,)),
             pltpu.SemaphoreType.DMA((copies,)),
-            pltpu.SemaphoreType.DMA((shard_count - 1,)),
-            pltpu.SemaphoreType.DMA((shard_count - 1,)),
-            pltpu.SemaphoreType.DMA((len(outs),)),
+            pltpu.SemaphoreType.DMA((smalls,)),
+            pltpu.SemaphoreType.DMA((smalls,)),
+            pltpu.SemaphoreType.DMA((len(locals_) + 4,)),
+            pltpu.SemaphoreType.DMA((slots,)),
+            pltpu.SemaphoreType.DMA((slots,)),
         ],
         compiler_params=pltpu.CompilerParams(
-            collective_id=0, has_side_effects=True, vmem_limit_bytes=40 * 1024 * 1024
+            collective_id=0, has_side_effects=True, vmem_limit_bytes=56 * 1024 * 1024
         ),
         cost_estimate=pl.CostEstimate(flops=0, bytes_accessed=200_000_000, transcendentals=0),
-        name="gather_weights",
-    )(*locals_, pack)
-    whole = [w.reshape(shard_count * rows, width) for w in found[: len(squares)]]
-    whole.append(found[-3].reshape(shard_count * rows, up.shape[1]))
-    whole.append(found[-2].reshape(shard_count * down.shape[0], width))
-    return whole, found[-1]
-
-
-def add_into(target, other, count):
-    def step(i, unused):
-        target[i] = to_half(to_float(target[i]) + to_float(other[i]))
-        return unused
-
-    lax.fori_loop(0, count, step, 0)
+        name="gather_all",
+    )(
+        order,
+        unpack,
+        tokens.reshape(piece_shape),
+        cotangent.reshape(piece_shape),
+        *locals_,
+        pack,
+        *params,
+    )
+    count = len(squares)
+    whole = [w.reshape(shard_count * rows, width) for w in found[:count]]
+    whole.append(found[count].reshape(shard_count * rows, up.shape[1]))
+    whole.append(found[count + 1].reshape(shard_count * down.shape[0], width))
+    packs, balanced, grads = found[count + 2 : count + 5]
+    return whole, packs, balanced.reshape(half, width), grads.reshape(half, width), found[count + 5 :]
 
 
 class Reduction:
@@ -407,17 +673,24 @@
 
 
 REDUCE_AHEAD = 4
-
-
-def reduce_body(rep_count, shard_count, units, tensors, *refs):
+REDUCE_LAG = 2
+
+
+def reduce_body(rep_count, shard_count, units, tensors, kinds_count, *refs):
     planes = len(plane_masks(rep_count, 0))
-    sources, outs = refs[:tensors], refs[tensors : 2 * tensors]
-    rest = refs[2 * tensors :]
+    order, unpack, grads, coef_ref, rate_ref, kernel_grad, taps_grad = refs[:7]
+    sources = list(refs[7 : 6 + tensors])
+    outs = refs[6 + tensors : 6 + 2 * tensors]
+    grads_out = refs[6 + 2 * tensors]
+    rest = refs[7 + 2 * tensors :]
     per_kind = planes + 4
-    kinds = [rest[i * per_kind : (i + 1) * per_kind] for i in range(2)]
-    send, receive, kept = rest[2 * per_kind :]
+    kinds = [rest[i * per_kind : (i + 1) * per_kind] for i in range(kinds_count)]
+    rest = rest[kinds_count * per_kind :]
+    made, flat, coef_grad, rate_grad, staged, landed = rest[:6]
+    send, receive, kept, deal_send, deal_receive = rest[6:]
+    sources.append(made)
     place = Place(rep_count, shard_count)
-    place.meet()
+    place.meet_all()
     count = flights_of(rep_count, shard_count)
     works = []
     for index, (tensor, pick, writer, kind, slot) in enumerate(units):
@@ -438,34 +711,62 @@
                 ),
             )
         )
+    taps, channels = taps_grad.shape
+
+    def ssm_job(tile):
+        lanes = slice(tile * 128, tile * 128 + 128)
+        tile_grads(coef_ref, rate_ref, kernel_grad, coef_grad, rate_grad, lanes)
+        both = jnp.concatenate([taps_grad[:, lanes], coef_grad[:, lanes]]).T
+        last = jnp.concatenate([rate_grad[:, lanes], rate_grad[:, lanes]]).T
+        flat[lanes, :] = jnp.concatenate([both, last[:, :taps]], axis=1)
+
+    def fill_job():
+        piece = channels // (shard_count * rep_count)
+        for i in range(shard_count * rep_count):
+            made[i // rep_count, (i % rep_count) // 2, i % 2] = to_half(
+                flat[i * piece : (i + 1) * piece, :]
+            )
+
+    jobs = [lambda tile=tile: ssm_job(tile) for tile in range(channels // 128)] + [fill_job]
     todo = [work.steps() for work in works]
     for work in works[:REDUCE_AHEAD]:
         work.start()
+    deal_start((grads,), order, staged, landed, (deal_send, deal_receive), place)
     length = len(todo[0])
-    for step in range(len(works) + length - 1):
+    for step in range(len(works) + (length - 1) * REDUCE_LAG):
+        if step < len(jobs):
+            jobs[step]()
         for position in range(length - 1, -1, -1):
-            index = step - position
+            index = step - position * REDUCE_LAG
             if 0 <= index < len(works):
                 todo[index][position]()
                 if position == 0 and index + REDUCE_AHEAD < len(works):
                     works[index + REDUCE_AHEAD].start()
+    deal_end((grads_out,), unpack, staged, landed, (deal_send, deal_receive), place)
     for work in works:
         work.finish()
 
 
-def reduce_grads(down, up, squares, pack, rep_count, shard_count):
+def reduce_all(order, unpack, grads, rows_in, down, up, squares, pack, counts):
+    rep_count, shard_count = counts
+    slots = rep_count * shard_count
     width = squares[0].shape[1]
-    piece = squares[0].shape[0] // (shard_count * rep_count)
+    piece = squares[0].shape[0] // slots
     parts = up.shape[1] // width
     lead = (shard_count, rep_count // 2, 2)
     tensors = [down.reshape(lead + (parts, piece, width)), up.reshape(lead + (piece, up.shape[1]))]
     tensors += [g.reshape(lead + (piece, width)) for g in squares]
     pack_rows, pack_width = pack.shape[1] // rep_count, pack.shape[2]
     tensors.append(pack.reshape(lead + (pack_rows, pack_width)))
+    states, channels = rows_in[0].shape
+    owned = channels // slots
     outs = [jax.ShapeDtypeStruct((rep_count, parts, piece, width), jnp.float32)]
     outs.append(jax.ShapeDtypeStruct((rep_count, piece, up.shape[1]), jnp.float32))
     outs += [jax.ShapeDtypeStruct((rep_count, piece, width), jnp.float32)] * len(squares)
     outs.append(jax.ShapeDtypeStruct((rep_count, pack_rows, pack_width), jnp.float32))
+    outs.append(jax.ShapeDtypeStruct((rep_count, owned, 3 * states), jnp.float32))
+    piece_shape = (slots, grads.shape[0] // slots, grads.shape[1])
+    outs.append(jax.ShapeDtypeStruct(piece_shape, grads.dtype))
 
     def whole_writer(out, at, value):
         out[at] = value
@@ -495,6 +796,7 @@
         units.append((2 + i, lambda ref: ref, whole_writer, 0, len(units)))
     plain = len(units)
     units.append((2 + len(squares), lambda ref: ref, whole_writer, 1, 0))
+    units.append((3 + len(squares), lambda ref: ref, whole_writer, 2, 0))
     half = rep_count // 2
     planes = len(plane_masks(rep_count, 0))
 
@@ -509,141 +811,47 @@
 
     flights = len(units) * flights_of(rep_count, shard_count)
     anywhere = pl.BlockSpec(memory_space=pl.ANY)
+    here = pl.BlockSpec(memory_space=pltpu.VMEM)
+    scalars = pl.BlockSpec(memory_space=pltpu.SMEM)
     found = pl.pallas_call(
-        lambda *refs: reduce_body(rep_count, shard_count, units, len(tensors), *refs),
-        in_specs=[anywhere] * len(tensors),
-        out_specs=[pl.BlockSpec(memory_space=pltpu.VMEM)] * len(outs),
+        lambda *refs: reduce_body(rep_count, shard_count, units, len(tensors) + 1, 3, *refs),
+        in_specs=[scalars] * 2 + [here] * 5 + [anywhere] * len(tensors),
+        out_specs=[here] * len(outs),
         out_shape=outs,
         scratch_shapes=buffers(plain, piece, width)
         + buffers(1, pack_rows, pack_width)
-        + [pltpu.SemaphoreType.DMA((flights,))] * 3,
+        + buffers(1, owned, 3 * states)
+        + [
+            pltpu.VMEM(lead + (owned, 3 * states), jnp.bfloat16),
+            pltpu.VMEM((channels, 3 * states), jnp.float32),
+            pltpu.VMEM((states, channels), jnp.float32),
+            pltpu.VMEM((states, channels), jnp.float32),
+            pltpu.VMEM((slots, 1) + piece_shape[1:], jnp.bfloat16),
+            pltpu.VMEM((slots, 1) + piece_shape[1:], jnp.bfloat16),
+        ]
+        + [pltpu.SemaphoreType.DMA((flights,))] * 3
+        + [pltpu.SemaphoreType.DMA((slots,))] * 2,
         compiler_params=pltpu.CompilerParams(
             collective_id=1, has_side_effects=True, vmem_limit_bytes=60 * 1024 * 1024
         ),
         cost_estimate=pl.CostEstimate(flops=0, bytes_accessed=200_000_000, transcendentals=0),
-        name="reduce_grads",
-    )(*tensors)
+        name="reduce_all",
+    )(order, unpack, grads.reshape(piece_shape), *rows_in, *tensors)
     rows = rep_count * piece
     return (
+        found[-1].reshape(grads.shape),
         found[0].reshape(rows * parts, width),
         found[1].reshape(rows, up.shape[1]),
-        [g.reshape(rows, width) for g in found[2:-1]],
-        found[-1].reshape(pack.shape[1], pack_width),
-    )
-
-
-def ssm_kernel_body(coef_ref, rate_ref, out_ref):
-    states, lanes = coef_ref.shape
-    taps = 64
-    count = out_ref.shape[0] // taps
-    lag = to_float(lax.broadcasted_iota(jnp.int32, (taps, lanes), 0))
-
-    def step(n, totals):
-        rate = rate_ref[pl.ds(n, 1), :]
-        factor = coef_ref[pl.ds(n, 1), :]
-        block = jnp.exp(-rate * taps)
-        decay = jnp.exp(-rate * lag)
-        new = []
-        for q in range(count):
-            new.append(totals[q] + factor * decay)
-            factor = factor * block
-        return tuple(new)
-
-    zero = jnp.zeros((taps, lanes), jnp.float32)
-    totals = lax.fori_loop(0, states, step, (zero,) * count)
-    for q in range(count):
-        out_ref[q * taps : (q + 1) * taps, :] = totals[q]
-
-
-def ssm_kernel(coef, rate, length):
-    states, channels = coef.shape
-    return pl.pallas_call(
-        ssm_kernel_body,
-        grid=(channels // 128,),
-        in_specs=[pl.BlockSpec((states, 128), lambda i: (0, i))] * 2,
-        out_specs=pl.BlockSpec((length, 128), lambda i: (0, i)),
-        out_shape=jax.ShapeDtypeStruct((length, channels), jnp.float32),
-        cost_estimate=pl.CostEstimate(
-            flops=2 * states * length * channels,
-            bytes_accessed=4 * channels * (2 * states + length),
-            transcendentals=states * 64 * channels,
-        ),
-        name="ssm_kernel",
-    )(coef, rate)
-
-
-def ssm_grad_body(coef_ref, rate_ref, grad_ref, coef_out, rate_out):
-    states, lanes = coef_ref.shape
-    taps = 64
-    count = grad_ref.shape[0] // taps
-    lag = to_float(lax.broadcasted_iota(jnp.int32, (taps, lanes), 0))
-
-    def step(n, unused):
-        rate = rate_ref[pl.ds(n, 1), :]
-        block = jnp.exp(-rate * taps)
-        decay = jnp.exp(-rate * lag)
-        plain = jnp.zeros((taps, lanes), jnp.float32)
-        ramp = jnp.zeros((taps, lanes), jnp.float32)
-        for q in range(count - 1, -1, -1):
-            grad = grad_ref[q * taps : (q + 1) * taps, :]
-            plain = plain * block + grad
-            ramp = ramp * block + grad * float(q * taps)
-        ramp = ramp + plain * lag
-        coef_out[pl.ds(n, 1), :] = jnp.sum(plain * decay, axis=0, keepdims=True)
-        rate_out[pl.ds(n, 1), :] = -coef_ref[pl.ds(n, 1), :] * jnp.sum(
-            ramp * decay, axis=0, keepdims=True
-        )
-        return unused
-
-    lax.fori_loop(0, states, step, 0)
-
-
-def ssm_grad(coef, rate, grad):
-    states, channels = coef.shape
-    length = grad.shape[0]
-    return pl.pallas_call(
-        ssm_grad_body,
-        grid=(channels // 128,),
-        in_specs=[pl.BlockSpec((states, 128), lambda i: (0, i))] * 2
-        + [pl.BlockSpec((length, 128), lambda i: (0, i))],
-        out_specs=[pl.BlockSpec((states, 128), lambda i: (0, i))] * 2,
-        out_shape=[jax.ShapeDtypeStruct((states, channels), jnp.float32)] * 2,
-        cost_estimate=pl.CostEstimate(
-            flops=6 * states * length * channels,
-            bytes_accessed=4 * channels * (4 * states + length),
-            transcendentals=states * 64 * channels,
-        ),
-        name="ssm_grad",
-    )(coef, rate, grad)
-
-
-def wave_tables(rows, period, length):
-    freq = lax.broadcasted_iota(jnp.int32, (rows, length), 0)
-    time = lax.broadcasted_iota(jnp.int32, (rows, length), 1)
-    phase = ((2 * freq + 1) * time) % (2 * period)
-    angle = to_float(phase) * (jnp.pi / period)
-    return jnp.cos(angle), -jnp.sin(angle)
+        [g.reshape(rows, width) for g in found[2 : 2 + len(squares)]],
+        found[-3].reshape(pack.shape[1], pack_width),
+        found[-2].reshape(owned * rep_count, 3 * states),
+    )
 
 
 class Waves:
-    def __init__(self, length, short, count):
-        self.length, self.short, self.count = length, short, count
+    def __init__(self, table, length, short, count):
+        self.low, self.length, self.short, self.count = table, length, short, count
         self.half = length + short * count
-        top = wave_tables(length, 2 * length, length)
-        low = wave_tables(short, 2 * short, short)
-        self.long_rows = top
-        self.short_rows = low
-        parts = []
-        for a, b in zip(top, low):
-            rows = [jnp.pad(a, ((0, 0), (0, short * count)))]
-            for i in range(count):
-                rows.append(
-                    jnp.pad(b, ((0, 0), (length + i * short, (count - 1 - i) * short)))
-                )
-            parts.append(jnp.concatenate(rows))
-        full = jnp.concatenate(parts)
-        self.exact = lax.optimization_barrier(full)
-        self.low = lax.optimization_barrier(to_half(full))
         self.gain = jnp.concatenate(
             [
                 jnp.full((length, 1), 1.0 / length, jnp.float32),
@@ -656,13 +864,6 @@
 
     def back(self, real, imag):
         return dot_tn(self.low, jnp.concatenate([to_half(real), to_half(imag)]))
-
-    def filter(self, taps):
-        lags, channels = taps.shape
-        first = jnp.pad(taps, ((0, self.length - lags), (0, 0)))
-        rows = jnp.concatenate([first] + [taps[: self.short]] * self.count)
-        wave = jnp.dot(self.exact, rows, precision=lax.Precision.HIGH)
-        return wave[: self.half] * self.gain, wave[self.half :] * self.gain
 
     def lags(self, real, imag, count):
         real, imag = real * self.gain, imag * self.gain
@@ -765,21 +966,13 @@
     sending = jnp.sum(jnp.where(own_target[None, :] == ids[:, None], ids[None, :], 0), axis=1)
     unpacking = jnp.sum(jnp.where(arrival[None, :] == ids[:, None], ids[None, :], 0), axis=1)
 
-    def deal(array):
-        pieces = array.reshape(slots, piece_rows, width)[sending]
-        came = lax.all_to_all(pieces, ("rep", "shard"), split_axis=0, concat_axis=0, tiled=True)
-        return came[unpacking].reshape(rows, width)
-
     def give_back(array):
         pieces = array.reshape(slots, piece_rows, width)[arrival]
         came = lax.all_to_all(pieces, ("rep", "shard"), split_axis=0, concat_axis=0, tiled=True)
         return came[own_target].reshape(rows, width)
 
-    balanced = to_float(deal(tokens))
-
     pack = jnp.concatenate(
-        [shift_taps.T, ssm_coef.T, ssm_rate.T]
-        + [
+        [
             vector.reshape(1, owned)
             for vector in (
                 ln1_scale,
@@ -796,13 +989,25 @@
         ]
         + [b_up.reshape(-1, owned)]
     )
-    (weight_q, weight_k, weight_v, weight_o, weight_up, weight_down), packs = gather_weights(
-        [w_query, w_key, w_value, w_out], w_up, w_down, pack, rep_count, shard_count
-    )
-    tops = 3 * taps + 10
-    up_bias = to_float(packs[:, tops:].reshape(1, -1))
-    small = to_float(jnp.swapaxes(packs[:, :tops], 0, 1).reshape(tops, width))
-    tap_rows, coef_rows, rate_rows = small[:taps], small[taps : 2 * taps], small[2 * taps : 3 * taps]
+    counts = (rep_count, shard_count)
+    weights, packs, balanced, grad_low, spectra = gather_all(
+        sending,
+        unpacking,
+        tokens,
+        cotangent,
+        [w_query, w_key, w_value, w_out],
+        w_up,
+        w_down,
+        pack,
+        [shift_taps, ssm_coef, ssm_rate],
+        counts,
+        shorts,
+    )
+    weight_q, weight_k, weight_v, weight_o, weight_up, weight_down = weights
+    kernel_wave, taps_wave, table, coef_rows, rate_rows = spectra
+    balanced = to_float(balanced)
+    up_bias = to_float(packs[:, 10:].reshape(1, -1))
+    small = to_float(jnp.swapaxes(packs[:, :10], 0, 1).reshape(10, width))
     (
         gain_one,
         bias_one,
@@ -814,13 +1019,12 @@
         gain_two,
         bias_two,
         down_bias,
-    ) = [small[3 * taps + i][None] for i in range(10)]
-
-    waves = Waves(long_blocks * taps, taps, shorts)
+    ) = [small[i : i + 1] for i in range(10)]
+
+    waves = Waves(table, long_blocks * taps, taps, shorts)
     half = waves.half
-    kernel = ssm_kernel(coef_rows, rate_rows, long_blocks * taps)
-    ker_re, ker_im = waves.filter(kernel)
-    tap_re, tap_im = waves.filter(tap_rows)
+    ker_re, ker_im = kernel_wave[:half], kernel_wave[half:]
+    tap_re, tap_im = taps_wave[:half], taps_wave[half:]
 
     hat_one, scale_one = row_stats(balanced)
     normed = to_half(hat_one * gain_one + bias_one)
@@ -852,7 +1056,6 @@
     result = middle + (branch + down_bias)
     block_output = give_back(to_half(result))
 
-    grad_low = deal(cotangent)
     grad_out = to_float(grad_low)
     part_down = dot_tn(active, grad_low, jnp.bfloat16)
     g_b_down = column_sum(grad_low)
@@ -880,7 +1083,6 @@
     grad_kernel = waves.lags(
         g_re * in_re + g_im * in_im, g_im * in_re - g_re * in_im, long_blocks * taps
     )
-    g_coef, g_rate = ssm_grad(coef_rows, rate_rows, grad_kernel)
     grad_shifted = grad_inputs * values
     grad_value = to_half(grad_inputs * shifted)
     part_value = dot_tn(normed, grad_value, jnp.bfloat16)
@@ -895,7 +1097,6 @@
     g_ln1_scale = jnp.sum(grad_normed * hat_one, axis=0)
     g_ln1_shift = jnp.sum(grad_normed, axis=0)
     grad_input = grad_middle + norm_back(grad_normed, hat_one, scale_one, gain_one)
-    grad_tokens = give_back(to_half(grad_input))
 
     vectors = [
         g_ln1_scale,
@@ -909,21 +1110,24 @@
         g_ln2_shift,
         g_b_down,
     ]
-    wide = jnp.concatenate([g_taps, g_coef, g_rate] + [v[None] for v in vectors])
-    wide = jnp.swapaxes(wide.reshape(tops, shard_count, owned), 0, 1)
+    wide = jnp.concatenate([v[None] for v in vectors])
+    wide = jnp.swapaxes(wide.reshape(10, shard_count, owned), 0, 1)
     wide = jnp.concatenate([wide, g_b_up.reshape(shard_count, -1, owned)], axis=1)
     wide = to_half(jnp.pad(wide, ((0, 0), (0, -wide.shape[1] % rep_count), (0, 0))))
     ups = b_up.shape[0] // owned
-    grad_w_down, grad_w_up, squares, mine = reduce_grads(
+    grad_tokens, grad_w_down, grad_w_up, squares, mine, ssm = reduce_all(
+        arrival,
+        own_target,
+        to_half(grad_input),
+        [coef_rows, rate_rows, grad_kernel, g_taps],
         part_down,
         part_up,
         [part_out, part_query, part_value, part_key],
         wide,
-        rep_count,
-        shard_count,
+        counts,
     )
     grad_w_out, grad_w_query, grad_w_value, grad_w_key = squares
-    vec = [mine[3 * taps + i] for i in range(10)]
+    vec = [mine[i] for i in range(10)]
     return (
         block_output,
         grad_tokens,
@@ -935,16 +1139,16 @@
         vec[3],
         grad_w_value,
         vec[4],
-        mine[:taps].T,
-        mine[taps : 2 * taps].T,
-        mine[2 * taps : 3 * taps].T,
+        ssm[:, :taps],
+        ssm[:, taps : 2 * taps],
+        ssm[:, 2 * taps :],
         vec[5],
         grad_w_out,
         vec[6],
         vec[7],
         vec[8],
         grad_w_up,
-        mine[tops : tops + ups].reshape(-1),
+        mine[10 : 10 + ups].reshape(-1),
         grad_w_down,
         vec[9],
     )

time: 525 us -> 442 us (0.84)
  Pallas kernels: 281 us -> 236 us
  starting transfers between devices: 24.6 us -> 4.22 us
  matrix products: 97.5 us -> 82.4 us
    pallas_call x4 -> x2, Pallas kernels: 281 us -> 236 us  [the longest x1 124 us: gather_all(): pl.pallas_call(lambda *refs: gather_body(rep_count, shard_count, units, s...]
    all_to_all x2 -> x0, starting transfers between devices: 12.6 us -> none  [deal(): lax.all_to_all(pieces, ('rep', 'shard'), split_axis=0, concat_axis=0, til...]
    dot_general x2 -> x0, matrix products: 10.4 us -> none  [filter(): wave = jnp.dot(self.exact, rows, precision=lax.Precision.HIGH)]
    concatenate x16 -> x12, local copies, waits for them, and re-layouts: 6.41 us -> 15.7 us  [the longest x11 14.5 us: local(): wide = jnp.concatenate([v[None] for v in vectors])]
    all_to_all x2 -> x1, starting transfers between devices: 12 us -> 4.22 us  [give_back(): lax.all_to_all(pieces, ('rep', 'shard'), split_axis=0, concat_axis=0, til...]
    gather x4 -> x0, local copies, waits for them, and re-layouts: 7.46 us -> none  [the longest x2 4.51 us: deal(): return came[unpacking].reshape(rows, width)]
    reshape x10, local copies, waits for them, and re-layouts: 0.05 us -> 6.58 us  [local(): vector.reshape(1, owned)]
    dot_general x14, matrix products: 35.6 us -> 30 us  [dot_tn(): lax.dot_general(one, two, (((0,), (0,)), ((), ())), preferred_element_typ...]
  transfers between devices with their start and end apart: 4 -> 1, of which waited for: 0 -> 0; matrix products, arithmetic and copies ran while one was open for 24% -> 25% of each run, Pallas kernels for 54% -> 26%
where the time goes in v2:
time: 442 us; the launch traced here: 435 us
  Pallas kernels  236 us (53%)
  matrix products  82.4 us (19%)
  local copies, waits for them, and re-layouts  78.3 us (18%)
  other arithmetic  31.7 us (7%)
    pallas_call x1, Pallas kernels, gather_all(): pl.pallas_call(lambda *refs: gather_body(rep_count, shard_count, units, s...  124 us
    pallas_call x1, Pallas kernels, reduce_all(): pl.pallas_call(lambda *refs: reduce_body(rep_count, shard_count, units, l...  112 us
    unnamed x150, local copies, waits for them, and re-layouts  34.3 us
    dot_general x14, matrix products, dot_tn(): lax.dot_general(one, two, (((0,), (0,)), ((), ())), preferred_element_typ...  30 us
    dot_general x9, matrix products, dot_nn(): return jnp.dot(one, two, preferred_element_type=jnp.float32).astype(out)  29.7 us
    dot_general x6, matrix products, dot_nt(): lax.dot_general(one, two, (((1,), (1,)), ((), ())), preferred_element_typ...  22.8 us
    concatenate x11, local copies, waits for them, and re-layouts, local(): wide = jnp.concatenate([v[None] for v in vectors])  14.5 us
    convert_element_type x4, other arithmetic, to_half(): return array.astype(jnp.bfloat16)  10.1 us
  transfers between devices with their start and end apart: 1, of which 0 were waited for; matrix products, arithmetic and copies ran while one was open for 25% of the time, Pallas kernels for 26%

profile of v2, /device:TPU:1, one launch (start us, length us, event | category | flops | bytes accessed | tf_op | source)
XLA Modules:
  0.0 434.7 jit_solution(10439229136885274027)
XLA Ops:
  2.3 1.3 fusion.85
  10.9 1.5 copy.67.refs_11_
  12.4 1.5 copy.68.refs_12_
  13.9 1.5 copy.69.refs_13_
  18.7 123.7 %gather_all.1 = (bf16[4,8,24,768]{3,2,1,0:T(8,128)(2,1)}, bf16[4,8,24,768]{3,2,1,0:T(8,128)(2,1)}, bf16[4,8,24,768]{3,2,1,0:T(8,128)(2,1)}, bf16[4,8,24,768]{3,2...) custom-call(s32[32]{0:T(128)} %get-tuple-element.145.refs_0_, ...), custom_call_target="tpu_custom_call" | custom-call | bytes 200000000 | tf_op jit(solution)/shard_map/gather_all/pallas_call | solution.py:476
  145.0 1.3 convert_reduce_fusion
  147.2 3.5 convolution_add_fusion
  150.7 4.6 %fusion.49 = f32[1024,768]{1,0:T(8,128)} fusion(bf16[1024,512]{1,0:T(8,128)(2,1)S(1)} %copy-done, bf16[512,768]{1,0:T(8,128)(2,1)S(1)} %bitcast.168, bf16[768,768]{1,0:T(8,128)(2,1)} %bitcast.219, f32[768]{0:T(1024)S(1)} %add.278), kind=kOutput, calls=%fused_computation.92 | convolution fusion | flops 1410072576 | bytes 6163456 | tf_op jit(solution)/shard_map/dot_general | solution.py:22
  155.4 3.4 subtract_convert_fusion.3
  158.8 2.2 fusion.108
  161.0 2.7 fusion.61
  164.1 3.4 subtract_convert_fusion.2
  172.8 5.7 %fusion.100 = f32[512,3072]{1,0:T(8,128)S(1)} fusion(bf16[768,3072]{1,0:T(8,128)(2,1)} %bitcast.213, f32[512,768]{1,0:T(8,128)} %copy-done.13, f32[768]{0:T(1024)S(1)} %add.292, f32[768]{0:T(1024)S(1)} %mul.343, f32[512]{0:T(512)S(1)} %add_rsqrt_fusion.1, f32[512]{0:T(512)S(1)} %broadcast_multiply_fusion.5), kind=kOutput, calls=%fused_computation.224 | convolution fusion | flops 2417885184 | bytes 12593152 | tf_op jit(solution)/shard_map/dot_general | solution.py:22
  178.6 9.5 %add_convert_fusion.2 = bf16[512,768]{1,0:T(8,128)(2,1)} fusion(f32[512,768]{1,0:T(8,128)S(1)} %copy-done.14, bf16[3072,768]{1,0:T(8,128)(2,1)} %bitcast.215, f32[768]{0:T(1024)S(1)} %add.299, f32[512,3072]{1,0:T(8,128)S(1)} %fusion.100, f32[3072]{0:T(1024)S(1)} %reshape.692), kind=kOutput, calls=%fused_computation.70 | convolution fusion | flops 2432827392 | bytes 13384704 | tf_op jit(solution)/shard_map/dot_general | solution.py:22
  188.0 2.6 gather_fusion
  190.6 4.2 all-to-all-start
  195.1 9.6 %fusion.110 = (bf16[3072]{0:T(1024)(128)(2,1)}, bf16[512,3072]{1,0:T(8,128)(2,1)S(1)}) fusion(f32[512,3072]{1,0:T(8,128)} %copy-done.61, f32[3072]{0:T(1024)S(1)} %reshape.692, bf16[512,768]{1,0:T(8,128)(2,1)} %bitcast.170, bf16[3072,768]{1,0:T(8,128)(2,1)} %bitcast.216), kind=kOutput, calls=%fused_computation.234 | convolution fusion | flops 2448946176 | bytes 14960640 | tf_op jit(solution)/shard_map/dot_general | solution.py:32
  204.7 7.1 %multiply_reduce_fusion = (bf16[768]{0:T(1024)(128)(2,1)}, f32[512]{0:T(512)S(1)}, f32[512]{0:T(512)S(1)}, bf16[768]{0:T(1024)(128)(2,1)}, f32[512,768]{1,0:T(8,128)S(1)}) fusion(f32[512,768]{1,0:T(8,128)S(1)} %copy-done.15, f32[512]{0:T(512)S(1)} %add_rsqrt_fusion.1, f32[512]{0:T(512)S(1)} %broadcast_multiply_fusion.5, f32[768]{0:T(1024)S(1)} %mul.343, ...), kind=kOutput, calls=%fused_computation.53 | convolution fusion | flops 2419455488 | bytes 11024384 | tf_op jit(solution)/shard_map/dot_general | solution.py:32
  213.7 1.4 fusion.102
  222.2 1.8 fusion.101
  231.4 9.1 %convolution_convert_fusion.1 = bf16[3072,768]{1,0:T(8,128)(2,1)} fusion(bf16[512,768]{1,0:T(8,128)(2,1)S(1)} %bitcast.171, f32[512,3072]{1,0:T(8,128)} %copy-done.61, f32[3072]{0:T(1024)S(1)} %reshape.692), kind=kOutput, calls=%fused_computation.13 | convolution fusion | flops 2434007040 | bytes 11808768 | tf_op jit(solution)/shard_map/dot_general | solution.py:26
  240.4 1.8 convolution_convert_fusion.5
  243.1 1.6 fusion.111
  246.0 3.0 fusion.41
  249.0 1.9 convolution_convert_fusion.4
  250.9 1.8 convolution_convert_fusion.3
  252.7 1.8 convolution_convert_fusion.2
  257.3 1.4 copy-done.27
  259.4 1.9 reduce_sum.271
  263.4 1.4 reshape.679
  264.8 1.3 copy.70
  266.1 1.3 concatenate.86
  268.7 1.3 concatenate.87
  270.0 1.3 concatenate.88
  271.4 1.3 concatenate.89
  272.7 1.3 concatenate.90
  274.0 1.3 concatenate.91
  275.3 1.3 concatenate.92
  276.6 1.4 concatenate.93
  278.0 1.3 concatenate.94
  279.3 1.9 reduce.7
  281.2 1.3 concatenate.95
  295.2 3.0 fusion.38
  300.8 4.8 %convolution_convert_fusion = bf16[768,3072]{1,0:T(8,128)(2,1)} fusion(bf16[512,3072]{1,0:T(8,128)(2,1)S(1)} %copy-done.63, f32[512,768]{1,0:T(8,128)S(1)} %copy-done.16, f32[768]{0:T(1024)S(1)} %copy-done.58, f32[768]{0:T(1024)S(1)} %copy-done.48, f32[512]{0:T(512)S(1)} %copy-done.52, f32[512]{0:T(512)S(1)} %copy-done.46), kind=kOutput, calls=%fused_computation.12 | convolution fusion | flops 2420244480 | bytes 9447424 | tf_op jit(solution)/shard_map/dot_general | solution.py:26
  305.6 111.9 %reduce_all.1 = (f32[8,4,24,768]{3,2,1,0:T(8,128)}, f32[8,24,3072]{2,1,0:T(8,128)}, f32[8,24,768]{2,1,0:T(8,128)}, f32[8,24,768]{2,1,0:T(8,128)}, f32[8,24,768]{...) custom-call(s32[32]{0:T(128)} %copy-done.56, ...), custom_call_target="tpu_custom_call" | custom-call | bytes 200000000 | tf_op jit(solution)/shard_map/reduce_all/pallas_call | solution.py:816
  423.5 2.7 gather_fusion.1
  430.4 1.4 copy.100
  432.9 1.4 copy.101
  (235 shorter events, 72.4 us)
Async XLA Ops:
  15.5 3.2 copy-start.54
  142.4 3.9 copy-start.6
  145.0 100.6 %copy-start.44 = (f32[768]{0:T(1024)}, f32[768]{0:T(1024)S(1)}, u32[]{:S(2)}) copy-start(f32[768]{0:T(1024)S(1)} %mul.324) | copy-start | bytes 9220
  147.2 3.5 copy-start.21
  147.2 3.5 copy-start
  155.4 3.4 copy-start.11
  161.0 6.5 %copy-start.4 = (f32[512,768]{1,0:T(8,128)}, f32[512,768]{1,0:T(8,128)S(1)}, u32[]{:S(2)}) copy-start(f32[512,768]{1,0:T(8,128)S(1)} %get-tuple-element.130) | copy-start | bytes 4718596
  164.0 8.8 %copy-start.57 = (f32[768]{0:T(1024)}, f32[768]{0:T(1024)S(1)}, u32[]{:S(2)}) copy-start(f32[768]{0:T(1024)S(1)} %add.292) | copy-start | bytes 9220
  164.1 47.8 %copy-start.47 = (f32[768]{0:T(1024)}, f32[768]{0:T(1024)S(1)}, u32[]{:S(2)}) copy-start(f32[768]{0:T(1024)S(1)} %mul.343) | copy-start | bytes 9220
  171.3 40.6 %copy-start.45 = (f32[512]{0:T(512)}, f32[512]{0:T(512)S(1)}, u32[]{:S(2)}) copy-start(f32[512]{0:T(512)S(1)} %broadcast_multiply_fusion.5) | copy-start | bytes 6148
  172.7 39.2 %copy-start.51 = (f32[512]{0:T(512)}, f32[512]{0:T(512)S(1)}, u32[]{:S(2)}) copy-start(f32[512]{0:T(512)S(1)} %add_rsqrt_fusion.1) | copy-start | bytes 6148
  172.8 5.7 %copy-start.14 = (f32[512,768]{1,0:T(8,128)S(1)}, f32[512,768]{1,0:T(8,128)}, u32[]{:S(2)}) copy-start(f32[512,768]{1,0:T(8,128)} %copy-done.13) | copy-start | bytes 4718596
  178.5 9.5 %copy-start.61 = (f32[512,3072]{1,0:T(8,128)}, f32[512,3072]{1,0:T(8,128)S(1)}, u32[]{:S(2)}) copy-start(f32[512,3072]{1,0:T(8,128)S(1)} %fusion.100) | copy-start | bytes 18874372
  190.6 232.9 %all-to-all-start = ((bf16[32,16,768]{2,1,0:T(8,128)(2,1)}), bf16[32,16,768]{2,1,0:T(8,128)(2,1)}, u32[]{:S(2)}, u32[]{:S(2)}) async-start(bf16[32,16,768]{2,1,0:T(8,128)(2,1)} %gather_fusion), calls=%async_computation | async-start | bytes 1572864 | tf_op jit(solution)/shard_map/all_to_all | solution.py:971
  195.0 50.6 %copy-start.49 = (f32[512]{0:T(512)}, f32[512]{0:T(512)S(1)}, u32[]{:S(2)}) copy-start(f32[512]{0:T(512)S(1)} %div.105) | copy-start | bytes 6148
  195.0 50.5 %copy-start.50 = (f32[512]{0:T(512)}, f32[512]{0:T(512)S(1)}, u32[]{:S(2)}) copy-start(f32[512]{0:T(512)S(1)} %rsqrt.22) | copy-start | bytes 6148
  195.1 9.6 %copy-start.15 = (f32[512,768]{1,0:T(8,128)S(1)}, f32[512,768]{1,0:T(8,128)}, u32[]{:S(2)}) copy-start(f32[512,768]{1,0:T(8,128)} %copy-done.13) | copy-start | bytes 4718596
  204.7 7.1 %copy-start.62 = (bf16[512,3072]{1,0:T(8,128)(2,1)}, bf16[512,3072]{1,0:T(8,128)(2,1)S(1)}, u32[]{:S(2)}) copy-start(bf16[512,3072]{1,0:T(8,128)(2,1)S(1)} %get-tuple-element.141) | copy-start | bytes 9437188
  204.7 7.2 %copy-start.24 = (bf16[32,16,768]{2,1,0:T(8,128)(2,1)S(1)}, bf16[32,16,768]{2,1,0:T(8,128)(2,1)}, u32[]{:S(2)}) copy-start(bf16[32,16,768]{2,1,0:T(8,128)(2,1)} %get-tuple-element.56) | copy-start | bytes 2359300
  213.2 27.2 %copy-start.2 = (f32[512,768]{1,0:T(8,128)}, f32[512,768]{1,0:T(8,128)S(1)}, u32[]{:S(2)}) copy-start(f32[512,768]{1,0:T(8,128)S(1)} %get-tuple-element.89) | copy-start | bytes 4718596
  215.1 2.9 copy-start.8
  215.1 2.9 copy-start.53
  219.9 2.3 copy-start.10
  224.1 1.9 copy-start.7
  224.1 2.8 copy-start.9
  231.4 9.1 %copy-start.20 = (bf16[512,768]{1,0:T(8,128)(2,1)S(1)}, bf16[512,768]{1,0:T(8,128)(2,1)}, u32[]{:S(2)}) copy-start(bf16[512,768]{1,0:T(8,128)(2,1)} %copy-done.19) | copy-start | bytes 2359300
  257.3 40.9 %copy-start.23 = (f32[320,768]{1,0:T(8,128)}, f32[320,768]{1,0:T(8,128)S(1)}, u32[]{:S(2)}) copy-start(f32[320,768]{1,0:T(8,128)S(1)} %fusion.50) | copy-start | bytes 2949124
  259.4 35.8 %copy-start.3 = (f32[512,768]{1,0:T(8,128)S(1)}, f32[512,768]{1,0:T(8,128)}, u32[]{:S(2)}) copy-start(f32[512,768]{1,0:T(8,128)} %copy-done.2) | copy-start | bytes 4718596
  295.1 3.1 copy-start.39
  295.1 3.1 copy-start.40
  295.1 3.1 copy-start.41
  295.1 3.3 copy-start.37
  295.1 3.3 copy-start.38
  295.2 3.3 copy-start.42
  295.2 3.3 copy-start.43
  295.2 5.6 %copy-start.63 = (bf16[512,3072]{1,0:T(8,128)(2,1)S(1)}, bf16[512,3072]{1,0:T(8,128)(2,1)}, u32[]{:S(2)}) copy-start(bf16[512,3072]{1,0:T(8,128)(2,1)} %copy-done.62) | copy-start | bytes 9437188
  298.8 2.0 copy-start.16
  298.8 1.9 copy-start.46
  298.8 1.9 copy-start.48
  298.8 1.9 copy-start.52
  298.8 1.9 copy-start.58
  305.6 117.3 %copy-start.55 = (s32[32]{0:T(128)S(1)}, s32[32]{0:T(128)}, u32[]{:S(2)}) copy-start(s32[32]{0:T(128)} %copy-done.54) | copy-start | bytes 388
  417.5 8.7 %copy-start.32 = (bf16[32,16,768]{2,1,0:T(8,128)(2,1)S(1)}, bf16[32,16,768]{2,1,0:T(8,128)(2,1)}, u32[]{:S(2)}) copy-start(bf16[32,16,768]{2,1,0:T(8,128)(2,1)} %get-tuple-element.59) | copy-start | bytes 2359300
  423.5 3.6 copy-start.36
  426.2 2.5 copy-start.34
  427.1 2.5 copy-start.33
  427.9 2.5 copy-start.26
  430.4 2.5 copy-start.25
  (18 other events, 27.7 us)

commit v3 on v2

--- a/solution.py
+++ b/solution.py
@@ -256,11 +256,11 @@
     locals_, pack, params = refs[4 : 4 + tensors], refs[4 + tensors], refs[5 + tensors : 8 + tensors]
     rest = refs[8 + tensors :]
     outs, pack_out = rest[:tensors], rest[tensors]
-    tokens_out, cotangent_out, kernel_wave, taps_wave, waves, coef_ref, rate_ref = rest[
-        tensors + 1 : tensors + 8
+    tokens_out, cotangent_out, kernel_wave, taps_wave, waves, waves_t, coef_ref, rate_ref = rest[
+        tensors + 1 : tensors + 9
     ]
-    (held, table, kernel, params_in, staged, landed) = rest[tensors + 8 : tensors + 14]
-    send, receive, small_send, small_receive, done, deal_send, deal_receive = rest[tensors + 14 :]
+    (held, table, kernel, params_in, staged, landed) = rest[tensors + 9 : tensors + 15]
+    send, receive, small_send, small_receive, done, deal_send, deal_receive = rest[tensors + 15 :]
     place = Place(rep_count, shard_count)
     place.meet_all()
     me, shard = place.rep, place.shard
@@ -351,6 +351,7 @@
                 at = length + i * taps
                 table[base + at : base + at + taps, at : at + taps] = short
         waves[...] = to_half(table[...])
+        waves_t[...] = to_half(table[...].T)
 
     def arrive():
         for copy in small + own:
@@ -376,7 +377,7 @@
                 top = dot_fine(left, right)
             else:
                 top = dot_nn(left[0], right[0]) + dot_nn(left[1], right[0])
-            out[base : base + length, :] = top * (1.0 / length)
+            out[base : base + length, :] = to_half(top * (1.0 / length))
             left = split_half(table[base + length : base + length + taps, length : length + taps])
             head = [part[:taps] if part is not None else None for part in right]
             if fine:
@@ -385,7 +386,7 @@
                 low = dot_nn(left[0], head[0]) + dot_nn(left[1], head[0])
             for i in range(shorts):
                 at = base + length + i * taps
-                out[at : at + taps, :] = low * (1.0 / taps)
+                out[at : at + taps, :] = to_half(low * (1.0 / taps))
 
     jobs.append(tables)
     jobs.append(arrive)
@@ -468,10 +469,11 @@
     length = half - shorts * taps
     piece_shape = (slots, half // slots, width)
     outs = [jax.ShapeDtypeStruct((shard_count,) + w.shape, w.dtype) for w in locals_ + [pack]]
-    spaces = [anywhere] * len(outs) + [here] * 7
+    spaces = [anywhere] * len(outs) + [here] * 8
     outs += [jax.ShapeDtypeStruct(piece_shape, tokens.dtype)] * 2
-    outs += [jax.ShapeDtypeStruct((2 * half, channels), jnp.float32)] * 2
+    outs += [jax.ShapeDtypeStruct((2 * half, channels), jnp.bfloat16)] * 2
     outs += [jax.ShapeDtypeStruct((2 * half, half), jnp.bfloat16)]
+    outs += [jax.ShapeDtypeStruct((half, 2 * half), jnp.bfloat16)]
     outs += [jax.ShapeDtypeStruct((taps, channels), jnp.float32)] * 2
     found = pl.pallas_call(
         lambda *refs: gather_body(rep_count, shard_count, units, shorts, *refs),
@@ -528,10 +530,13 @@
     def start(self):
         place = self.place
         core = place.bit(1)
-        self.kept = pltpu.make_async_copy(
-            self.source.at[:, :, core], self.half, self.sems[2].at[self.base]
-        )
-        self.kept.start()
+        if self.half is None:
+            self.half = self.source.at[:, :, core]
+        else:
+            self.kept = pltpu.make_async_copy(
+                self.source.at[:, :, core], self.half, self.sems[2].at[self.base]
+            )
+            self.kept.start()
         self.fly(self.source.at[:, :, 1 - core], self.came[0], 0, place.by_rep(1))
 
     def fly(self, source, target, index, device):
@@ -547,7 +552,8 @@
         todo = []
 
         def after_core():
-            self.kept.wait()
+            if self.kept is not None:
+                self.kept.wait()
             self.flight.wait_recv()
             half, came = self.half, self.came[0]
 
@@ -633,7 +639,7 @@
                 total = total + to_float(self.came[1 + count][k - 1])
             self.back[0] = to_half(total)
             double(0)
-            self.write(place.rep, self.back[0])
+            self.write(place.rep, self.back.at[0])
 
         def double(stage):
             masks = self.masks + [1]
@@ -652,7 +658,7 @@
             if stage < count:
                 double(stage + 1)
             for m in range(size, 2 * size):
-                self.write(lax.bitwise_xor(place.rep, offset_of(m, masks)), self.back[m])
+                self.write(lax.bitwise_xor(place.rep, offset_of(m, masks)), self.back.at[m])
 
         todo.append(after_core)
         for stage in range(count):
@@ -676,42 +682,216 @@
 REDUCE_LAG = 2
 
 
-def reduce_body(rep_count, shard_count, units, tensors, kinds_count, *refs):
+def loads_of(pairs, sems):
+    copies = []
+    for i, (source, target) in enumerate(pairs):
+        copy = pltpu.make_async_copy(source, target, sems.at[i])
+        copy.start()
+        copies.append(copy)
+    return copies
+
+
+VECTORS = 16
+
+
+def sum_everywhere(place, totals, came, sems, base):
+    devices, mask = [], 1
+    while mask < place.rep_count:
+        devices.append(place.by_rep(mask))
+        mask *= 2
+    mask = 1
+    while mask < place.shard_count:
+        devices.append(place.by_shard(mask))
+        mask *= 2
+    flights = []
+
+    def send(stage):
+        copy = remote(totals.at[stage], came.at[stage], sems, base + stage, devices[stage])
+        copy.start()
+        flights.append(copy)
+
+    def step(stage):
+        if stage:
+            flights[-1].wait_recv()
+            totals[stage] = totals[stage - 1] + came[stage - 1]
+        if stage < len(devices):
+            send(stage)
+
+    def finish():
+        for copy in flights:
+            copy.wait_send()
+
+    return [lambda stage=stage: step(stage) for stage in range(len(devices) + 1)], finish
+
+
+def reduce_body(rep_count, shard_count, units, tensors, shorts, *refs):
     planes = len(plane_masks(rep_count, 0))
-    order, unpack, grads, coef_ref, rate_ref, kernel_grad, taps_grad = refs[:7]
-    sources = list(refs[7 : 6 + tensors])
-    outs = refs[6 + tensors : 6 + 2 * tensors]
-    grads_out = refs[6 + 2 * tensors]
-    rest = refs[7 + 2 * tensors :]
+    order, unpack, vectors, wide_vector, coef_ref, rate_ref, skip_ref, gain_ref, output = refs[:9]
+    stored, streams, rest = refs[9:18], refs[18:26], refs[26:]
+    sources, rest = list(rest[:3]), rest[3:]
+    outs, rest = rest[:tensors], rest[tensors:]
+    grads_out, output_out, vectors_out, wide_out = rest[:4]
+    rest = rest[4:]
+    held, flows, rest = rest[:9], rest[9:17], rest[17:]
     per_kind = planes + 4
-    kinds = [rest[i * per_kind : (i + 1) * per_kind] for i in range(kinds_count)]
-    rest = rest[kinds_count * per_kind :]
-    made, flat, coef_grad, rate_grad, staged, landed = rest[:6]
-    send, receive, kept, deal_send, deal_receive = rest[6:]
-    sources.append(made)
+    kinds = [rest[:per_kind], (None,) + rest[per_kind : 2 * per_kind - 1]]
+    kinds.append((None,) + rest[2 * per_kind - 1 : 3 * per_kind - 2])
+    rest = rest[3 * per_kind - 2 :]
+    (made, ssm_made, flat, coef_grad, rate_grad, kernel_grad, taps_grad) = rest[:7]
+    (grad_q, grad_k, grad_v, grad_b, grads, totals, came_totals, wide, came_wide) = rest[7:16]
+    staged, landed, landed_two = rest[16:19]
+    send, receive, kept, load_sems, wrote, deal_one, deal_two, sums, flow_sems = rest[19:]
+    for i in range(3):
+        sources.append(made.at[i])
+    sources.append(ssm_made)
     place = Place(rep_count, shard_count)
     place.meet_all()
     count = flights_of(rep_count, shard_count)
     works = []
-    for index, (tensor, pick, writer, kind, slot) in enumerate(units):
+
+    def writer(tensor, pick):
+        def write(piece, value):
+            pltpu.make_async_copy(
+                value, pick(outs[tensor].at[piece]), wrote.at[tensor]
+            ).start()
+
+        return write
+
+    for index, (tensor, pick, target, kind, slot) in enumerate(units):
         bufs = kinds[kind]
-        came = [buf.at[slot] for buf in bufs[1 : 1 + planes + 2]]
         works.append(
             Reduction(
                 place,
                 index % 2,
                 pick(sources[tensor]),
-                bufs[0].at[slot],
-                came,
+                None if bufs[0] is None else bufs[0].at[slot],
+                [buf.at[slot] for buf in bufs[1 : 1 + planes + 2]],
                 bufs[-1].at[slot],
                 (send, receive, kept),
                 index * count,
-                lambda piece, value, tensor=tensor, writer=writer: writer(
-                    outs[tensor], piece, to_float(value)
-                ),
+                writer(tensor, target),
             )
         )
-    taps, channels = taps_grad.shape
+    todo = [work.steps() for work in works]
+    started = [0]
+
+    def start_to(limit):
+        while started[0] < min(limit, len(works)):
+            works[started[0]].start()
+            started[0] += 1
+
+    start_to(REDUCE_AHEAD)
+    loads = loads_of(zip(stored, held), load_sems)
+    middle, tokens, normed, table, table_t, w_out = held[:6]
+    w_qkv = held[6:9]
+    tile = flows[0].shape[2]
+
+    def flow(index):
+        lanes = pl.ds(index * tile, tile)
+        return loads_of(
+            [(a.at[:, lanes], b.at[index % 2]) for a, b in zip(streams, flows)],
+            flow_sems.at[index],
+        )
+
+    flowing = [flow(0), flow(1)]
+    deal_start(
+        (output,), order, staged, landed, (deal_one.at[0], deal_one.at[1]), place
+    )
+
+    rows, channels = middle.shape
+    taps = taps_grad.shape[0]
+    length = rows - shorts * taps
+    totals[0] = vectors[...]
+    wide[0] = wide_vector[...]
+
+    def arrive():
+        for copy in loads:
+            copy.wait()
+        grad_b[...] = to_half(middle[...])
+        totals[0, 6:7, :] = column_sums(grad_b[...])
+
+    def store_grad(index, left, right):
+        parts = shard_count // 2
+        wide_rows = channels // 2
+        for i in range(2):
+            part = dot_tn(left[:, i * wide_rows : (i + 1) * wide_rows], right[...], jnp.bfloat16)
+            made[index, i * parts : (i + 1) * parts] = part.reshape(
+                (parts,) + made.shape[2:]
+            )
+
+    def lags_of(real, imag, out, lags, lanes):
+        top_re, top_im = to_half(real[:length] * (1.0 / length)), to_half(imag[:length] * (1.0 / length))
+        low_re, low_im = real[length : length + taps], imag[length : length + taps]
+        for i in range(1, shorts):
+            at = length + i * taps
+            low_re, low_im = low_re + real[at : at + taps], low_im + imag[at : at + taps]
+        low_re, low_im = to_half(low_re * (1.0 / taps)), to_half(low_im * (1.0 / taps))
+        total = dot_nn(table_t[0:lags, 0:length], top_re)
+        total = total + dot_nn(table_t[0:lags, rows : rows + length], top_im)
+        at = slice(length, length + taps)
+        head = dot_nn(table_t[at, at], low_re)
+        head = head + dot_nn(table_t[at, rows + length : rows + length + taps], low_im)
+        out[0:taps, lanes] = total[:taps] + head
+        if lags > taps:
+            out[taps:lags, lanes] = total[taps:]
+
+    def mix_job(index):
+        lanes = slice(index * tile, (index + 1) * tile)
+        for copy in flowing[index]:
+            copy.wait()
+        queries, values, shifted, mixed, in_wave, key_wave, kernel_wave, taps_wave = [
+            ref.at[index % 2] for ref in flows
+        ]
+        gate = dot_nt(grad_b[...], w_out[lanes, :])
+        grad_q[:, lanes] = to_half(gate * to_float(mixed[...]))
+        grad = gate * to_float(queries[...])
+        wave = dot_nn(table[...], to_half(grad))
+        g_re, g_im = wave[:rows], wave[rows:]
+        k_re, k_im = to_float(kernel_wave[:rows]), to_float(kernel_wave[rows:])
+        back = dot_nn(table_t[:, :rows], to_half(g_re * k_re + g_im * k_im))
+        back = back + dot_nn(table_t[:, rows:], to_half(g_im * k_re - g_re * k_im))
+        back = back + skip_ref[:, lanes] * grad
+        value, moved = to_float(values[...]), to_float(shifted[...])
+        totals[0, 5:6, lanes] = jnp.sum(grad * (value * moved), axis=0, keepdims=True)
+        u_re, u_im = to_float(in_wave[:rows]), to_float(in_wave[rows:])
+        lags_of(g_re * u_re + g_im * u_im, g_im * u_re - g_re * u_im, kernel_grad, length, lanes)
+        grad_v[:, lanes] = to_half(back * moved)
+        wave = dot_nn(table[...], to_half(back * value))
+        s_re, s_im = wave[:rows], wave[rows:]
+        t_re, t_im = to_float(taps_wave[:rows]), to_float(taps_wave[rows:])
+        back = dot_nn(table_t[:, :rows], to_half(s_re * t_re + s_im * t_im))
+        back = back + dot_nn(table_t[:, rows:], to_half(s_im * t_re - s_re * t_im))
+        grad_k[:, lanes] = to_half(back)
+        x_re, x_im = to_float(key_wave[:rows]), to_float(key_wave[rows:])
+        lags_of(s_re * x_re + s_im * x_im, s_im * x_re - s_re * x_im, taps_grad, taps, lanes)
+        if (index + 2) * tile < channels:
+            flowing.append(flow(index + 2))
+
+    def column_sums(array):
+        return jnp.sum(to_float(array), axis=0, keepdims=True)
+
+    def bias_job():
+        totals[0, 2:3, :] = column_sums(grad_q[...])
+        totals[0, 3:4, :] = column_sums(grad_k[...])
+        totals[0, 4:5, :] = column_sums(grad_v[...])
+
+    piece_rows = grads.shape[1]
+
+    def norm_job(tile):
+        size = 128
+        at = slice(tile * size, tile * size + size)
+        error = dot_nt(grad_q[at, :], w_qkv[0][...]) + dot_nt(grad_k[at, :], w_qkv[1][...])
+        error = error + dot_nt(grad_v[at, :], w_qkv[2][...])
+        hat, scale = row_stats(to_float(tokens[at, :]))
+        first = jnp.sum(error * hat, axis=0, keepdims=True)
+        second = jnp.sum(error, axis=0, keepdims=True)
+        if tile:
+            first, second = first + totals[0, 0:1, :], second + totals[0, 1:2, :]
+        totals[0, 0:1, :] = first
+        totals[0, 1:2, :] = second
+        grad = to_half(middle[at, :] + norm_back(error, hat, scale, gain_ref[...]))
+        count = size // piece_rows
+        grads[tile * count : (tile + 1) * count] = grad.reshape(count, piece_rows, channels)
 
     def ssm_job(tile):
         lanes = slice(tile * 128, tile * 128 + 128)
@@ -723,85 +903,132 @@
     def fill_job():
         piece = channels // (shard_count * rep_count)
         for i in range(shard_count * rep_count):
-            made[i // rep_count, (i % rep_count) // 2, i % 2] = to_half(
+            ssm_made[i // rep_count, (i % rep_count) // 2, i % 2] = to_half(
                 flat[i * piece : (i + 1) * piece, :]
             )
 
-    jobs = [lambda tile=tile: ssm_job(tile) for tile in range(channels // 128)] + [fill_job]
-    todo = [work.steps() for work in works]
-    for work in works[:REDUCE_AHEAD]:
-        work.start()
-    deal_start((grads,), order, staged, landed, (deal_send, deal_receive), place)
-    length = len(todo[0])
-    for step in range(len(works) + (length - 1) * REDUCE_LAG):
+    def deal_job():
+        deal_end(
+            (output_out,), unpack, staged, landed, (deal_one.at[0], deal_one.at[1]), place
+        )
+        deal_start(
+            (grads,), order, staged, landed_two, (deal_two.at[0], deal_two.at[1]), place
+        )
+
+    vector_steps, vector_end = sum_everywhere(place, totals, came_totals, (sums.at[0], sums.at[1]), 0)
+    wide_steps, wide_end = sum_everywhere(
+        place, wide, came_wide, (sums.at[0], sums.at[1]), len(vector_steps)
+    )
+    mixes = [lambda i=i: mix_job(i) for i in range(channels // tile)]
+    third = -(-len(mixes) // 3)
+    norms = [lambda i=i: norm_job(i) for i in range(rows // 128)]
+    ssms = [lambda i=i: ssm_job(i) for i in range(channels // 128)]
+    jobs = [
+        [arrive] + mixes[:third],
+        mixes[third : 2 * third],
+        mixes[2 * third :],
+        [
+            lambda: store_grad(0, normed, grad_q),
+            lambda: store_grad(1, normed, grad_v),
+            lambda: store_grad(2, normed, grad_k),
+            bias_job,
+        ],
+        norms[:2],
+        norms[2:] + [deal_job],
+        ssms[:2],
+        ssms[2:4],
+        ssms[4:] + [fill_job],
+    ]
+    for i, pair in enumerate(zip(vector_steps, wide_steps)):
+        while len(jobs) < 7 + i:
+            jobs.append([])
+        jobs[6 + i] = list(pair) + jobs[6 + i]
+    steps = len(todo[0])
+    for step in range(len(works) + (steps - 1) * REDUCE_LAG):
         if step < len(jobs):
-            jobs[step]()
-        for position in range(length - 1, -1, -1):
+            for job in jobs[step]:
+                job()
+        start_to(step + REDUCE_AHEAD + 1 if step < 8 else len(works))
+        for position in range(steps - 1, -1, -1):
             index = step - position * REDUCE_LAG
             if 0 <= index < len(works):
                 todo[index][position]()
-                if position == 0 and index + REDUCE_AHEAD < len(works):
-                    works[index + REDUCE_AHEAD].start()
-    deal_end((grads_out,), unpack, staged, landed, (deal_send, deal_receive), place)
+    deal_end(
+        (grads_out,), unpack, staged, landed_two, (deal_two.at[0], deal_two.at[1]), place
+    )
+    owned = channels // shard_count
+    last = len(vector_steps) - 1
+    total = totals[last]
+    narrow = jnp.zeros((VECTORS, owned), jnp.float32)
+    step_wide = wide.shape[2] // shard_count
+    total_wide = wide[last]
+    chosen = jnp.zeros((1, step_wide), jnp.float32)
+    for s in range(shard_count):
+        here = place.shard == s
+        turned = pltpu.roll(total, (channels - s * owned) % channels, axis=1) if s else total
+        narrow = narrow + jnp.where(here, turned[:, :owned], 0.0)
+        chosen = chosen + jnp.where(here, total_wide[:, s * step_wide : (s + 1) * step_wide], 0.0)
+    vectors_out[...] = narrow
+    wide_out[...] = chosen
+    vector_end()
+    wide_end()
     for work in works:
         work.finish()
-
-
-def reduce_all(order, unpack, grads, rows_in, down, up, squares, pack, counts):
+    for tensor in range(tensors):
+        pltpu.make_async_copy(outs[tensor], outs[tensor], wrote.at[tensor]).wait()
+
+
+def reduce_all(
+    order, unpack, vectors, wide, rows_in, output, stored, streams, down, up, square, counts, shorts
+):
     rep_count, shard_count = counts
     slots = rep_count * shard_count
-    width = squares[0].shape[1]
-    piece = squares[0].shape[0] // slots
+    rows, width = output.shape
+    piece = width // slots
     parts = up.shape[1] // width
     lead = (shard_count, rep_count // 2, 2)
     tensors = [down.reshape(lead + (parts, piece, width)), up.reshape(lead + (piece, up.shape[1]))]
-    tensors += [g.reshape(lead + (piece, width)) for g in squares]
-    pack_rows, pack_width = pack.shape[1] // rep_count, pack.shape[2]
-    tensors.append(pack.reshape(lead + (pack_rows, pack_width)))
+    tensors.append(square.reshape(lead + (piece, width)))
     states, channels = rows_in[0].shape
-    owned = channels // slots
-    outs = [jax.ShapeDtypeStruct((rep_count, parts, piece, width), jnp.float32)]
-    outs.append(jax.ShapeDtypeStruct((rep_count, piece, up.shape[1]), jnp.float32))
-    outs += [jax.ShapeDtypeStruct((rep_count, piece, width), jnp.float32)] * len(squares)
-    outs.append(jax.ShapeDtypeStruct((rep_count, pack_rows, pack_width), jnp.float32))
-    outs.append(jax.ShapeDtypeStruct((rep_count, owned, 3 * states), jnp.float32))
-    piece_shape = (slots, grads.shape[0] // slots, grads.shape[1])
-    outs.append(jax.ShapeDtypeStruct(piece_shape, grads.dtype))
-
-    def whole_writer(out, at, value):
-        out[at] = value
+    length = rows - shorts * states
+    outs = [jax.ShapeDtypeStruct((rep_count, parts, piece, width), jnp.bfloat16)]
+    outs.append(jax.ShapeDtypeStruct((rep_count, piece, up.shape[1]), jnp.bfloat16))
+    outs += [jax.ShapeDtypeStruct((rep_count, piece, width), jnp.bfloat16)] * 4
+    outs.append(jax.ShapeDtypeStruct((rep_count, piece, 3 * states), jnp.bfloat16))
+    plain_outs = len(outs)
+    piece_shape = (slots, rows // slots, width)
+    outs += [jax.ShapeDtypeStruct(piece_shape, output.dtype)] * 2
+    outs.append(jax.ShapeDtypeStruct((VECTORS, width // shard_count), jnp.float32))
+    outs.append(jax.ShapeDtypeStruct((1, wide.shape[1] // shard_count), jnp.float32))
+
+    def whole(ref):
+        return ref
 
     units = []
     for q in range(parts):
-
-        def part_writer(out, at, value, q=q):
-            out[at, q] = value
-
-        units.append((0, lambda ref, q=q: ref.at[:, :, :, q], part_writer, 0, len(units)))
+        units.append(
+            (0, lambda ref, q=q: ref.at[:, :, :, q], lambda ref, q=q: ref.at[q], 0, len(units))
+        )
     for q in range(parts):
-
-        def column_writer(out, at, value, q=q):
-            out[at, :, q * width : (q + 1) * width] = value
-
         units.append(
             (
                 1,
                 lambda ref, q=q: ref.at[:, :, :, :, pl.ds(q * width, width)],
-                column_writer,
+                lambda ref, q=q: ref.at[:, pl.ds(q * width, width)],
                 0,
                 len(units),
             )
         )
-    for i in range(len(squares)):
-        units.append((2 + i, lambda ref: ref, whole_writer, 0, len(units)))
+    units.append((2, whole, whole, 0, len(units)))
     plain = len(units)
-    units.append((2 + len(squares), lambda ref: ref, whole_writer, 1, 0))
-    units.append((3 + len(squares), lambda ref: ref, whole_writer, 2, 0))
+    for i in range(3):
+        units.append((3 + i, whole, whole, 1, i))
+    units.append((6, whole, whole, 2, 0))
     half = rep_count // 2
     planes = len(plane_masks(rep_count, 0))
 
-    def buffers(count, rows, columns):
-        shapes = [(shard_count, half), (shard_count, half)]
+    def buffers(count, rows, columns, kept):
+        shapes = [(shard_count, half)] * (2 if kept else 1)
         size = half
         for _ in range(planes):
             size //= 2
@@ -809,84 +1036,66 @@
         shapes += [(shard_count - 1,), (rep_count,)]
         return [pltpu.VMEM((count,) + shape + (rows, columns), jnp.bfloat16) for shape in shapes]
 
+    tile = 128 if piece % 8 else 256
     flights = len(units) * flights_of(rep_count, shard_count)
+    stages = slots.bit_length()
     anywhere = pl.BlockSpec(memory_space=pl.ANY)
     here = pl.BlockSpec(memory_space=pltpu.VMEM)
     scalars = pl.BlockSpec(memory_space=pltpu.SMEM)
     found = pl.pallas_call(
-        lambda *refs: reduce_body(rep_count, shard_count, units, len(tensors) + 1, 3, *refs),
-        in_specs=[scalars] * 2 + [here] * 5 + [anywhere] * len(tensors),
-        out_specs=[here] * len(outs),
+        lambda *refs: reduce_body(rep_count, shard_count, units, plain_outs, shorts, *refs),
+        in_specs=[scalars] * 2 + [here] * 7 + [anywhere] * (len(stored) + len(streams) + 3),
+        out_specs=[anywhere] * plain_outs + [here] * 4,
         out_shape=outs,
-        scratch_shapes=buffers(plain, piece, width)
-        + buffers(1, pack_rows, pack_width)
-        + buffers(1, owned, 3 * states)
+        scratch_shapes=[pltpu.VMEM(array.shape, array.dtype) for array in stored]
+        + [pltpu.VMEM((2, array.shape[0], tile), array.dtype) for array in streams]
+        + buffers(plain, piece, width, True)
+        + buffers(3, piece, width, False)
+        + buffers(1, piece, 3 * states, False)
         + [
-            pltpu.VMEM(lead + (owned, 3 * states), jnp.bfloat16),
+            pltpu.VMEM((3,) + lead + (piece, width), jnp.bfloat16),
+            pltpu.VMEM(lead + (piece, 3 * states), jnp.bfloat16),
             pltpu.VMEM((channels, 3 * states), jnp.float32),
             pltpu.VMEM((states, channels), jnp.float32),
             pltpu.VMEM((states, channels), jnp.float32),
-            pltpu.VMEM((slots, 1) + piece_shape[1:], jnp.bfloat16),
-            pltpu.VMEM((slots, 1) + piece_shape[1:], jnp.bfloat16),
+            pltpu.VMEM((length, channels), jnp.float32),
+            pltpu.VMEM((states, channels), jnp.float32),
         ]
+        + [pltpu.VMEM((rows, width), jnp.bfloat16)] * 4
+        + [
+            pltpu.VMEM(piece_shape, jnp.bfloat16),
+            pltpu.VMEM((stages, VECTORS, width), jnp.float32),
+            pltpu.VMEM((stages - 1, VECTORS, width), jnp.float32),
+            pltpu.VMEM((stages, 1, wide.shape[1]), jnp.float32),
+            pltpu.VMEM((stages - 1, 1, wide.shape[1]), jnp.float32),
+        ]
+        + [pltpu.VMEM((slots, 1) + piece_shape[1:], jnp.bfloat16)] * 3
         + [pltpu.SemaphoreType.DMA((flights,))] * 3
-        + [pltpu.SemaphoreType.DMA((slots,))] * 2,
+        + [
+            pltpu.SemaphoreType.DMA((len(stored),)),
+            pltpu.SemaphoreType.DMA((plain_outs,)),
+            pltpu.SemaphoreType.DMA((2, slots)),
+            pltpu.SemaphoreType.DMA((2, slots)),
+            pltpu.SemaphoreType.DMA((2, 2 * stages)),
+            pltpu.SemaphoreType.DMA((width // tile, len(streams))),
+        ],
         compiler_params=pltpu.CompilerParams(
-            collective_id=1, has_side_effects=True, vmem_limit_bytes=60 * 1024 * 1024
+            collective_id=1, has_side_effects=True, vmem_limit_bytes=63 * 1024 * 1024
         ),
         cost_estimate=pl.CostEstimate(flops=0, bytes_accessed=200_000_000, transcendentals=0),
         name="reduce_all",
-    )(order, unpack, grads.reshape(piece_shape), *rows_in, *tensors)
-    rows = rep_count * piece
+    )(order, unpack, vectors, wide, *rows_in, output.reshape(piece_shape), *stored, *streams, *tensors)
+    own = rep_count * piece
     return (
-        found[-1].reshape(grads.shape),
-        found[0].reshape(rows * parts, width),
-        found[1].reshape(rows, up.shape[1]),
-        [g.reshape(rows, width) for g in found[2 : 2 + len(squares)]],
-        found[-3].reshape(pack.shape[1], pack_width),
-        found[-2].reshape(owned * rep_count, 3 * states),
-    )
-
-
-class Waves:
-    def __init__(self, table, length, short, count):
-        self.low, self.length, self.short, self.count = table, length, short, count
-        self.half = length + short * count
-        self.gain = jnp.concatenate(
-            [
-                jnp.full((length, 1), 1.0 / length, jnp.float32),
-                jnp.full((short * count, 1), 1.0 / short, jnp.float32),
-            ]
-        )
-
-    def forward(self, rows):
-        return dot_nn(self.low, to_half(rows))
-
-    def back(self, real, imag):
-        return dot_tn(self.low, jnp.concatenate([to_half(real), to_half(imag)]))
-
-    def lags(self, real, imag, count):
-        real, imag = real * self.gain, imag * self.gain
-        channels = real.shape[1]
-        length, short = self.length, self.short
-        top = jnp.concatenate([real[:length], imag[:length]])
-        low = jnp.concatenate(
-            [
-                jnp.sum(part[length:].reshape(self.count, short, channels), axis=0)
-                for part in (real, imag)
-            ]
-        )
-        half, width = self.half, min(count, length)
-        table = jnp.concatenate([self.low[:length, :width], self.low[half : half + length, :width]])
-        small = jnp.concatenate(
-            [
-                self.low[length : length + short, length : length + short],
-                self.low[half + length : half + length + short, length : length + short],
-            ]
-        )
-        total = dot_tn(table, to_half(top))
-        head = total[:short] + dot_tn(small, to_half(low))
-        return jnp.concatenate([head, total[short:]]) if count > short else head
+        found[plain_outs].reshape(output.shape),
+        found[plain_outs + 1].reshape(output.shape),
+        to_float(found[0].reshape(own * parts, width)),
+        to_float(found[1].reshape(own, up.shape[1])),
+        [to_float(g.reshape(own, width)) for g in found[2:6]],
+        to_float(found[6].reshape(own, 3 * states)),
+        found[plain_outs + 2],
+        found[plain_outs + 3],
+    )
 
 
 def row_stats(values):
@@ -966,11 +1175,6 @@
     sending = jnp.sum(jnp.where(own_target[None, :] == ids[:, None], ids[None, :], 0), axis=1)
     unpacking = jnp.sum(jnp.where(arrival[None, :] == ids[:, None], ids[None, :], 0), axis=1)
 
-    def give_back(array):
-        pieces = array.reshape(slots, piece_rows, width)[arrival]
-        came = lax.all_to_all(pieces, ("rep", "shard"), split_axis=0, concat_axis=0, tiled=True)
-        return came[own_target].reshape(rows, width)
-
     pack = jnp.concatenate(
         [
             vector.reshape(1, owned)
@@ -990,7 +1194,7 @@
         + [b_up.reshape(-1, owned)]
     )
     counts = (rep_count, shard_count)
-    weights, packs, balanced, grad_low, spectra = gather_all(
+    weights, packs, balanced_low, grad_low, spectra = gather_all(
         sending,
         unpacking,
         tokens,
@@ -1004,8 +1208,8 @@
         shorts,
     )
     weight_q, weight_k, weight_v, weight_o, weight_up, weight_down = weights
-    kernel_wave, taps_wave, table, coef_rows, rate_rows = spectra
-    balanced = to_float(balanced)
+    kernel_wave, taps_wave, table, table_t, coef_rows, rate_rows = spectra
+    balanced = to_float(balanced_low)
     up_bias = to_float(packs[:, 10:].reshape(1, -1))
     small = to_float(jnp.swapaxes(packs[:, :10], 0, 1).reshape(10, width))
     (
@@ -1021,26 +1225,25 @@
         down_bias,
     ) = [small[i : i + 1] for i in range(10)]
 
-    waves = Waves(table, long_blocks * taps, taps, shorts)
-    half = waves.half
-    ker_re, ker_im = kernel_wave[:half], kernel_wave[half:]
-    tap_re, tap_im = taps_wave[:half], taps_wave[half:]
+    half = rows
+
+    def times(wave, filter_wave):
+        real, imag = wave[:half], wave[half:]
+        f_re, f_im = to_float(filter_wave[:half]), to_float(filter_wave[half:])
+        return jnp.concatenate(
+            [to_half(real * f_re - imag * f_im), to_half(real * f_im + imag * f_re)]
+        )
 
     hat_one, scale_one = row_stats(balanced)
     normed = to_half(hat_one * gain_one + bias_one)
     queries = dot_nn(normed, weight_q) + query_bias
     keys = to_half(dot_nn(normed, weight_k) + key_bias)
     values = dot_nn(normed, weight_v) + value_bias
-    wave_k = waves.forward(keys)
-    key_re, key_im = wave_k[:half], wave_k[half:]
-    shifted = waves.back(key_re * tap_re - key_im * tap_im, key_re * tap_im + key_im * tap_re)
+    key_wave = dot_nn(table, keys)
+    shifted = dot_nn(table_t, times(key_wave, taps_wave))
     inputs = shifted * values
-    wave_u = waves.forward(inputs)
-    in_re, in_im = wave_u[:half], wave_u[half:]
-    mixed = (
-        waves.back(in_re * ker_re - in_im * ker_im, in_re * ker_im + in_im * ker_re)
-        + skip * inputs
-    )
+    in_wave = dot_nn(table, to_half(inputs))
+    mixed = dot_nn(table_t, times(in_wave, kernel_wave)) + skip * inputs
     gated = to_half(queries * mixed)
     middle = balanced + (dot_nn(gated, weight_o) + out_bias)
     hat_two, scale_two = row_stats(middle)
@@ -1054,7 +1257,7 @@
     )
     branch = dot_nn(active, weight_down)
     result = middle + (branch + down_bias)
-    block_output = give_back(to_half(result))
+    output = to_half(result)
 
     grad_out = to_float(grad_low)
     part_down = dot_tn(active, grad_low, jnp.bfloat16)
@@ -1066,68 +1269,50 @@
     g_ln2_scale = jnp.sum(error * hat_two, axis=0)
     g_ln2_shift = jnp.sum(error, axis=0)
     grad_middle = grad_out + norm_back(error, hat_two, scale_two, gain_two)
-    grad_branch = to_half(grad_middle)
-    part_out = dot_tn(gated, grad_branch, jnp.bfloat16)
-    g_b_out = column_sum(grad_branch)
-    grad_gated = dot_nt(grad_branch, weight_o)
-    grad_query = to_half(grad_gated * mixed)
-    part_query = dot_tn(normed, grad_query, jnp.bfloat16)
-    grad_mixed = grad_gated * queries
-    wave_g = waves.forward(grad_mixed)
-    g_re, g_im = wave_g[:half], wave_g[half:]
-    grad_inputs = (
-        waves.back(g_re * ker_re + g_im * ker_im, g_im * ker_re - g_re * ker_im)
-        + skip * grad_mixed
-    )
-    g_skip = jnp.sum(grad_mixed * inputs, axis=0)
-    grad_kernel = waves.lags(
-        g_re * in_re + g_im * in_im, g_im * in_re - g_re * in_im, long_blocks * taps
-    )
-    grad_shifted = grad_inputs * values
-    grad_value = to_half(grad_inputs * shifted)
-    part_value = dot_tn(normed, grad_value, jnp.bfloat16)
-    wave_s = waves.forward(grad_shifted)
-    s_re, s_im = wave_s[:half], wave_s[half:]
-    grad_key = to_half(waves.back(s_re * tap_re + s_im * tap_im, s_im * tap_re - s_re * tap_im))
-    g_taps = waves.lags(s_re * key_re + s_im * key_im, s_im * key_re - s_re * key_im, taps)
-    part_key = dot_tn(normed, grad_key, jnp.bfloat16)
-    grad_normed = (
-        dot_nt(grad_query, weight_q) + dot_nt(grad_key, weight_k) + dot_nt(grad_value, weight_v)
-    )
-    g_ln1_scale = jnp.sum(grad_normed * hat_one, axis=0)
-    g_ln1_shift = jnp.sum(grad_normed, axis=0)
-    grad_input = grad_middle + norm_back(grad_normed, hat_one, scale_one, gain_one)
-
-    vectors = [
-        g_ln1_scale,
-        g_ln1_shift,
-        column_sum(grad_query),
-        column_sum(grad_key),
-        column_sum(grad_value),
-        g_skip,
-        g_b_out,
-        g_ln2_scale,
-        g_ln2_shift,
-        g_b_down,
-    ]
-    wide = jnp.concatenate([v[None] for v in vectors])
-    wide = jnp.swapaxes(wide.reshape(10, shard_count, owned), 0, 1)
-    wide = jnp.concatenate([wide, g_b_up.reshape(shard_count, -1, owned)], axis=1)
-    wide = to_half(jnp.pad(wide, ((0, 0), (0, -wide.shape[1] % rep_count), (0, 0))))
-    ups = b_up.shape[0] // owned
-    grad_tokens, grad_w_down, grad_w_up, squares, mine, ssm = reduce_all(
+    vectors = jnp.concatenate(
+        [
+            jnp.zeros((7, width), jnp.float32),
+            g_ln2_scale[None],
+            g_ln2_shift[None],
+            g_b_down[None],
+            jnp.zeros((VECTORS - 10, width), jnp.float32),
+        ]
+    )
+    grad_tokens, block_output, grad_w_down, grad_w_up, squares, ssm, vec, wide = reduce_all(
         arrival,
         own_target,
-        to_half(grad_input),
-        [coef_rows, rate_rows, grad_kernel, g_taps],
+        vectors,
+        g_b_up[None],
+        [coef_rows, rate_rows, skip, gain_one],
+        output,
+        [
+            grad_middle,
+            balanced_low,
+            normed,
+            table,
+            table_t,
+            weight_o,
+            weight_q,
+            weight_k,
+            weight_v,
+        ],
+        [
+            to_half(queries),
+            to_half(values),
+            to_half(shifted),
+            to_half(mixed),
+            to_half(in_wave),
+            to_half(key_wave),
+            kernel_wave,
+            taps_wave,
+        ],
         part_down,
         part_up,
-        [part_out, part_query, part_value, part_key],
-        wide,
+        dot_tn(gated, to_half(grad_middle), jnp.bfloat16),
         counts,
+        shorts,
     )
     grad_w_out, grad_w_query, grad_w_value, grad_w_key = squares
-    vec = [mine[i] for i in range(10)]
     return (
         block_output,
         grad_tokens,
@@ -1148,7 +1333,7 @@
         vec[7],
         vec[8],
         grad_w_up,
-        mine[10 : 10 + ups].reshape(-1),
+        wide[0],
         grad_w_down,
         vec[9],
     )

time: 442 us -> 350 us (0.79)
  local copies, waits for them, and re-layouts: 78.3 us -> 24.5 us
  matrix products: 82.4 us -> 46.7 us
  Pallas kernels: 236 us -> 248 us
  other arithmetic: 31.7 us -> 21.8 us
    unnamed x150 -> x64, local copies, waits for them, and re-layouts: 34.3 us -> 9.78 us
    dot_general x14 -> x3, matrix products: 30 us -> 12.3 us  [dot_tn(): lax.dot_general(one, two, (((0,), (0,)), ((), ())), preferred_element_typ...]
    concatenate x11 -> x1, local copies, waits for them, and re-layouts: 14.5 us -> 1.25 us  [local(): jnp.concatenate([jnp.zeros((7, width), jnp.float32), g_ln2_scale[None], g...]
    dot_general x6 -> x2, matrix products: 22.8 us -> 9.81 us  [dot_nt(): lax.dot_general(one, two, (((1,), (1,)), ((), ())), preferred_element_typ...]
    pallas_call x1, Pallas kernels: 112 us -> 125 us  [reduce_all(): pl.pallas_call(lambda *refs: reduce_body(rep_count, shard_count, units, p...]
    reduce_sum x8 -> x2, other arithmetic: 8.94 us -> 0.76 us  [the longest x1 0.63 us: local(): jnp.sum(jnp.where(own_target[None, :] == ids[:, None], ids[None, :], 0),...]
    convert_element_type x2 -> x9, other arithmetic: 1.56 us -> 8.64 us  [to_float(): return array.astype(jnp.float32)]
    slice x15 -> x1, local copies, waits for them, and re-layouts: 7.95 us -> 1.59 us  [local(): vec[9]]
  transfers between devices with their start and end apart: 1 -> 0, of which waited for: 0 -> 0; matrix products, arithmetic and copies ran while one was open for 25% -> 0% of each run, Pallas kernels for 26% -> 0%
where the time goes in v3:
time: 350 us; the launch traced here: 343 us
  Pallas kernels  248 us (71%)
  matrix products  46.7 us (13%)
  local copies, waits for them, and re-layouts  24.5 us (7%)
  other arithmetic  21.8 us (6%)
    pallas_call x1, Pallas kernels, reduce_all(): pl.pallas_call(lambda *refs: reduce_body(rep_count, shard_count, units, p...  125 us
    pallas_call x1, Pallas kernels, gather_all(): pl.pallas_call(lambda *refs: gather_body(rep_count, shard_count, units, s...  124 us
    dot_general x9, matrix products, dot_nn(): return jnp.dot(one, two, preferred_element_type=jnp.float32).astype(out)  24.6 us
    dot_general x3, matrix products, dot_tn(): lax.dot_general(one, two, (((0,), (0,)), ((), ())), preferred_element_typ...  12.3 us
    dot_general x2, matrix products, dot_nt(): lax.dot_general(one, two, (((1,), (1,)), ((), ())), preferred_element_typ...  9.81 us
    unnamed x64, local copies, waits for them, and re-layouts  9.78 us
    convert_element_type x9, other arithmetic, to_float(): return array.astype(jnp.float32)  8.64 us

profile of v3, /device:TPU:1, one launch (start us, length us, event | category | flops | bytes accessed | tf_op | source)
XLA Modules:
  0.0 343.4 jit_solution(4884975304245688210)
XLA Ops:
  0.7 0.7 and_select_fusion.1
  1.5 1.3 fusion.46
  3.5 0.7 reshape.456
  10.1 0.8 reshape.466
  10.8 1.2 concatenate.12.refs_10_
  12.1 0.8 reshape.446
  13.0 0.7 fusion.45.refs_0_
  14.9 1.5 copy.58.refs_11_
  16.4 1.5 copy.59.refs_12_
  17.8 1.5 copy.60.refs_13_
  19.3 123.6 %gather_all.1 = (bf16[4,8,24,768]{3,2,1,0:T(8,128)(2,1)}, bf16[4,8,24,768]{3,2,1,0:T(8,128)(2,1)}, bf16[4,8,24,768]{3,2,1,0:T(8,128)(2,1)}, bf16[4,8,24,768]{3,2...) custom-call(s32[32]{0:T(128)} %select_reduce_fusion.1.refs_0_, ...), custom_call_target="tpu_custom_call" | custom-call | bytes 200000000 | tf_op jit(solution)/shard_map/gather_all/pallas_call | solution.py:478
  143.0 0.8 slice_convert_fusion
  143.9 1.6 convert_reduce_fusion.1
  146.3 0.7 slice.132.refs_6_
  147.0 0.7 slice.133.refs_7_
  148.7 1.2 fusion.16.refs_11_
  149.9 1.9 convolution_add_fusion.1
  151.8 2.2 fusion.54
  154.0 5.5 %fusion.57 = (bf16[1024,768]{1,0:T(8,128)(2,1)}, f32[1024,768]{1,0:T(8,128)}) fusion(bf16[1024,512]{1,0:T(8,128)(2,1)S(1)} %copy-done.5, bf16[512,768]{1,0:T(8,128)(2,1)} %bitcast.123, bf16[768,768]{1,0:T(8,128)(2,1)} %bitcast.111, f32[768]{0:T(1024)S(1)} %add.197), kind=kOutput, calls=%fused_computation.144 | convolution fusion | flops 1410859008 | bytes 7736320 | tf_op jit(solution)/shard_map/dot_general | solution.py:22
  159.5 2.5 fusion.18
  162.1 1.9 fusion.55
  163.9 2.3 fusion.56
  166.8 0.8 copy-done.8
  167.6 2.2 fusion.50
  169.8 0.9 fusion.53
  171.1 2.7 fusion.49
  173.9 5.1 %add_convert_fusion = bf16[512,768]{1,0:T(8,128)(2,1)} fusion(f32[512,768]{1,0:T(8,128)S(1)} %get-tuple-element.111, bf16[3072,768]{1,0:T(8,128)(2,1)S(1)} %bitcast.148, f32[768]{0:T(1024)S(1)} %add.220, f32[512,3072]{1,0:T(8,128)S(1)} %fusion.49, f32[3072]{0:T(1024)S(1)} %reshape.481), kind=kOutput, calls=%fused_computation.53 | convolution fusion | flops 2432827392 | bytes 13384704 | tf_op jit(solution)/shard_map/dot_general | solution.py:22
  178.9 6.8 %convert_reduce_fusion = (f32[3072]{0:T(1024)}, bf16[512,3072]{1,0:T(8,128)(2,1)S(1)}) fusion(f32[512,3072]{1,0:T(8,128)S(1)} %fusion.49, f32[3072]{0:T(1024)S(1)} %reshape.481, bf16[512,768]{1,0:T(8,128)(2,1)S(1)} %bitcast.107, bf16[3072,768]{1,0:T(8,128)(2,1)S(1)} %bitcast.149), kind=kOutput, calls=%fused_computation.10 | convolution fusion | flops 2450519040 | bytes 14966784 | tf_op jit(solution)/shard_map/dot_general | solution.py:32
  185.7 5.5 %convolution_convert_fusion.1 = bf16[3072,768]{1,0:T(8,128)(2,1)} fusion(bf16[512,768]{1,0:T(8,128)(2,1)S(1)} %bitcast.108, f32[512,3072]{1,0:T(8,128)S(1)} %fusion.49, f32[3072]{0:T(1024)S(1)} %reshape.481), kind=kOutput, calls=%fused_computation.12 | convolution fusion | flops 2434007040 | bytes 11808768 | tf_op jit(solution)/shard_map/dot_general | solution.py:26
  191.2 3.1 multiply_reduce_fusion
  194.9 4.9 %convolution_convert_fusion = bf16[768,3072]{1,0:T(8,128)(2,1)} fusion(bf16[512,3072]{1,0:T(8,128)(2,1)S(1)} %get-tuple-element.114, f32[512,768]{1,0:T(8,128)S(1)} %get-tuple-element.111, f32[768]{0:T(1024)S(1)} %add.211, f32[768]{0:T(1024)S(1)} %mul.207, f32[512]{0:T(512)S(1)} %add_rsqrt_fusion.1, f32[512]{0:T(512)S(1)} %broadcast_multiply_fusion.3), kind=kOutput, calls=%fused_computation.11 | convolution fusion | flops 2420244480 | bytes 9447424 | tf_op jit(solution)/shard_map/dot_general | solution.py:26
  199.8 1.3 concatenate.15.refs_2_
  201.0 1.9 convolution_convert_fusion.2
  202.9 124.7 %reduce_all.1 = (bf16[8,4,24,768]{3,2,1,0:T(8,128)(2,1)}, bf16[8,24,3072]{2,1,0:T(8,128)(2,1)}, bf16[8,24,768]{2,1,0:T(8,128)(2,1)}, bf16[8,24,768]{2,1,0:T(8,12...) custom-call(s32[32]{0:T(128)} %copy-done.23, ...), custom_call_target="tpu_custom_call" | custom-call | bytes 200000000 | tf_op jit(solution)/shard_map/reduce_all/pallas_call | solution.py:1045
  327.6 1.3 reduce.15
  329.0 1.6 fusion.52
  330.6 1.0 bitcast_convert_fusion.6
  331.6 0.7 copy.66
  332.4 0.7 copy.65
  333.1 0.7 copy.64
  333.8 0.9 bitcast_convert_fusion.5
  334.7 0.9 bitcast_convert_fusion.4
  335.5 0.9 bitcast_convert_fusion.3
  336.4 0.9 bitcast_convert_fusion.2
  337.3 1.7 bitcast_convert_fusion.1
  339.0 1.7 bitcast_convert_fusion
  340.7 0.9 copy.69
  342.1 0.9 copy.70
  (103 shorter events, 11.6 us)
Async XLA Ops:
  12.9 130.0 %copy-start.22 = (s32[32]{0:T(128)}, s32[32]{0:T(128)S(1)}, u32[]{:S(2)}) copy-start(s32[32]{0:T(128)S(1)} %get-tuple-element.88.refs_1_) | copy-start | bytes 388
  13.6 129.3 %copy-start.23 = (s32[32]{0:T(128)}, s32[32]{0:T(128)S(1)}, u32[]{:S(2)}) copy-start(s32[32]{0:T(128)S(1)} %fusion.45.refs_0_) | copy-start | bytes 388
  143.0 2.6 copy-start
  143.0 3.1 copy-start.21
  148.3 1.6 copy-start.9
  148.6 3.2 copy-start.16
  149.9 1.9 copy-start.10
  151.8 2.2 copy-start.5
  154.0 5.5 %copy-start.3 = (bf16[1024,768]{1,0:T(8,128)(2,1)S(1)}, bf16[1024,768]{1,0:T(8,128)(2,1)}, u32[]{:S(2)}) copy-start(bf16[1024,768]{1,0:T(8,128)(2,1)} %get-tuple-element.56.refs_25_) | copy-start | bytes 4718596
  159.5 2.5 copy-start.6
  162.1 1.9 copy-start.4
  163.9 2.3 copy-start.2
  166.2 1.4 copy-start.8
  166.2 4.8 %slice-start = ((s8[4718592]{0:T(1024)(128)(4,1)}), s8[4194304]{0:T(1024)(128)(4,1)S(1)}, s32[]{:S(2)}) async-start(s8[4718592]{0:T(1024)(128)(4,1)} %bitcast.142), calls=%async_computation | async-start | bytes 8388608
  167.6 2.2 copy-start.11
  167.6 3.4 %slice-start.1 = ((s8[4718592]{0:T(1024)(128)(4,1)}), s8[524288]{0:T(1024)(128)(4,1)S(1)}, s32[]{:S(2)}) async-start(s8[4718592]{0:T(1024)(128)(4,1)} %bitcast.142), calls=%async_computation.1 | async-start | bytes 1048576
  170.7 3.1 slice-start.2
  171.1 2.8 slice-start.3
  173.9 5.1 %copy-start.7 = (bf16[32,16,768]{2,1,0:T(8,128)(2,1)S(1)}, bf16[32,16,768]{2,1,0:T(8,128)(2,1)}, u32[]{:S(2)}) copy-start(bf16[32,16,768]{2,1,0:T(8,128)(2,1)} %get-tuple-element.48) | copy-start | bytes 2359300
  194.9 6.2 %copy-start.1 = (f32[512,768]{1,0:T(8,128)}, f32[512,768]{1,0:T(8,128)S(1)}, u32[]{:S(2)}) copy-start(f32[512,768]{1,0:T(8,128)S(1)} %multiply_add_fusion.1.refs_9_) | copy-start | bytes 4718596
  327.6 6.2 %copy-start.20 = (bf16[8,24,768]{2,1,0:T(8,128)(2,1)S(1)}, bf16[8,24,768]{2,1,0:T(8,128)(2,1)}, u32[]{:S(2)}) copy-start(bf16[8,24,768]{2,1,0:T(8,128)(2,1)} %get-tuple-element.66) | copy-start | bytes 884740
  327.6 7.0 %copy-start.19 = (bf16[8,24,768]{2,1,0:T(8,128)(2,1)S(1)}, bf16[8,24,768]{2,1,0:T(8,128)(2,1)}, u32[]{:S(2)}) copy-start(bf16[8,24,768]{2,1,0:T(8,128)(2,1)} %get-tuple-element.67) | copy-start | bytes 884740
  330.6 5.0 %copy-start.18 = (bf16[8,24,768]{2,1,0:T(8,128)(2,1)S(1)}, bf16[8,24,768]{2,1,0:T(8,128)(2,1)}, u32[]{:S(2)}) copy-start(bf16[8,24,768]{2,1,0:T(8,128)(2,1)} %get-tuple-element.68) | copy-start | bytes 884740
  331.6 4.8 %copy-start.17 = (bf16[8,24,768]{2,1,0:T(8,128)(2,1)S(1)}, bf16[8,24,768]{2,1,0:T(8,128)(2,1)}, u32[]{:S(2)}) copy-start(bf16[8,24,768]{2,1,0:T(8,128)(2,1)} %get-tuple-element.70) | copy-start | bytes 884740
  333.8 3.5 %copy-start.13 = (bf16[8,24,3072]{2,1,0:T(8,128)(2,1)S(1)}, bf16[8,24,3072]{2,1,0:T(8,128)(2,1)}, u32[]{:S(2)}) copy-start(bf16[8,24,3072]{2,1,0:T(8,128)(2,1)} %get-tuple-element.71) | copy-start | bytes 3538948
  337.3 1.7 copy-start.12
  339.0 1.7 copy-start.15
  340.7 1.4 copy-start.14
